TPU v7x, 32 devices: a whole 2x2x4 slice. The times are simulated.
32 devices in a mesh: seq: 4 (over x, core), fsdp: 8 (over z, y).
Axes of the slice: x: 2, y: 2, z: 4, core: 2. Of those that a mesh axis runs over, the one named last changes fastest.
Arguments:
- inputs: bfloat16 [8, 8192, 1024], P('fsdp', 'seq'), may hold values from -8 to 8
- cotangent: bfloat16 [8, 8192, 1024], P('fsdp', 'seq'), may hold values from -6 to 6
- routed: int32 [8, 4, 256], P('fsdp'), may hold values from 0 to 2047, as said below
- doc_starts: int32 [8, 16], P('fsdp'), may hold values from 0 to 8191, as said below
- router: bfloat16 [1024], P('fsdp'), may hold values from -0.1875 to 0.1875
- attn_gain: bfloat16 [1024], P('fsdp'), may hold values from 0.5 to 1.5
- qkv_weight: bfloat16 [1024, 3072], P('fsdp'), may hold values from -0.1875 to 0.1875
- out_weight: bfloat16 [1024, 1024], P('fsdp'), may hold values from -1.5 to 1.5
- mlp_gain: bfloat16 [1024], P('fsdp'), may hold values from 0.5 to 1.5
- up_weight: bfloat16 [1024, 4096], P('fsdp'), may hold values from -0.1875 to 0.1875
- down_weight: bfloat16 [4096, 1024], P('fsdp'), may hold values from -0.09375 to 0.09375
Outputs:
- output: bfloat16 [8, 8192, 1024], P('fsdp', 'seq')
- input_grad: bfloat16 [8, 8192, 1024], P('fsdp', 'seq')
- router_grad: float32 [1024], P(('seq', 'fsdp'))
- attn_gain_grad: float32 [1024], P(('seq', 'fsdp'))
- qkv_grad: float32 [1024, 3072], P(('seq', 'fsdp'))
- out_grad: float32 [1024, 1024], P(('seq', 'fsdp'))
- mlp_gain_grad: float32 [1024], P(('seq', 'fsdp'))
- up_grad: float32 [1024, 4096], P(('seq', 'fsdp'))
- down_grad: float32 [4096, 1024], P(('seq', 'fsdp'))
Inputs may be any that keep to these rules, and one draw needn't show every extreme that they name: `routed`: each window of 2048 positions of a stream routes 256 distinct positions, counted from the window's first position and listed in ascending order. `doc_starts`: the first positions of the documents of each stream, in non-decreasing order, the first one 0; equal entries leave empty documents.
All inputs are finite; a program needn't handle non-finite values.
Results may differ from a plain program's by a relative error of at most 0.011.
Values may be sent and summed in bfloat16 or wider, within the bound.
No kernel may reach another device: no remote copies, remote signals or barrier semaphores. Data moves between devices by JAX's collectives and lax.ppermute only.
A program may use at most 256 MiB of HBM per device.

v0:
```python
import jax
import jax.numpy as jnp
from jax import lax
from jax.sharding import PartitionSpec as P

H = 16
HD = 64
WIN = 2048


EPS = 1e-05
NEG_FILL = -1e30
HIGH = lax.Precision.HIGHEST


def normed(values, gain_vec):
    return values * lax.rsqrt(jnp.mean(values * values, axis=-1, keepdims=True) + EPS) * gain_vec


def gelu_exact(values):
    return jax.nn.gelu(values, approximate=False)


def shards(
    inputs,
    cotangent,
    routed,
    doc_starts,
    router,
    attn_gain,
    qkv_weight,
    out_weight,
    mlp_gain,
    up_weight,
    down_weight,
):
    seq_count = lax.axis_size("seq")
    seq_rank = lax.axis_index("seq")
    width = inputs.shape[2]
    tok_count = inputs.shape[1]
    own_windows = tok_count // WIN
    stream_windows = routed.shape[1]
    head_local = H // seq_count
    head_scale = HD ** (-0.5)
    window_base = jnp.arange(stream_windows, dtype=jnp.int32) * WIN
    stream_rows = (window_base[:, None] + routed[0]).reshape(-1)
    routed_len = stream_rows.shape[0]
    own_routes = lax.dynamic_slice_in_dim(routed[0], seq_rank * own_windows, own_windows, 0)
    row_ids = ((jnp.arange(own_windows, dtype=jnp.int32) * WIN)[:, None] + own_routes).reshape(-1)
    segment = jnp.sum((doc_starts[0][None, :] <= stream_rows[:, None]).astype(jnp.int32), axis=1)
    ranks = jnp.arange(routed_len, dtype=jnp.int32)
    block_rows = min(512, routed_len)
    block_count = routed_len // block_rows
    stream_in = inputs[0]
    grad_in = cotangent[0]
    picked = stream_in[row_ids]
    picked_f = picked.astype(jnp.float32)
    router_w, gain_a, w_qkv, w_out = (
        lax.all_gather(router, "fsdp", axis=0, tiled=True),
        lax.all_gather(attn_gain, "fsdp", axis=0, tiled=True),
        lax.all_gather(qkv_weight, "fsdp", axis=0, tiled=True),
        lax.all_gather(out_weight, "fsdp", axis=0, tiled=True),
    )
    gain_m, w_up, w_down = (
        lax.all_gather(mlp_gain, "fsdp", axis=0, tiled=True),
        lax.all_gather(up_weight, "fsdp", axis=0, tiled=True),
        lax.all_gather(down_weight, "fsdp", axis=0, tiled=True),
    )
    logit = jnp.dot(picked, router_w, preferred_element_type=jnp.float32)
    router_rate = jax.nn.sigmoid(logit)
    gain_af = gain_a.astype(jnp.float32)
    normal_a = normed(picked_f, gain_af).astype(jnp.bfloat16)
    projected = jnp.dot(normal_a, w_qkv, preferred_element_type=jnp.float32).astype(jnp.bfloat16)
    query = projected[:, :width]
    keyed = projected[:, width : 2 * width]
    valued = projected[:, 2 * width :]
    query_h, keys_h, values_h = (
        lax.all_to_all(query, "seq", split_axis=1, concat_axis=0, tiled=True),
        lax.all_to_all(keyed, "seq", split_axis=1, concat_axis=0, tiled=True),
        lax.all_to_all(valued, "seq", split_axis=1, concat_axis=0, tiled=True),
    )
    query_h = query_h.reshape(routed_len, head_local, HD)
    keys_h = keys_h.reshape(routed_len, head_local, HD)
    values_h = values_h.reshape(routed_len, head_local, HD)

    def masked_scores(query_block, first_row):
        raw = (
            jnp.einsum("qhd,khd->hqk", query_block, keys_h, preferred_element_type=jnp.float32)
            * head_scale
        )
        seg_block = lax.dynamic_slice_in_dim(segment, first_row, block_rows)
        rank_block = first_row + jnp.arange(block_rows, dtype=jnp.int32)
        allowed = (seg_block[:, None] == segment[None, :]) & (rank_block[:, None] >= ranks[None, :])
        return jnp.where(allowed[None], raw, NEG_FILL)

    def forward_block(block_index):
        first_row = block_index * block_rows
        query_block = lax.dynamic_slice_in_dim(query_h, first_row, block_rows, 0)
        scores = masked_scores(query_block, first_row)
        row_max = jnp.max(scores, axis=-1, keepdims=True)
        exponent = jnp.exp(scores - row_max)
        row_total = jnp.sum(exponent, axis=-1, keepdims=True)
        weights_p = (exponent / row_total).astype(jnp.bfloat16)
        out_block = jnp.einsum(
            "hqk,khd->qhd", weights_p, values_h, preferred_element_type=jnp.float32
        )
        return (out_block.astype(jnp.bfloat16), (row_max + jnp.log(row_total))[..., 0])

    attended, log_totals = lax.map(forward_block, jnp.arange(block_count, dtype=jnp.int32))
    attended = attended.reshape(routed_len, head_local * HD)
    returned = lax.all_to_all(attended, "seq", split_axis=0, concat_axis=1, tiled=True)
    branch_a = jnp.dot(returned, w_out, preferred_element_type=jnp.float32)
    middle = picked_f + branch_a
    gain_mf = gain_m.astype(jnp.float32)
    normal_m = normed(middle, gain_mf).astype(jnp.bfloat16)
    pre_act = jnp.dot(normal_m, w_up, preferred_element_type=jnp.float32)
    activated = gelu_exact(pre_act).astype(jnp.bfloat16)
    branch_f = jnp.dot(activated, w_down, preferred_element_type=jnp.float32)
    branch_sum = branch_a + branch_f
    result = picked_f + router_rate[:, None] * branch_sum
    output = stream_in.at[row_ids].set(result.astype(jnp.bfloat16))
    router_w, gain_a, w_qkv, w_out = (
        lax.all_gather(router, "fsdp", axis=0, tiled=True),
        lax.all_gather(attn_gain, "fsdp", axis=0, tiled=True),
        lax.all_gather(qkv_weight, "fsdp", axis=0, tiled=True),
        lax.all_gather(out_weight, "fsdp", axis=0, tiled=True),
    )
    gain_m, w_up, w_down = (
        lax.all_gather(mlp_gain, "fsdp", axis=0, tiled=True),
        lax.all_gather(up_weight, "fsdp", axis=0, tiled=True),
        lax.all_gather(down_weight, "fsdp", axis=0, tiled=True),
    )
    grad_rows = grad_in[row_ids].astype(jnp.float32)
    carried = router_rate[:, None] * grad_rows
    carried_b = carried.astype(jnp.bfloat16)
    grad_down = jnp.einsum("rf,rd->fd", activated, carried_b, preferred_element_type=jnp.float32)
    grad_act = jnp.einsum("rd,fd->rf", carried_b, w_down, preferred_element_type=jnp.float32)
    grad_pre = jax.vjp(gelu_exact, pre_act)[1](grad_act)[0].astype(jnp.bfloat16)
    grad_up = jnp.einsum("rd,rf->df", normal_m, grad_pre, preferred_element_type=jnp.float32)
    grad_normal_m = jnp.einsum("rf,df->rd", grad_pre, w_up, preferred_element_type=jnp.float32)
    norm_back_m = jax.vjp(normed, middle, gain_mf)[1]
    grad_middle, grad_gain_m = norm_back_m(grad_normal_m)
    grad_a = (carried + grad_middle).astype(jnp.bfloat16)
    grad_out = jnp.einsum("rq,rd->qd", returned, grad_a, preferred_element_type=jnp.float32)
    grad_returned = jnp.einsum(
        "rd,qd->rq", grad_a, w_out, preferred_element_type=jnp.float32
    ).astype(jnp.bfloat16)
    grad_heads = lax.all_to_all(grad_returned, "seq", split_axis=1, concat_axis=0, tiled=True)
    grad_heads = grad_heads.reshape(routed_len, head_local, HD)

    def backward_block(carried_sums, block_index):
        key_sum, value_sum = carried_sums
        first_row = block_index * block_rows
        query_block = lax.dynamic_slice_in_dim(query_h, first_row, block_rows, 0)
        grad_block = lax.dynamic_slice_in_dim(grad_heads, first_row, block_rows, 0)
        scores = masked_scores(query_block, first_row)
        weights_f = jnp.exp(scores - log_totals[block_index][..., None])
        grad_prob = jnp.einsum(
            "qhd,khd->hqk", grad_block, values_h, preferred_element_type=jnp.float32
        )
        inner_sum = jnp.sum(weights_f * grad_prob, axis=-1, keepdims=True)
        grad_scores = (weights_f * (grad_prob - inner_sum)).astype(jnp.bfloat16)
        query_grad = (
            jnp.einsum("hqk,khd->qhd", grad_scores, keys_h, preferred_element_type=jnp.float32)
            * head_scale
        )
        key_sum = (
            key_sum
            + jnp.einsum(
                "hqk,qhd->khd", grad_scores, query_block, preferred_element_type=jnp.float32
            )
            * head_scale
        )
        value_sum = value_sum + jnp.einsum(
            "hqk,qhd->khd",
            weights_f.astype(jnp.bfloat16),
            grad_block,
            preferred_element_type=jnp.float32,
        )
        return ((key_sum, value_sum), query_grad)

    zero_heads = jnp.zeros((routed_len, head_local, HD), jnp.float32)
    (key_grad, value_grad), query_grad = lax.scan(
        backward_block, (zero_heads, zero_heads), jnp.arange(block_count, dtype=jnp.int32)
    )
    query_grad = query_grad.reshape(routed_len, head_local * HD).astype(jnp.bfloat16)
    key_grad = key_grad.reshape(routed_len, head_local * HD).astype(jnp.bfloat16)
    value_grad = value_grad.reshape(routed_len, head_local * HD).astype(jnp.bfloat16)
    back_q, back_k, back_v = (
        lax.all_to_all(query_grad, "seq", split_axis=0, concat_axis=1, tiled=True),
        lax.all_to_all(key_grad, "seq", split_axis=0, concat_axis=1, tiled=True),
        lax.all_to_all(value_grad, "seq", split_axis=0, concat_axis=1, tiled=True),
    )
    grad_proj = jnp.concatenate([back_q, back_k, back_v], axis=1)
    grad_qkv = jnp.einsum("rd,re->de", normal_a, grad_proj, preferred_element_type=jnp.float32)
    grad_normal_a = jnp.einsum("re,de->rd", grad_proj, w_qkv, preferred_element_type=jnp.float32)
    norm_back_a = jax.vjp(normed, picked_f, gain_af)[1]
    grad_norm_x, grad_gain_a = norm_back_a(grad_normal_a)
    grad_rate = jnp.sum(grad_rows * branch_sum, axis=-1)
    grad_logit = grad_rate * router_rate * (1.0 - router_rate)
    grad_router = jnp.dot(grad_logit, picked_f, precision=HIGH)
    grad_picked = (
        grad_rows + grad_middle + grad_norm_x + grad_logit[:, None] * router_w.astype(jnp.float32)
    )
    input_grad = grad_in.at[row_ids].set(grad_picked.astype(jnp.bfloat16))
    every_sum = (
        lax.psum_scatter(grad_router, ("seq", "fsdp"), scatter_dimension=0, tiled=True),
        lax.psum_scatter(grad_gain_a, ("seq", "fsdp"), scatter_dimension=0, tiled=True),
        lax.psum_scatter(grad_qkv, ("seq", "fsdp"), scatter_dimension=0, tiled=True),
        lax.psum_scatter(grad_out, ("seq", "fsdp"), scatter_dimension=0, tiled=True),
        lax.psum_scatter(grad_gain_m, ("seq", "fsdp"), scatter_dimension=0, tiled=True),
        lax.psum_scatter(grad_up, ("seq", "fsdp"), scatter_dimension=0, tiled=True),
        lax.psum_scatter(grad_down, ("seq", "fsdp"), scatter_dimension=0, tiled=True),
    )
    router_out, gain_a_out, qkv_out, out_proj, gain_m_out, up_out, down_out = every_sum
    return (
        output[None],
        input_grad[None],
        router_out,
        gain_a_out,
        qkv_out,
        out_proj,
        gain_m_out,
        up_out,
        down_out,
    )


def solution(mesh):
    return jax.shard_map(
        shards,
        mesh=mesh,
        in_specs=(
            P("fsdp", "seq", None),
            P("fsdp", "seq", None),
            P("fsdp", None, None),
            P("fsdp", None),
            P("fsdp"),
            P("fsdp"),
            P("fsdp", None),
            P("fsdp", None),
            P("fsdp"),
            P("fsdp", None),
            P("fsdp", None),
        ),
        out_specs=(
            P("fsdp", "seq", None),
            P("fsdp", "seq", None),
            P(("seq", "fsdp")),
            P(("seq", "fsdp")),
            P(("seq", "fsdp"), None),
            P(("seq", "fsdp"), None),
            P(("seq", "fsdp")),
            P(("seq", "fsdp"), None),
            P(("seq", "fsdp"), None),
        ),
        check_vma=False,
    )
```

profile of v0, /device:TPU:1, one launch (start us, length us, event | category | flops | bytes accessed | tf_op | source)
XLA Modules:
  0.0 1478.9 jit_solution(5551582042403831735)
XLA Ops:
  7.2 4.8 copy.129
  16.2 18.0 %all-gather.1 = bf16[8,1,128]{2,1,0:T(2,128)(2,1)S(1)} all-gather(bf16[1,1,128]{2,1,0:T(2,128)(2,1)S(1)} %bitcast.197), channel_id=1, replica_groups=mesh['seq'=4,'fsdp'=8] {'fsdp'}, dimensions={0}, use_global_device_ids=true | all-gather | bytes 2304 | tf_op jit(solution)/shard_map/all_gather | solution.py:60
  38.7 76.1 %all-gather.8.cloned.1.call-done = bf16[1024,3072]{1,0:T(8,128)(2,1)} async-done(((bf16[128,3072]{1,0:T(8,128)(2,1)}), bf16[1024,3072]{1,0:T(8,128)(2,1)}) %all-gather.8.cloned.1.call-update) | async-done | bytes 6291472 | tf_op jit(solution)/shard_map/all_gather | solution.py:61
  126.0 7.3 all-to-all-done
  138.3 7.3 all-to-all-done.1
  151.5 6.5 all-to-all-done.2
  158.7 18.0 %while.28 = (s32[]{:T(128)}, bf16[2,512,4,64]{1,3,2,0:T(8,128)(2,1)S(1)}, f32[2,4,512]{2,1,0:T(4,128)S(1)}, s32[2]{0:T(128)S(1)}, s32[1024]{0:T(1024)S(1)}, /*in...) while((s32[]{:T(128)}, ...), condition=%wide.region_5.6_spmd.clone, body=%wide.region_2.5_spmd.clone.sunk | while | flops 563739136 | bytes 28915908 | solution.py:109
  182.5 14.2 all-gather.2
  196.7 5.1 gather_fusion.1
  201.8 14.2 all-gather
  221.3 68.9 %all-gather.12.cloned.1.call-done = bf16[1024,4096]{1,0:T(8,128)(2,1)} async-done(((bf16[128,4096]{1,0:T(8,128)(2,1)}), bf16[1024,4096]{1,0:T(8,128)(2,1)}) %all-gather.12.cloned.1.call-update) | async-done | bytes 8388624 | tf_op jit(solution)/shard_map/all_gather | solution.py:66
  290.2 15.7 %multiply_convert_fusion.1 = (bf16[256,4096]{1,0:T(8,128)(2,1)}, f32[256,4096]{1,0:T(8,128)}, f32[256,4096]{1,0:T(8,128)}) fusion(bf16[1024,4096]{1,0:T(8,128)(2,1)} %all-gather.12.cloned.1.call-done, f32[256,1024]{1,0:T(8,128)S(1)} %get-tuple-element.251, f32[1024]{0:T(1024)S(1)} %bitcast.179, f32[256]{0:T(256)S(1)} %fusion.86), kind=kOutput, calls=%fused_computation.57 | convolution fusion | flops 2216427520 | bytes 19928064 | tf_op jit(solution)/shard_map/dot_general | solution.py:116
  305.9 109.4 %all-gather.14.cloned.1.call-done = bf16[4096,1024]{1,0:T(8,128)(2,1)} async-done(((bf16[512,1024]{1,0:T(8,128)(2,1)}), bf16[4096,1024]{1,0:T(8,128)(2,1)}) %all-gather.14.cloned.1.call-update) | async-done | bytes 8388624 | tf_op jit(solution)/shard_map/all_gather | solution.py:67
  415.4 7.7 fusion.59
  423.6 11.4 add_convert_fusion
  440.9 5.2 all-to-all-start.4
  456.7 60.9 %while.29 = (s32[]{:T(128)}, f32[1024,4,64]{0,2,1:T(8,128)S(1)}, f32[1024,4,64]{0,2,1:T(8,128)}, bf16[2,512,4,64]{1,3,2,0:T(8,128)(2,1)}, s32[2]{0:T(128)S(1)}, ...) while((s32[]{:T(128)}, f32[1024,4,64]{0,2,1:T(8,128)S(1)}, ...), condition=%wide.region_11.12_spmd.clone, body=%wide.region_9.11_spmd.clone.sunk | while | flops 1376647680 | bytes 133241736 | solution.py:183
  465.3 5.7 multiply_reduce_fusion.5
  495.2 5.8 multiply_reduce_fusion.5
  525.9 6.7 all-to-all-done.5
  538.6 6.3 all-to-all-done.6
  544.9 11.4 all_to_all.131
  557.1 6.5 fusion.63
  564.8 9.8 fusion.89
  575.7 9.8 fusion.75
  586.7 6.8 scatter_custom_fusion
  593.8 6.2 fusion.54
  600.0 39.8 %all-reduce.3 = (f32[1024]{0:T(1024)S(1)}, f32[1024]{0:T(1024)S(1)}, f32[1024]{0:T(1024)S(1)}) all-reduce(f32[1024]{0:T(1024)S(1)} %bitcast.188, f32[1024]{0:T(1024)S(1)} %get-tuple-element.203, f32[1024]{0:T(1024)S(1)} %copy-done.32), channel_id=2, replica_groups=mesh['seq'=4,'fsdp'=8] {'seq','fsdp'}, use_global_device_ids=true, to_apply=%region_15.16.clone | all-reduce | flops 3072 | bytes 24576
  641.6 7.9 scatter_custom_fusion.1
  649.5 100.8 %reduce-scatter.5.cloned.1.call-done = f32[32,3072]{1,0:T(8,128)} async-done(((f32[1024,3072]{1,0:T(8,128)}), f32[32,3072]{1,0:T(8,128)}) %reduce-scatter.5.cloned.1.call-update) | async-done | bytes 393232 | tf_op jit(solution)/shard_map/reduce_scatter | solution.py:209
  750.4 361.1 %reduce-scatter.9.cloned.1.call-done = f32[32,4096]{1,0:T(8,128)} async-done(((f32[1024,4096]{1,0:T(8,128)}), f32[32,4096]{1,0:T(8,128)}) %reduce-scatter.9.cloned.1.call-update) | async-done | bytes 524304 | tf_op jit(solution)/shard_map/reduce_scatter | solution.py:212
  1111.5 360.4 %reduce-scatter.11.cloned.1.call-done = f32[128,1024]{1,0:T(8,128)} async-done(((f32[4096,1024]{1,0:T(8,128)}), f32[128,1024]{1,0:T(8,128)}) %reduce-scatter.11.cloned.1.call-update) | async-done | bytes 524304 | tf_op jit(solution)/shard_map/reduce_scatter | solution.py:213
  (220 shorter events, 140.4 us)
Async XLA Ops:
  7.2 107.7 %all-gather.8.cloned.1.call-start = ((), (), s32[]{:S(2)}) async-start(), calls=%async_computation.12 | async-start | bytes 7077888 | tf_op jit(solution)/shard_map/all_gather | solution.py:61
  12.1 22.1 %copy-start.31 = (s32[1,4,256]{2,1,0:T(4,128)S(1)}, s32[1,4,256]{2,1,0:T(4,128)}, u32[]{:S(2)}) copy-start(s32[1,4,256]{2,1,0:T(4,128)} %param.17) | copy-start | bytes 12292
  14.1 202.1 %all-gather.10.cloned.1.call-start = ((), (), s32[]{:S(2)}) async-start(), calls=%async_computation.13 | async-start | bytes 2359296 | tf_op jit(solution)/shard_map/all_gather | solution.py:62
  14.8 275.4 %all-gather.12.cloned.1.call-start = ((), (), s32[]{:S(2)}) async-start(), calls=%async_computation.14 | async-start | bytes 9437184 | tf_op jit(solution)/shard_map/all_gather | solution.py:66
  15.6 399.8 %all-gather.14.cloned.1.call-start = ((), (), s32[]{:S(2)}) async-start(), calls=%async_computation.15 | async-start | bytes 9437184 | tf_op jit(solution)/shard_map/all_gather | solution.py:67
  34.2 85.4 %copy-start.20 = (f32[8,1,128]{2,1,0:T(1,128)}, f32[8,1,128]{2,1,0:T(1,128)S(1)}, u32[]{:S(2)}) copy-start(f32[8,1,128]{2,1,0:T(1,128)S(1)} %convert_element_type.106) | copy-start | bytes 12292
  34.2 85.3 %copy-start.33 = (s32[256,1]{0,1:T(1,128)}, s32[256,1]{0,1:T(1,128)S(1)}, u32[]{:S(2)}) copy-start(s32[256,1]{0,1:T(1,128)S(1)} %compare_select_fusion) | copy-start | bytes 3076
  38.5 178.8 %copy-start.1 = (bf16[256,1024]{1,0:T(8,128)(2,1)}, bf16[256,1024]{1,0:T(8,128)(2,1)S(1)}, u32[]{:S(2)}) copy-start(bf16[256,1024]{1,0:T(8,128)(2,1)S(1)} %gather_fusion) | copy-start | bytes 1572868
  38.7 80.8 %copy-start.29 = (f32[256]{0:T(256)}, f32[256]{0:T(256)S(1)}, u32[]{:S(2)}) copy-start(f32[256]{0:T(256)S(1)} %fusion.60) | copy-start | bytes 3076
  38.7 80.8 %copy-start.24 = (f32[256]{0:T(256)}, f32[256]{0:T(256)S(1)}, u32[]{:S(2)}) copy-start(f32[256]{0:T(256)S(1)} %fusion.85) | copy-start | bytes 3076
  119.6 30.5 %copy-start.35 = (s32[1,16]{1,0:T(1,128)S(1)}, s32[1,16]{1,0:T(1,128)}, u32[]{:S(2)}) copy-start(s32[1,16]{1,0:T(1,128)} %param.18) | copy-start | bytes 196
  120.5 12.7 all-to-all-start
  133.2 12.3 all-to-all-start.1
  145.5 12.4 all-to-all-start.2
  177.2 24.5 %copy-start.37 = (bf16[128]{0:T(256)(128)(2,1)S(1)}, bf16[128]{0:T(256)(128)(2,1)}, u32[]{:S(2)}) copy-start(bf16[128]{0:T(256)(128)(2,1)} %param.19) | copy-start | bytes 772
  178.3 37.9 %all-to-all-start.3 = ((bf16[4,256,256]{1,2,0:T(8,128)(2,1)}), bf16[4,256,256]{1,2,0:T(8,128)(2,1)S(1)}, u32[]{:S(2)}, u32[]{:S(2)}) async-start(bf16[4,256,256]{1,2,0:T(8,128)(2,1)} %copy.80), calls=%async_computation.3 | async-start | bytes 1048576 | tf_op jit(solution)/shard_map/all_to_all | solution.py:111
  221.3 217.0 %copy-start.3 = (f32[256,1024]{1,0:T(8,128)}, f32[256,1024]{1,0:T(8,128)S(1)}, u32[]{:S(2)}) copy-start(f32[256,1024]{1,0:T(8,128)S(1)} %get-tuple-element.251) | copy-start | bytes 3145732
  290.2 125.1 %copy-start.5 = (bf16[256,1024]{1,0:T(8,128)(2,1)S(1)}, bf16[256,1024]{1,0:T(8,128)(2,1)}, u32[]{:S(2)}) copy-start(bf16[256,1024]{1,0:T(8,128)(2,1)} %gather_fusion.1) | copy-start | bytes 1572868
  440.9 13.3 all-to-all-start.4
  446.1 203.4 %reduce-scatter.7.cloned.1.call-start = ((), (), s32[]{:S(2)}) async-start(), calls=%async_computation.17 | async-start | bytes 4325376 | tf_op jit(solution)/shard_map/reduce_scatter | solution.py:210
  520.3 12.3 all-to-all-start.5
  524.6 32.5 %copy-start.2 = (bf16[256,1024]{1,0:T(8,128)(2,1)S(1)}, bf16[256,1024]{1,0:T(8,128)(2,1)}, u32[]{:S(2)}) copy-start(bf16[256,1024]{1,0:T(8,128)(2,1)} %copy-done.1) | copy-start | bytes 1572868
  524.6 32.4 %copy-start.21 = (f32[8,1,128]{2,1,0:T(1,128)S(1)}, f32[8,1,128]{2,1,0:T(1,128)}, u32[]{:S(2)}) copy-start(f32[8,1,128]{2,1,0:T(1,128)} %copy-done.20) | copy-start | bytes 12292
  524.6 32.4 %copy-start.25 = (f32[256]{0:T(256)S(1)}, f32[256]{0:T(256)}, u32[]{:S(2)}) copy-start(f32[256]{0:T(256)} %copy-done.24) | copy-start | bytes 3076
  532.6 31.0 %copy-start.15 = (bf16[4,256,256]{1,2,0:T(8,128)(2,1)}, bf16[4,256,256]{1,2,0:T(8,128)(2,1)S(1)}, u32[]{:S(2)}) copy-start(bf16[4,256,256]{1,2,0:T(8,128)(2,1)S(1)} %all-to-all-done.5) | copy-start | bytes 1572868
  532.6 12.3 all-to-all-start.6
  536.8 213.5 %reduce-scatter.5.cloned.1.call-start = ((), (), s32[]{:S(2)}) async-start(), calls=%async_computation.16 | async-start | bytes 12976128 | tf_op jit(solution)/shard_map/reduce_scatter | solution.py:209
  563.6 547.9 %reduce-scatter.9.cloned.1.call-start = ((), (), s32[]{:S(2)}) async-start(), calls=%async_computation.18 | async-start | bytes 17301504 | tf_op jit(solution)/shard_map/reduce_scatter | solution.py:212
  574.6 897.2 %reduce-scatter.11.cloned.1.call-start = ((), (), s32[]{:S(2)}) async-start(), calls=%async_computation.19 | async-start | bytes 17301504 | tf_op jit(solution)/shard_map/reduce_scatter | solution.py:213
  593.8 47.8 %copy-start.30 = (f32[256]{0:T(256)S(1)}, f32[256]{0:T(256)}, u32[]{:S(2)}) copy-start(f32[256]{0:T(256)} %copy-done.29) | copy-start | bytes 3076
  593.8 47.8 %copy-start.11 = (f32[256,1024]{1,0:T(8,128)S(1)}, f32[256,1024]{1,0:T(8,128)}, u32[]{:S(2)}) copy-start(f32[256,1024]{1,0:T(8,128)} %copy-done.10) | copy-start | bytes 3145732
  593.8 47.8 %copy-start.27 = (f32[256]{0:T(256)S(1)}, f32[256]{0:T(256)}, u32[]{:S(2)}) copy-start(f32[256]{0:T(256)} %copy-done.26) | copy-start | bytes 3076
  (29 other events, 153.0 us)
Sparse Core Ops, SparseCore 0:
  14.2 100.6 all-gather.7
  117.0 46.8 all-gather.9
  166.0 124.1 all-gather.11
  292.2 123.1 all-gather.13
  450.0 135.9 reduce-scatter.6
  592.4 157.9 reduce-scatter.4
  753.3 358.0 reduce-scatter.8
  1114.4 357.3 reduce-scatter.10
where the time goes:
time: 1490 us; the launch traced here: 1480 us
  waiting for transfers between devices  1120 us (75%)
  matrix products  138 us (9%)
  blocking collectives  97.5 us (7%)
  local copies, waits for them, and re-layouts  40.8 us (3%)
  other arithmetic  31.8 us (2%)
  starting transfers between devices  31.5 us (2%)
  between operations  14.9 us (1%)
    reduce_scatter x1, waiting for transfers between devices, shards(): lax.psum_scatter(grad_up, ('seq', 'fsdp'), scatter_dimension=0, tiled=True)  361 us
    reduce_scatter x1, waiting for transfers between devices, shards(): lax.psum_scatter(grad_down, ('seq', 'fsdp'), scatter_dimension=0, tiled=T...  360 us
    all_gather x1, waiting for transfers between devices, shards(): lax.all_gather(down_weight, 'fsdp', axis=0, tiled=True)  109 us
    reduce_scatter x1, waiting for transfers between devices, shards(): lax.psum_scatter(grad_qkv, ('seq', 'fsdp'), scatter_dimension=0, tiled=True)  101 us
    all_gather x1, waiting for transfers between devices, shards(): lax.all_gather(qkv_weight, 'fsdp', axis=0, tiled=True)  76.1 us
    all_gather x1, waiting for transfers between devices, shards(): lax.all_gather(up_weight, 'fsdp', axis=0, tiled=True)  68.9 us
    unnamed x1, blocking collectives  39.8 us
  transfers between devices with their start and end apart: 15, of which 12 were waited for; matrix products, arithmetic and copies ran while one was open for 12% of the time, Pallas kernels for 0%

commit v1 on v0

v1 whole, which is shorter than its diff:
```python
from functools import partial

import jax
import jax.numpy as jnp
from jax import lax
from jax.experimental import pallas as pl
from jax.experimental.pallas import tpu as pltpu
from jax.sharding import PartitionSpec as P

H = 16
HD = 64
WIN = 2048
EPS = 1e-05
NEG_FILL = -1e30
PAIR = 2 * HD
LANES = 128
BF16 = jnp.bfloat16
F32 = jnp.float32


def mm(a, b, dims):
    return lax.dot_general(a, b, (dims, ((), ())), preferred_element_type=F32)


NN = ((1,), (0,))
NT = ((1,), (1,))
TN = ((0,), (0,))


def flip(values, axis, bit):
    count = lax.axis_size(axis)
    return lax.ppermute(values, axis, [(j, j ^ bit) for j in range(count)])


def bits_down(count):
    bit = count // 2
    while bit:
        yield bit
        bit //= 2


def gather_blocks(own, axis):
    blocks = {0: own}
    for bit in bits_down(lax.axis_size(axis)):
        for key in list(blocks):
            blocks[key ^ bit] = flip(blocks[key], axis, bit)
    return [blocks[key] for key in sorted(blocks)]


def scatter_blocks(blocks, axis):
    parts = dict(enumerate(blocks))
    bit = 1
    while bit < lax.axis_size(axis):
        for key in [k for k in parts if k & bit]:
            got = flip(parts.pop(key).astype(BF16), axis, bit)
            parts[key ^ bit] = parts[key ^ bit] + got.astype(F32)
        bit *= 2
    return parts[0]


def head_lanes(rows):
    return lax.broadcasted_iota(jnp.int32, (rows, PAIR), 1) < HD


def allowed_tile(cols_ref, where, rows_pos, rows_start):
    cols = cols_ref[where]
    return (cols <= rows_pos) & (cols >= rows_start)


def attention_forward_kernel(
    window_ref, place_ref, first_ref, q_ref, k_ref, v_ref, pos_ref, start_ref, cols_ref, o_ref, lse_ref
):
    block = pl.program_id(0)
    tile = q_ref.shape[0]
    pairs = q_ref.shape[1] // PAIR
    low_lanes = head_lanes(tile)
    rows_pos = pos_ref[...]
    rows_start = start_ref[...]
    last = window_ref[block]
    count = last - first_ref[block] + 1
    lane = lax.broadcasted_iota(jnp.int32, (tile, LANES), 1)
    lse = jnp.zeros((tile, LANES), F32)
    for pair in range(pairs):
        lanes = pl.ds(pair * PAIR, PAIR)
        q_pair = q_ref[:, lanes] * jnp.asarray(HD**-0.5, BF16)
        halves = []
        for half in range(2):
            q_half = jnp.where(low_lanes == (half == 0), q_pair, jnp.zeros_like(q_pair))

            def step(i, carry):
                top, total, acc = carry
                where = place_ref[last - i]
                scores = mm(q_half, k_ref[where, :, lanes], NT)
                scores = jnp.where(
                    allowed_tile(cols_ref, where, rows_pos, rows_start), scores, NEG_FILL
                )
                new_top = jnp.maximum(top, jnp.max(scores, axis=1, keepdims=True))
                shrink = jnp.exp(top - new_top)
                exponent = jnp.exp(scores - new_top)
                total = total * shrink + jnp.sum(exponent, axis=1, keepdims=True)
                acc = acc * shrink + mm(exponent.astype(BF16), v_ref[where, :, lanes], NN)
                return (new_top, total, acc)

            top, total, acc = lax.fori_loop(
                0,
                count,
                step,
                (
                    jnp.full((tile, 1), NEG_FILL, F32),
                    jnp.zeros((tile, 1), F32),
                    jnp.zeros((tile, PAIR), F32),
                ),
            )
            halves.append(acc / total)
            lse = jnp.where(lane == 2 * pair + half, top + jnp.log(total), lse)
        o_ref[:, lanes] = jnp.where(low_lanes, halves[0], halves[1]).astype(BF16)
    lse_ref[...] = lse


def attention_backward_kernel(
    window_ref,
    place_ref,
    first_ref,
    q_ref,
    k_ref,
    v_ref,
    g_ref,
    lse_ref,
    pos_ref,
    start_ref,
    cols_ref,
    dq_ref,
    dk_ref,
    dv_ref,
    dk_sum,
    dv_sum,
    prob_keep,
    grad_keep,
):
    block = pl.program_id(0)
    tile = q_ref.shape[0]
    pairs = q_ref.shape[1] // PAIR
    scale = HD**-0.5
    low_lanes = head_lanes(tile)
    rows_pos = pos_ref[...]
    rows_start = start_ref[...]
    last = window_ref[block]
    count = last - first_ref[block] + 1

    @pl.when(block == 0)
    def _():
        dk_sum[...] = jnp.zeros_like(dk_sum)
        dv_sum[...] = jnp.zeros_like(dv_sum)

    for pair in range(pairs):
        lanes = pl.ds(pair * PAIR, PAIR)
        q_pair = q_ref[:, lanes] * jnp.asarray(scale, BF16)
        g_pair = g_ref[:, lanes]
        halves = []
        for half in range(2):
            keep = low_lanes == (half == 0)
            q_half = jnp.where(keep, q_pair, jnp.zeros_like(q_pair))
            g_half = jnp.where(keep, g_pair, jnp.zeros_like(g_pair))
            lse = lse_ref[:, 2 * pair + half : 2 * pair + half + 1]

            def first_pass(i, inner):
                where = place_ref[last - i]
                scores = mm(q_half, k_ref[where, :, lanes], NT)
                prob = jnp.where(
                    allowed_tile(cols_ref, where, rows_pos, rows_start),
                    jnp.exp(scores - lse),
                    0.0,
                )
                grad_prob = mm(g_half, v_ref[where, :, lanes], NT)
                prob_keep[i] = prob
                grad_keep[i] = grad_prob
                dv_sum[where, :, lanes] += mm(prob.astype(BF16), g_half, TN)
                return inner + jnp.sum(prob * grad_prob, axis=1, keepdims=True)

            inner = lax.fori_loop(0, count, first_pass, jnp.zeros((tile, 1), F32))

            def second_pass(i, acc):
                where = place_ref[last - i]
                grad_scores = (prob_keep[i] * (grad_keep[i] - inner)).astype(BF16)
                dk_sum[where, :, lanes] += mm(grad_scores, q_half, TN)
                return acc + mm(grad_scores, k_ref[where, :, lanes], NN)

            acc = lax.fori_loop(0, count, second_pass, jnp.zeros((tile, PAIR), F32))
            halves.append(acc * scale)
        dq_ref[:, lanes] = jnp.where(low_lanes, halves[0], halves[1]).astype(BF16)

    @pl.when(block == pl.num_programs(0) - 1)
    def _():
        dk_ref[...] = dk_sum[...].astype(BF16)
        dv_ref[...] = dv_sum[...].astype(BF16)


VMEM_LIMIT = 48 * 1024 * 1024


def attention_specs(blocks, tile, width):
    by_rows = lambda cols: pl.BlockSpec((tile, cols), lambda b, *_: (b, 0))
    whole = lambda *dims: pl.BlockSpec(dims, lambda b, *_: (0,) * len(dims))
    keys = whole(blocks, tile, width)
    return by_rows, keys, whole(blocks, 1, tile)


def attention_forward(tables, q, k, v, pos, start, tile):
    rows, width = q.shape
    blocks = rows // tile
    by_rows, keys, cols = attention_specs(blocks, tile, width)
    return pl.pallas_call(
        attention_forward_kernel,
        grid_spec=pltpu.PrefetchScalarGridSpec(
            num_scalar_prefetch=3,
            grid=(blocks,),
            in_specs=[by_rows(width), keys, keys, by_rows(1), by_rows(1), cols],
            out_specs=[by_rows(width), by_rows(LANES)],
        ),
        out_shape=[
            jax.ShapeDtypeStruct((rows, width), BF16),
            jax.ShapeDtypeStruct((rows, LANES), F32),
        ],
        compiler_params=pltpu.CompilerParams(vmem_limit_bytes=VMEM_LIMIT),
        cost_estimate=pl.CostEstimate(
            flops=2 * rows * rows * width,
            transcendentals=rows * rows * width // HD // 2,
            bytes_accessed=8 * rows * width,
        ),
        name="attention_forward",
    )(
        *tables,
        q,
        k.reshape(blocks, tile, width),
        v.reshape(blocks, tile, width),
        pos[:, None],
        start[:, None],
        pos.reshape(blocks, 1, tile),
    )


def attention_backward(tables, q, k, v, grad, lse, pos, start, tile):
    rows, width = q.shape
    blocks = rows // tile
    by_rows, keys, cols = attention_specs(blocks, tile, width)
    dq, dk, dv = pl.pallas_call(
        attention_backward_kernel,
        grid_spec=pltpu.PrefetchScalarGridSpec(
            num_scalar_prefetch=3,
            grid=(blocks,),
            in_specs=[by_rows(width), keys, keys, by_rows(width), by_rows(LANES), by_rows(1), by_rows(1), cols],
            out_specs=[by_rows(width), keys, keys],
            scratch_shapes=[
                pltpu.VMEM((blocks, tile, width), F32),
                pltpu.VMEM((blocks, tile, width), F32),
                pltpu.VMEM((blocks, tile, tile), F32),
                pltpu.VMEM((blocks, tile, tile), F32),
            ],
        ),
        out_shape=[
            jax.ShapeDtypeStruct((rows, width), BF16),
            jax.ShapeDtypeStruct((blocks, tile, width), BF16),
            jax.ShapeDtypeStruct((blocks, tile, width), BF16),
        ],
        compiler_params=pltpu.CompilerParams(vmem_limit_bytes=VMEM_LIMIT),
        cost_estimate=pl.CostEstimate(
            flops=5 * rows * rows * width,
            transcendentals=rows * rows * width // HD // 2,
            bytes_accessed=14 * rows * width,
        ),
        name="attention_backward",
    )(
        *tables,
        q,
        k.reshape(blocks, tile, width),
        v.reshape(blocks, tile, width),
        grad,
        lse,
        pos[:, None],
        start[:, None],
        pos.reshape(blocks, 1, tile),
    )
    return dq, dk.reshape(rows, width), dv.reshape(rows, width)


def norm_back(values, scale, gain, grad):
    weighted = grad * gain
    inner = jnp.mean(weighted * values, axis=1, keepdims=True)
    return scale * weighted - values * (scale * scale * scale) * inner


def shards(
    inputs,
    cotangent,
    routed,
    doc_starts,
    router,
    attn_gain,
    qkv_weight,
    out_weight,
    mlp_gain,
    up_weight,
    down_weight,
):
    seqs = lax.axis_size("seq")
    fsdps = lax.axis_size("fsdp")
    me = lax.axis_index("seq")
    width = inputs.shape[2]
    tok_count = inputs.shape[1]
    own_windows = tok_count // WIN
    windows = routed.shape[1]
    tile = routed.shape[2]
    own_rows = own_windows * tile
    rows = windows * tile
    heads_width = width // seqs
    hidden = up_weight.shape[1]
    own_hidden = hidden // seqs

    order = jnp.arange(seqs, dtype=jnp.int32) ^ me
    window_of = (order[:, None] * own_windows + jnp.arange(own_windows, dtype=jnp.int32)).reshape(-1)
    stream_pos = jnp.arange(windows, dtype=jnp.int32)[:, None] * WIN + routed[0]
    pos = stream_pos[window_of].reshape(-1)
    starts = doc_starts[0]
    start = jnp.max(jnp.where(starts[None, :] <= pos[:, None], starts[None, :], 0), axis=1)
    first_window = start.reshape(windows, tile)[:, 0] // WIN
    place_of = jnp.zeros((windows,), jnp.int32).at[window_of].set(jnp.arange(windows, dtype=jnp.int32))
    tables = (window_of, place_of, first_window)

    own_routes = lax.dynamic_slice_in_dim(routed[0], me * own_windows, own_windows, 0)
    row_ids = ((jnp.arange(own_windows, dtype=jnp.int32) * WIN)[:, None] + own_routes).reshape(-1)
    stream_in = inputs[0]
    grad_in = cotangent[0]
    picked = jnp.concatenate([stream_in[row_ids], grad_in[row_ids]], axis=1)

    heads = lambda w: lax.dynamic_slice_in_dim(w, me * heads_width, heads_width, 1)
    qkv_own = jnp.concatenate(
        [heads(qkv_weight[:, i * width : (i + 1) * width]) for i in range(3)]
        + [
            jnp.stack([router, attn_gain, mlp_gain], axis=1),
            jnp.zeros((router.shape[0], LANES - 3), BF16),
        ],
        axis=1,
    )
    qkv_full = lax.all_gather(qkv_own, "fsdp", axis=0, tiled=True)
    w_qkv = qkv_full[:, : 3 * heads_width]
    vectors = qkv_full[:, 3 * heads_width : 3 * heads_width + 3].astype(F32).T
    router_w, gain_a, gain_m = vectors[0:1], vectors[1:2], vectors[2:3]
    w_out = lax.all_gather(out_weight, "fsdp", axis=0, tiled=True)
    w_up = lax.all_gather(
        lax.dynamic_slice_in_dim(up_weight, me * own_hidden, own_hidden, 1), "fsdp", axis=0, tiled=True
    )
    piece = hidden // (seqs * fsdps)
    down_piece = lax.dynamic_slice_in_dim(down_weight, me * piece, piece, 0)
    down_piece = lax.ppermute(
        down_piece,
        ("seq", "fsdp"),
        [(s * fsdps + f, f * seqs + s) for s in range(seqs) for f in range(fsdps)],
    )
    w_down = lax.all_gather(down_piece, "fsdp", axis=0, tiled=True)

    both = gather_blocks(picked, "seq")
    x_rows = jnp.concatenate([b[:, :width] for b in both], axis=0)
    g_rows = jnp.concatenate([b[:, width:] for b in both], axis=0).astype(F32)
    x_f = x_rows.astype(F32)
    rate = jax.nn.sigmoid(mm(x_rows, router_w.astype(BF16), NT))
    scale_a = lax.rsqrt(jnp.mean(x_f * x_f, axis=1, keepdims=True) + EPS)
    normal_a = (x_f * scale_a * gain_a).astype(BF16)
    proj = mm(normal_a, w_qkv, NN).astype(BF16)
    q, k, v = (proj[:, i * heads_width : (i + 1) * heads_width] for i in range(3))
    att_own, lse = attention_forward(tables, q, k, v, pos, start, tile)

    att_blocks = gather_blocks(att_own, "seq")
    out_blocks = [
        lax.dynamic_slice_in_dim(w_out, (me ^ b) * heads_width, heads_width, 0) for b in range(seqs)
    ]
    cut = lambda a, b: a[b * own_rows : (b + 1) * own_rows]
    att = jnp.concatenate(
        [
            jnp.concatenate([cut(blk, j ^ b) for j in range(seqs)], axis=0)
            for b, blk in enumerate(att_blocks)
        ],
        axis=1,
    )
    out_ordered = jnp.concatenate(out_blocks, axis=0)
    branch_a = mm(att, out_ordered, NN)
    middle = x_f + branch_a
    scale_m = lax.rsqrt(jnp.mean(middle * middle, axis=1, keepdims=True) + EPS)
    normal_m = (middle * scale_m * gain_m).astype(BF16)
    pre_act = mm(normal_m, w_up, NN)
    cdf = 0.5 * (1.0 + lax.erf(pre_act * (0.5**0.5)))
    activated = (pre_act * cdf).astype(BF16)
    slope = cdf + pre_act * (jnp.exp(-0.5 * pre_act * pre_act) * (2.0 * jnp.pi) ** -0.5)

    carried = rate * g_rows
    carried_b = carried.astype(BF16)
    grad_act = mm(carried_b, w_down, NT)
    grad_pre = (grad_act * slope).astype(BF16)
    grad_normal_m = scatter_blocks([mm(cut(grad_pre, b), w_up, NT) for b in range(seqs)], "seq")
    middle_o = cut(middle, 0)
    scale_mo = cut(scale_m, 0)
    grad_middle = norm_back(middle_o, scale_mo, gain_m, grad_normal_m)
    gain_m_part = jnp.sum(grad_normal_m * middle_o * scale_mo, axis=0)
    grad_a_own = (cut(carried, 0) + grad_middle).astype(BF16)
    grad_a = jnp.concatenate(gather_blocks(grad_a_own, "seq"), axis=0)
    grad_att = mm(grad_a, out_blocks[0], NT).astype(BF16)
    dq, dk, dv = attention_backward(tables, q, k, v, grad_att, lse, pos, start, tile)
    grad_proj = jnp.concatenate([dq, dk, dv], axis=1)
    grad_normal_a = scatter_blocks([mm(cut(grad_proj, b), w_qkv, NT) for b in range(seqs)], "seq")

    branch_f = scatter_blocks([mm(cut(activated, b), w_down, NN) for b in range(seqs)], "seq")

    x_o, g_o, rate_o, scale_ao = (cut(a, 0) for a in (x_f, g_rows, rate, scale_a))
    branch_sum = cut(branch_a, 0) + branch_f
    result = x_o + rate_o * branch_sum
    output = stream_in.at[row_ids].set(result.astype(BF16))
    grad_norm_x = norm_back(x_o, scale_ao, gain_a, grad_normal_a)
    gain_a_part = jnp.sum(grad_normal_a * x_o * scale_ao, axis=0)
    grad_logit = jnp.sum(g_o * branch_sum, axis=1, keepdims=True) * rate_o * (1.0 - rate_o)
    router_part = jnp.sum(x_o * grad_logit, axis=0)
    grad_picked = g_o + grad_middle + grad_norm_x + grad_logit * router_w
    input_grad = grad_in.at[row_ids].set(grad_picked.astype(BF16))

    def reduce_rows(parts):
        cols = parts.shape[1]
        per = width // (seqs * fsdps)
        parts = parts.reshape(seqs, fsdps, per, cols).transpose(1, 0, 2, 3)
        mine = lax.psum_scatter(parts.astype(BF16), "fsdp", scatter_dimension=0, tiled=False)
        return lax.all_to_all(mine, "seq", split_axis=0, concat_axis=0, tiled=True)

    down_sum = lax.psum_scatter(
        mm(activated, carried_b, TN).astype(BF16), "fsdp", scatter_dimension=0, tiled=True
    ).astype(F32)
    up_sum = reduce_rows(mm(normal_m, grad_pre, TN))
    up_sum = up_sum.transpose(1, 0, 2).reshape(-1, hidden).astype(F32)
    out_sum = lax.psum_scatter(
        mm(att_own, grad_a, TN).astype(BF16), "fsdp", scatter_dimension=0, tiled=True
    ).astype(F32)
    small = jnp.stack([router_part, gain_a_part, gain_m_part], axis=1)
    small = jnp.concatenate([small, jnp.zeros((width, LANES - 3), F32)], axis=1)
    qkv_sum = reduce_rows(jnp.concatenate([mm(normal_a, grad_proj, TN), small], axis=1))
    per = qkv_sum.shape[1]
    tiny = jnp.sum(qkv_sum[:, :, 3 * heads_width : 3 * heads_width + 3].astype(F32), axis=0)
    qkv_sum = qkv_sum[:, :, : 3 * heads_width].reshape(seqs, per, 3, heads_width)
    qkv_sum = qkv_sum.transpose(1, 2, 0, 3).reshape(per, 3 * width).astype(F32)
    return (
        output[None],
        input_grad[None],
        tiny[:, 0],
        tiny[:, 1],
        qkv_sum,
        out_sum,
        tiny[:, 2],
        up_sum,
        down_sum,
    )


def solution(mesh):
    return jax.shard_map(
        shards,
        mesh=mesh,
        in_specs=(
            P("fsdp", "seq", None),
            P("fsdp", "seq", None),
            P("fsdp", None, None),
            P("fsdp", None),
            P("fsdp"),
            P("fsdp"),
            P("fsdp", None),
            P("fsdp", None),
            P("fsdp"),
            P("fsdp", None),
            P("fsdp", None),
        ),
        out_specs=(
            P("fsdp", "seq", None),
            P("fsdp", "seq", None),
            P(("seq", "fsdp")),
            P(("seq", "fsdp")),
            P(("seq", "fsdp"), None),
            P(("seq", "fsdp"), None),
            P(("seq", "fsdp")),
            P(("seq", "fsdp"), None),
            P(("seq", "fsdp"), None),
        ),
        check_vma=False,
    )
```

time: 1490 us -> 587 us (0.39)
  waiting for transfers between devices: 1120 us -> 345 us
  blocking collectives: 97.5 us -> 0 us
  matrix products: 138 us -> 62.9 us
  Pallas kernels: 0 us -> 39.4 us
  local copies, waits for them, and re-layouts: 40.8 us -> 62 us
    reduce_scatter x4 -> x3, waiting for transfers between devices: 822 us -> 166 us  [the longest x1 68.3 us: reduce_rows(): lax.psum_scatter(parts.astype(BF16), 'fsdp', scatter_dimension=0, tiled=F...]
    all_gather x4, waiting for transfers between devices: 254 us -> 88.5 us  [the longest x1 41.2 us: shards(): w_down = lax.all_gather(down_piece, 'fsdp', axis=0, tiled=True)]
    dot_general x28 -> x22, matrix products: 138 us -> 62.9 us  [mm(): return lax.dot_general(a, b, (dims, ((), ())), preferred_element_type=F32)]
    ppermute x0 -> x19, waiting for transfers between devices: none -> 66.3 us  [the longest x18 66.3 us: flip(): return lax.ppermute(values, axis, [(j, j ^ bit) for j in range(count)])]
    all_gather x3 -> x0, blocking collectives: 46.4 us -> none  [the longest x1 18 us: shards(): lax.all_gather(attn_gain, 'fsdp', axis=0, tiled=True)]
    unnamed x1 -> x0, blocking collectives: 39.8 us -> none
    pallas_call x0 -> x2, Pallas kernels: none -> 39.4 us  [the longest x1 22.3 us: attention_backward(): pl.pallas_call(attention_backward_kernel, grid_spec=pltpu.PrefetchScalarG...]
    all_to_all x7 -> x2, waiting for transfers between devices: 38.4 us -> 5.17 us  [reduce_rows(): return lax.all_to_all(mine, 'seq', split_axis=0, concat_axis=0, tiled=True)]
  transfers between devices with their start and end apart: 15 -> 29, of which waited for: 12 -> 13; matrix products, arithmetic and copies ran while one was open for 12% -> 21% of each run, Pallas kernels for 0% -> 7%
where the time goes in v1:
time: 587 us; the launch traced here: 576 us
  waiting for transfers between devices  345 us (59%)
  matrix products  62.9 us (11%)
  local copies, waits for them, and re-layouts  62 us (11%)
  Pallas kernels  39.4 us (7%)
  starting transfers between devices  31.8 us (5%)
  other arithmetic  19.4 us (3%)
  between operations  15.7 us (3%)
    reduce_scatter x1, waiting for transfers between devices, reduce_rows(): lax.psum_scatter(parts.astype(BF16), 'fsdp', scatter_dimension=0, tiled=F...  68.3 us
    ppermute x18, waiting for transfers between devices, flip(): return lax.ppermute(values, axis, [(j, j ^ bit) for j in range(count)])  66.3 us
    dot_general x22, matrix products, mm(): return lax.dot_general(a, b, (dims, ((), ())), preferred_element_type=F32)  62.9 us
    reduce_scatter x1, waiting for transfers between devices, shards(): lax.psum_scatter(mm(att_own, grad_a, TN).astype(BF16), 'fsdp', scatter_di...  50.5 us
    reduce_scatter x1, waiting for transfers between devices, shards(): lax.psum_scatter(mm(activated, carried_b, TN).astype(BF16), 'fsdp', scatt...  47.6 us
    all_gather x1, waiting for transfers between devices, shards(): w_down = lax.all_gather(down_piece, 'fsdp', axis=0, tiled=True)  41.2 us
    all_gather x1, waiting for transfers between devices, shards(): lax.all_gather(lax.dynamic_slice_in_dim(up_weight, me * own_hidden, own_h...  38.9 us
    pallas_call x1, Pallas kernels, attention_backward(): pl.pallas_call(attention_backward_kernel, grid_spec=pltpu.PrefetchScalarG...  22.3 us
  transfers between devices with their start and end apart: 29, of which 13 were waited for; matrix products, arithmetic and copies ran while one was open for 21% of the time, Pallas kernels for 7%

profile of v1, /device:TPU:1, one launch (start us, length us, event | category | flops | bytes accessed | tf_op | source)
XLA Modules:
  0.0 575.9 jit_solution(12802362230775238607)
XLA Ops:
  7.2 4.8 copy.217
  17.2 4.3 gather_fusion
  21.7 4.5 gather_fusion.1
  31.5 3.0 collective-permute-start.6
  35.2 27.7 %collective-permute-done.1 = bf16[256,2048]{0,1:T(8,128)(2,1)} collective-permute-done((bf16[256,2048]{0,1:T(8,128)(2,1)}, bf16[256,2048]{0,1:T(8,128)(2,1)}, u32[]{:S(2)}, u32[]{:S(2)}) %collective-permute-start.1) | collective-permute-done | bytes 1048608 | tf_op jit(solution)/shard_map/ppermute | solution.py:32
  78.7 3.6 convolution_convert_fusion.3
  82.4 17.1 %attention_forward.1 = (bf16[1024,256]{1,0:T(8,128)(2,1)S(1)}, f32[1024,128]{1,0:T(8,128)S(1)}) custom-call(s32[4]{0:T(128)S(1)} %iota_xor_fusion.window_ref, s32[4]{0:T(128)S(1)} %scatter_custom_fusion.place_ref, s32[4]{0:T(128)S(1)} %and_select_fusion.first_ref, bf16[1024,256]{1,0:T(8,128)(2,1)S(1)} %get-tuple-element.40.q_ref, ...), custom_call_target="tpu_custom_call" | custom-call | flops 536870912 | bytes 2097152 | tf_op jit(solution)/shard_map/attention_forward/pallas_call | solution.py:212
  106.5 7.8 %collective-permute-done.4 = bf16[1024,256]{1,0:T(8,128)(2,1)} collective-permute-done((bf16[1024,256]{1,0:T(8,128)(2,1)S(1)}, bf16[1024,256]{1,0:T(8,128)(2,1)}, u32[]{:S(2)}, u32[]{:S(2)}) %collective-permute-start.4) | collective-permute-done | bytes 524320 | tf_op jit(solution)/shard_map/ppermute | solution.py:32
  114.9 8.4 %all-gather.7.cloned.1.call-done = bf16[1024,1024]{1,0:T(8,128)(2,1)} async-done(((bf16[128,1024]{1,0:T(8,128)(2,1)}), bf16[1024,1024]{1,0:T(8,128)(2,1)}) %all-gather.7.cloned.1.call-update) | async-done | bytes 2097168 | tf_op jit(solution)/shard_map/all_gather | solution.py:348
  128.7 6.2 %multiply_reduce_fusion = (f32[1024]{0:T(1024)S(1)}, f32[1024,1024]{0,1:T(8,128)}, f32[1024,1024]{0,1:T(8,128)}) fusion(bf16[256,1024]{0,1:T(8,128)(2,1)S(1)} %copy-done.30, bf16[256,1024]{0,1:T(8,128)(2,1)S(1)} %copy-done.22, bf16[256,1024]{0,1:T(8,128)(2,1)S(1)} %copy-done.26, bf16[256,1024]{0,1:T(8,128)(2,1)S(1)} %copy-done.14, ...), kind=kOutput, calls=%fused_computation.16 | convolution fusion | flops 2190474240 | bytes 14684160 | tf_op jit(solution)/shard_map/dot_general | solution.py:22
  134.9 38.9 %all-gather.9.cloned.1.call-done = bf16[1024,1024]{1,0:T(8,128)(2,1)} async-done(((bf16[128,1024]{1,0:T(8,128)(2,1)}), bf16[1024,1024]{1,0:T(8,128)(2,1)}) %all-gather.9.cloned.1.call-update) | async-done | bytes 2097168 | tf_op jit(solution)/shard_map/all_gather | solution.py:349
  173.8 8.6 %multiply_convert_fusion = (bf16[1024,1024]{1,0:T(8,128)(2,1)}, f32[1024,1024]{1,0:T(8,128)}) fusion(bf16[1024,1024]{1,0:T(8,128)(2,1)} %all-gather.9.cloned.1.call-done, f32[1024,1024]{0,1:T(8,128)} %get-tuple-element.32, f32[1024]{0:T(1024)S(1)} %get-tuple-element.25, f32[1024]{0:T(1024)S(1)} %add_rsqrt_fusion), kind=kOutput, calls=%fused_computation.13 | convolution fusion | flops 2155872256 | bytes 12591104 | tf_op jit(solution)/shard_map/dot_general | solution.py:22
  182.3 41.2 %all-gather.11.cloned.1.call-done = bf16[1024,1024]{1,0:T(8,128)(2,1)} async-done(((bf16[128,1024]{1,0:T(8,128)(2,1)}), bf16[1024,1024]{1,0:T(8,128)(2,1)}) %all-gather.11.cloned.1.call-update) | async-done | bytes 2097168 | tf_op jit(solution)/shard_map/all_gather | solution.py:359
  223.6 7.0 %fusion.5 = bf16[1024,1024]{1,0:T(8,128)(2,1)S(1)} fusion(f32[1024,1024]{1,0:T(8,128)} %get-tuple-element.64, bf16[1024,1024]{1,0:T(8,128)(2,1)} %all-gather.11.cloned.1.call-done, f32[1024]{0:T(1024)S(1)} %add_divide_fusion, bf16[256,1024]{0,1:T(8,128)(2,1)} %copy-done.38, bf16[256,1024]{0,1:T(8,128)(2,1)} %copy-done.32, bf16[256,1024]{0,1:T(8,128)(2,1)} %copy-done.35, ...), kind=kOutput, calls=%fused_computation.12 | convolution fusion | flops 2168455168 | bytes 10489856 | tf_op jit(solution)/shard_map/dot_general | solution.py:22
  242.3 9.7 %collective-permute-done.12 = bf16[256,1024]{0,1:T(8,128)(2,1)S(1)} collective-permute-done((bf16[256,1024]{0,1:T(8,128)(2,1)S(1)}, bf16[256,1024]{0,1:T(8,128)(2,1)S(1)}, u32[]{:S(2)}, u32[]{:S(2)}) %collective-permute-start.12) | collective-permute-done | bytes 524320 | tf_op jit(solution)/shard_map/ppermute | solution.py:32
  257.1 3.8 convolution_convert_fusion.1
  263.9 10.6 %collective-permute-done.14 = bf16[256,1024]{0,1:T(8,128)(2,1)} collective-permute-done((bf16[256,1024]{0,1:T(8,128)(2,1)}, bf16[256,1024]{0,1:T(8,128)(2,1)}, u32[]{:S(2)}, u32[]{:S(2)}) %collective-permute-start.14) | collective-permute-done | bytes 524320 | tf_op jit(solution)/shard_map/ppermute | solution.py:32
  275.9 4.5 multiply_reduce_fusion.5
  282.7 22.3 %attention_backward.1 = (bf16[1024,256]{1,0:T(8,128)(2,1)S(1)}, bf16[4,256,256]{2,1,0:T(8,128)(2,1)S(1)}, bf16[4,256,256]{2,1,0:T(8,128)(2,1)S(1)}) custom-call(s32[4]{0:T(128)S(1)} %iota_xor_fusion.window_ref, s32[4]{0:T(128)S(1)} %scatter_custom_fusion.place_ref, s32[4]{0:T(128)S(1)} %and_select_fusion.first_ref, ...), custom_call_target="tpu_custom_call" | custom-call | flops 1342177280 | bytes 3670016 | tf_op jit(solution)/shard_map/attention_backward/pallas_call | solution.py:246
  317.4 10.4 %collective-permute-done.18 = bf16[256,1024]{0,1:T(8,128)(2,1)S(1)} collective-permute-done((bf16[256,1024]{0,1:T(8,128)(2,1)S(1)}, bf16[256,1024]{0,1:T(8,128)(2,1)S(1)}, u32[]{:S(2)}, u32[]{:S(2)}) %collective-permute-start.18) | collective-permute-done | bytes 524320 | tf_op jit(solution)/shard_map/ppermute | solution.py:32
  327.8 3.6 multiply_reduce_fusion.3
  334.3 4.2 concatenate.64
  338.6 5.5 convolution_convert_fusion
  344.7 17.4 %all-reduce.3.cloned.1.call-done = bf16[8,4,32,1024]{3,2,0,1:T(8,128)(2,1)} async-done(((bf16[8,4,32,1024]{3,2,0,1:T(8,128)(2,1)}), bf16[8,4,32,1024]{3,2,0,1:T(8,128)(2,1)}) %all-reduce.3.cloned.1.call-update) | async-done | bytes 2097168
  364.5 4.3 all-to-all-start.1
  368.7 5.2 all-to-all-done.1
  374.8 50.5 %reduce-scatter.9.cloned.1.call-done = bf16[32,1024]{1,0:T(8,128)(2,1)} async-done(((bf16[256,1024]{1,0:T(8,128)(2,1)}), bf16[32,1024]{1,0:T(8,128)(2,1)}) %reduce-scatter.9.cloned.1.call-update) | async-done | bytes 65552 | tf_op jit(solution)/shard_map/reduce_scatter | solution.py:435
  426.8 68.3 %reduce-scatter.7.cloned.1.call-done = bf16[1,4,32,896]{3,2,1,0:T(8,128)(2,1)} async-done(((bf16[8,4,32,896]{3,2,1,0:T(8,128)(2,1)}), bf16[1,4,32,896]{3,2,1,0:T(8,128)(2,1)}) %reduce-scatter.7.cloned.1.call-update) | async-done | bytes 229392 | tf_op jit(solution)/shard_map/reduce_scatter | solution.py:427
  495.1 5.5 all-to-all-start
  503.4 6.6 %scatter_fusion.1 = bf16[2048,1024]{1,0:T(8,128)(2,1)} fusion(bf16[2048,1024]{1,0:T(8,128)(2,1)} %bitcast.84, s32[256]{0:T(256)S(1)} %bitcast.97, bf16[256,1024]{1,0:T(8,128)(2,1)S(1)} %copy.187), kind=kCustom, calls=%fused_computation.5 | custom fusion | bytes 1573888 | tf_op jit(solution)/shard_map/scatter | solution.py:421
  510.3 6.7 %scatter_fusion = bf16[2048,1024]{1,0:T(8,128)(2,1)} fusion(bf16[2048,1024]{1,0:T(8,128)(2,1)} %bitcast.81, s32[256]{0:T(256)S(1)} %bitcast.98, bf16[256,1024]{1,0:T(8,128)(2,1)S(1)} %copy.175), kind=kCustom, calls=%fused_computation.4 | custom fusion | bytes 1573888 | tf_op jit(solution)/shard_map/scatter | solution.py:415
  517.0 47.6 %reduce-scatter.11.cloned.1.call-done = bf16[128,1024]{1,0:T(8,128)(2,1)} async-done(((bf16[1024,1024]{1,0:T(8,128)(2,1)}), bf16[128,1024]{1,0:T(8,128)(2,1)}) %reduce-scatter.11.cloned.1.call-update) | async-done | bytes 262160 | tf_op jit(solution)/shard_map/reduce_scatter | solution.py:430
  (275 shorter events, 90.2 us)
Async XLA Ops:
  7.2 69.7 %all-gather.5.cloned.1.call-start = ((), (), s32[]{:S(2)}) async-start(), calls=%async_computation.5 | async-start | bytes 2064384 | tf_op jit(solution)/shard_map/all_gather | solution.py:344
  15.5 107.8 %all-gather.7.cloned.1.call-start = ((), (), s32[]{:S(2)}) async-start(), calls=%async_computation.6 | async-start | bytes 2359296 | tf_op jit(solution)/shard_map/all_gather | solution.py:348
  16.2 157.5 %all-gather.9.cloned.1.call-start = ((), (), s32[]{:S(2)}) async-start(), calls=%async_computation.7 | async-start | bytes 2359296 | tf_op jit(solution)/shard_map/all_gather | solution.py:349
  17.1 206.5 %all-gather.11.cloned.1.call-start = ((), (), s32[]{:S(2)}) async-start(), calls=%async_computation.8 | async-start | bytes 2359296 | tf_op jit(solution)/shard_map/all_gather | solution.py:359
  27.5 35.4 %collective-permute-start.1 = (bf16[256,2048]{0,1:T(8,128)(2,1)}, bf16[256,2048]{0,1:T(8,128)(2,1)}, u32[]{:S(2)}, u32[]{:S(2)}) collective-permute-start(bf16[256,2048]{0,1:T(8,128)(2,1)} %pad_maximum_fusion.3), channel_id=1, source_target_pairs={{0,16},{8,24},{16,0},{24,8},{1,17},{9,25},{17,1},{25,9},{2,18},{10... | collective-permute-start | bytes 3145736 | tf_op jit(solution)/shard_map/ppermute | solution.py:32
  29.5 38.4 %collective-permute-start = (bf16[256,2048]{0,1:T(8,128)(2,1)}, bf16[256,2048]{0,1:T(8,128)(2,1)}, u32[]{:S(2)}, u32[]{:S(2)}) collective-permute-start(bf16[256,2048]{0,1:T(8,128)(2,1)} %pad_maximum_fusion.3), channel_id=1, source_target_pairs={{0,8},{8,0},{16,24},{24,16},{1,9},{9,1},{17,25},{25,17},{2,10},{10... | collective-permute-start | bytes 3145736 | tf_op jit(solution)/shard_map/ppermute | solution.py:32
  31.5 34.4 %collective-permute-start.6 = (bf16[128,1024]{1,0:T(8,128)(2,1)S(1)}, bf16[128,1024]{1,0:T(8,128)(2,1)S(1)}, u32[]{:S(2)}, u32[]{:S(2)}) collective-permute-start(bf16[128,1024]{1,0:T(8,128)(2,1)S(1)} %constant_dynamic-slice_fusion), channel_id=1, source_target_pairs={{0,0},{1,4},{2,8},{3,12},{4,16},{5,20},{6,24},{7,28},{8,1},{9,5},{... | collective-permute-start | bytes 786440 | tf_op jit(solution)/shard_map/ppermute | solution.py:354
  62.9 6.7 %collective-permute-start.2 = (bf16[256,2048]{0,1:T(8,128)(2,1)}, bf16[256,2048]{0,1:T(8,128)(2,1)}, u32[]{:S(2)}, u32[]{:S(2)}) collective-permute-start(bf16[256,2048]{0,1:T(8,128)(2,1)} %collective-permute-done.1), channel_id=1, source_target_pairs={{0,8},{8,0},{16,24},{24,16},{1,9},{9,1},{17,25},{25,17},{2,10},{10... | collective-permute-start | bytes 3145736 | tf_op jit(solution)/shard_map/ppermute | solution.py:32
  66.5 295.6 %all-reduce.3.cloned.1.call-start = ((), (), s32[]{:S(2)}) async-start(), calls=%async_computation.12 | async-start | bytes 4194304
  99.6 14.7 %collective-permute-start.4 = (bf16[1024,256]{1,0:T(8,128)(2,1)S(1)}, bf16[1024,256]{1,0:T(8,128)(2,1)}, u32[]{:S(2)}, u32[]{:S(2)}) collective-permute-start(bf16[1024,256]{1,0:T(8,128)(2,1)S(1)} %get-tuple-element.14), channel_id=1, source_target_pairs={{0,16},{8,24},{16,0},{24,8},{1,17},{9,25},{17,1},{25,9},{2,18},{10... | collective-permute-start | bytes 1572872 | tf_op jit(solution)/shard_map/ppermute | solution.py:32
  101.9 23.3 %collective-permute-start.3 = (bf16[1024,256]{1,0:T(8,128)(2,1)S(1)}, bf16[1024,256]{1,0:T(8,128)(2,1)}, u32[]{:S(2)}, u32[]{:S(2)}) collective-permute-start(bf16[1024,256]{1,0:T(8,128)(2,1)S(1)} %get-tuple-element.14), channel_id=1, source_target_pairs={{0,8},{8,0},{16,24},{24,16},{1,9},{9,1},{17,25},{25,17},{2,10},{10... | collective-permute-start | bytes 1572872 | tf_op jit(solution)/shard_map/ppermute | solution.py:32
  114.3 13.3 %collective-permute-start.5 = (bf16[1024,256]{1,0:T(8,128)(2,1)}, bf16[1024,256]{1,0:T(8,128)(2,1)}, u32[]{:S(2)}, u32[]{:S(2)}) collective-permute-start(bf16[1024,256]{1,0:T(8,128)(2,1)} %collective-permute-done.4), channel_id=1, source_target_pairs={{0,8},{8,0},{16,24},{24,16},{1,9},{9,1},{17,25},{25,17},{2,10},{10... | collective-permute-start | bytes 1572872 | tf_op jit(solution)/shard_map/ppermute | solution.py:32
  231.4 6.8 %collective-permute-start.11 = (bf16[256,1024]{0,1:T(8,128)(2,1)S(1)}, bf16[256,1024]{0,1:T(8,128)(2,1)S(1)}, u32[]{:S(2)}, u32[]{:S(2)}) collective-permute-start(bf16[256,1024]{0,1:T(8,128)(2,1)S(1)} %convolution_convert_fusion.6), channel_id=1, source_target_pairs={{0,8},{8,0},{16,24},{24,16},{1,9},{9,1},{17,25},{25,17},{2,10},{10... | collective-permute-start | bytes 1572872 | tf_op jit(solution)/shard_map/ppermute | solution.py:32
  234.0 8.3 %collective-permute-start.10 = (bf16[256,1024]{0,1:T(8,128)(2,1)S(1)}, bf16[256,1024]{0,1:T(8,128)(2,1)S(1)}, u32[]{:S(2)}, u32[]{:S(2)}) collective-permute-start(bf16[256,1024]{0,1:T(8,128)(2,1)S(1)} %convolution_convert_fusion.7), channel_id=1, source_target_pairs={{0,8},{8,0},{16,24},{24,16},{1,9},{9,1},{17,25},{25,17},{2,10},{10... | collective-permute-start | bytes 1572872 | tf_op jit(solution)/shard_map/ppermute | solution.py:32
  235.0 5.2 collective-permute-start.8
  237.4 38.5 %collective-permute-start.7 = (bf16[256,1024]{0,1:T(8,128)(2,1)}, bf16[256,1024]{0,1:T(8,128)(2,1)S(1)}, u32[]{:S(2)}, u32[]{:S(2)}) collective-permute-start(bf16[256,1024]{0,1:T(8,128)(2,1)} %convolution_convert_fusion.9), channel_id=1, source_target_pairs={{0,8},{8,0},{16,24},{24,16},{1,9},{9,1},{17,25},{25,17},{2,10},{10... | collective-permute-start | bytes 1572872 | tf_op jit(solution)/shard_map/ppermute | solution.py:32
  238.9 13.1 %collective-permute-start.12 = (bf16[256,1024]{0,1:T(8,128)(2,1)S(1)}, bf16[256,1024]{0,1:T(8,128)(2,1)S(1)}, u32[]{:S(2)}, u32[]{:S(2)}) collective-permute-start(bf16[256,1024]{0,1:T(8,128)(2,1)S(1)} %add_convert_fusion.2), channel_id=1, source_target_pairs={{0,16},{8,24},{16,0},{24,8},{1,17},{9,25},{17,1},{25,9},{2,18},{10... | collective-permute-start | bytes 1572872 | tf_op jit(solution)/shard_map/ppermute | solution.py:32
  242.0 33.9 %collective-permute-start.9 = (bf16[256,1024]{0,1:T(8,128)(2,1)}, bf16[256,1024]{0,1:T(8,128)(2,1)}, u32[]{:S(2)}, u32[]{:S(2)}) collective-permute-start(bf16[256,1024]{0,1:T(8,128)(2,1)} %fusion.36), channel_id=1, source_target_pairs={{0,16},{8,24},{16,0},{24,8},{1,17},{9,25},{17,1},{25,9},{2,18},{10... | collective-permute-start | bytes 1572872 | tf_op jit(solution)/shard_map/ppermute | solution.py:32
  255.9 18.7 %collective-permute-start.14 = (bf16[256,1024]{0,1:T(8,128)(2,1)}, bf16[256,1024]{0,1:T(8,128)(2,1)}, u32[]{:S(2)}, u32[]{:S(2)}) collective-permute-start(bf16[256,1024]{0,1:T(8,128)(2,1)} %fusion.37), channel_id=1, source_target_pairs={{0,16},{8,24},{16,0},{24,8},{1,17},{9,25},{17,1},{25,9},{2,18},{10... | collective-permute-start | bytes 1572872 | tf_op jit(solution)/shard_map/ppermute | solution.py:32
  260.9 164.5 %reduce-scatter.9.cloned.1.call-start = ((), (), s32[]{:S(2)}) async-start(), calls=%async_computation.10 | async-start | bytes 589824 | tf_op jit(solution)/shard_map/reduce_scatter | solution.py:435
  260.9 19.6 %collective-permute-start.13 = (bf16[256,1024]{0,1:T(8,128)(2,1)}, bf16[256,1024]{0,1:T(8,128)(2,1)}, u32[]{:S(2)}, u32[]{:S(2)}) collective-permute-start(bf16[256,1024]{0,1:T(8,128)(2,1)} %fusion.37), channel_id=1, source_target_pairs={{0,8},{8,0},{16,24},{24,16},{1,9},{9,1},{17,25},{25,17},{2,10},{10... | collective-permute-start | bytes 1572872 | tf_op jit(solution)/shard_map/ppermute | solution.py:32
  274.6 5.9 %collective-permute-start.15 = (bf16[256,1024]{0,1:T(8,128)(2,1)}, bf16[256,1024]{0,1:T(8,128)(2,1)S(1)}, u32[]{:S(2)}, u32[]{:S(2)}) collective-permute-start(bf16[256,1024]{0,1:T(8,128)(2,1)} %collective-permute-done.14), channel_id=1, source_target_pairs={{0,8},{8,0},{16,24},{24,16},{1,9},{9,1},{17,25},{25,17},{2,10},{10... | collective-permute-start | bytes 1572872 | tf_op jit(solution)/shard_map/ppermute | solution.py:32
  306.6 5.0 collective-permute-start.17
  308.1 9.3 %collective-permute-start.16 = (bf16[256,1024]{0,1:T(8,128)(2,1)}, bf16[256,1024]{0,1:T(8,128)(2,1)}, u32[]{:S(2)}, u32[]{:S(2)}) collective-permute-start(bf16[256,1024]{0,1:T(8,128)(2,1)} %convolution_convert_fusion.11), channel_id=1, source_target_pairs={{0,8},{8,0},{16,24},{24,16},{1,9},{9,1},{17,25},{25,17},{2,10},{10... | collective-permute-start | bytes 1572872 | tf_op jit(solution)/shard_map/ppermute | solution.py:32
  311.6 183.6 %reduce-scatter.7.cloned.1.call-start = ((), (), s32[]{:S(2)}) async-start(), calls=%async_computation.9 | async-start | bytes 2064384 | tf_op jit(solution)/shard_map/reduce_scatter | solution.py:427
  314.1 13.7 %collective-permute-start.18 = (bf16[256,1024]{0,1:T(8,128)(2,1)S(1)}, bf16[256,1024]{0,1:T(8,128)(2,1)S(1)}, u32[]{:S(2)}, u32[]{:S(2)}) collective-permute-start(bf16[256,1024]{0,1:T(8,128)(2,1)S(1)} %add_convert_fusion.1), channel_id=1, source_target_pairs={{0,16},{8,24},{16,0},{24,8},{1,17},{9,25},{17,1},{25,9},{2,18},{10... | collective-permute-start | bytes 1572872 | tf_op jit(solution)/shard_map/ppermute | solution.py:32
  338.5 226.1 %reduce-scatter.11.cloned.1.call-start = ((), (), s32[]{:S(2)}) async-start(), calls=%async_computation.11 | async-start | bytes 2359296 | tf_op jit(solution)/shard_map/reduce_scatter | solution.py:430
  344.1 156.6 %copy-start.11 = (f32[256,1024]{0,1:T(8,128)S(1)}, f32[256,1024]{0,1:T(8,128)}, u32[]{:S(2)}) copy-start(f32[256,1024]{0,1:T(8,128)} %copy-done.10) | copy-start | bytes 3145732
  344.1 156.6 %copy-start.45 = (f32[256,1024]{0,1:T(8,128)S(1)}, f32[256,1024]{0,1:T(8,128)}, u32[]{:S(2)}) copy-start(f32[256,1024]{0,1:T(8,128)} %get-tuple-element.67) | copy-start | bytes 3145732
  344.1 156.6 %copy-start.52 = (bf16[256,1024]{0,1:T(8,128)(2,1)S(1)}, bf16[256,1024]{0,1:T(8,128)(2,1)}, u32[]{:S(2)}) copy-start(bf16[256,1024]{0,1:T(8,128)(2,1)} %copy-done.51) | copy-start | bytes 1572868
  364.5 9.4 %all-to-all-start.1 = ((bf16[4,32,1024]{2,1,0:T(8,128)(2,1)}), bf16[4,32,1024]{2,1,0:T(8,128)(2,1)S(1)}, u32[]{:S(2)}, u32[]{:S(2)}) async-start(bf16[4,32,1024]{2,1,0:T(8,128)(2,1)} %dynamic-slice_bitcast_fusion), calls=%async_computation.3 | async-start | bytes 524288 | tf_op jit(solution)/shard_map/all_to_all | solution.py:428
  495.1 71.3 %all-to-all-start = ((bf16[4,32,896]{2,1,0:T(8,128)(2,1)}), bf16[4,32,896]{2,1,0:T(8,128)(2,1)S(1)}, u32[]{:S(2)}, u32[]{:S(2)}) async-start(bf16[4,32,896]{2,1,0:T(8,128)(2,1)} %bitcast.91), calls=%async_computation.1 | async-start | bytes 458752 | tf_op jit(solution)/shard_map/all_to_all | solution.py:428
  (60 other events, 609.0 us)
Sparse Core Ops, SparseCore 0:
  15.6 55.7 all-gather.4
  73.5 49.7 all-gather.6
  126.0 47.7 all-gather.8
  175.8 47.7 all-gather.10
  261.0 101.1 all-reduce.2
  365.3 59.9 reduce-scatter.8
  429.2 65.9 reduce-scatter.6
  498.7 65.9 reduce-scatter.10

commit v2 on v1

v2 whole, which is shorter than its diff:
```python
from functools import partial

import jax
import jax.numpy as jnp
from jax import lax
from jax.experimental import pallas as pl
from jax.experimental.pallas import tpu as pltpu
from jax.sharding import PartitionSpec as P

H = 16
HD = 64
WIN = 2048
EPS = 1e-05
NEG_FILL = -1e30
PAIR = 2 * HD
LANES = 128
BF16 = jnp.bfloat16
F32 = jnp.float32
VMEM_LIMIT = 48 * 1024 * 1024


def mm(a, b, dims):
    return lax.dot_general(a, b, (dims, ((), ())), preferred_element_type=F32)


NN = ((1,), (0,))
NT = ((1,), (1,))
TN = ((0,), (0,))


def flip(values, axis, bit):
    count = lax.axis_size(axis)
    return lax.ppermute(values, axis, [(j, j ^ bit) for j in range(count)])


def bits_down(count):
    bit = count // 2
    while bit:
        yield bit
        bit //= 2


def gather_blocks(own, axis):
    blocks = {0: own}
    for bit in bits_down(lax.axis_size(axis)):
        for key in list(blocks):
            blocks[key ^ bit] = flip(blocks[key], axis, bit)
    return [blocks[key] for key in sorted(blocks)]


def scatter_blocks(blocks, axis):
    parts = dict(enumerate(blocks))
    bit = 1
    while bit < lax.axis_size(axis):
        for key in [k for k in parts if k & bit]:
            got = flip(parts.pop(key).astype(BF16), axis, bit)
            parts[key ^ bit] = parts[key ^ bit] + got.astype(F32)
        bit *= 2
    return parts[0]


def after(values, *earlier):
    earlier = [e for e in earlier if e is not None]
    return lax.optimization_barrier((values, *earlier))[0] if earlier else values


def fsdp_sizes():
    count = lax.axis_size("fsdp")
    fast = 2 ** ((count.bit_length() - 1) // 2)
    return count // fast, fast


def gather_slow(own, *waits):
    slow, fast = fsdp_sizes()
    own_late = after(own, *waits)
    return [own_late] + [flip(own_late, "fsdp", k * fast) for k in range(1, slow)]


def gather_fast(held, joined):
    _, fast = fsdp_sizes()
    held = [jnp.stack(held)] if joined else [h[None] for h in held]
    return held + [flip(h, "fsdp", k) for k in range(1, fast) for h in held]


def order_rows_kernel(me_ref, *refs, fast):
    slow = refs[-1].shape[0] // fast
    done = 0
    for ref in refs[:-1]:
        for i in range(ref.shape[0]):
            block = lax.rem(done, slow) * fast + lax.div(done, slow)
            refs[-1][me_ref[0] ^ block] = ref[i]
            done += 1


def order_rows(pieces):
    slow, fast = fsdp_sizes()
    rows, cols = pieces[0].shape[1:]
    whole = lambda shape: pl.BlockSpec(shape, lambda i, *_: (0,) * len(shape))
    out = pl.pallas_call(
        partial(order_rows_kernel, fast=fast),
        grid_spec=pltpu.PrefetchScalarGridSpec(
            num_scalar_prefetch=1,
            grid=(1,),
            in_specs=[whole(p.shape) for p in pieces],
            out_specs=whole((slow * fast, rows, cols)),
        ),
        out_shape=jax.ShapeDtypeStruct((slow * fast, rows, cols), BF16),
        compiler_params=pltpu.CompilerParams(vmem_limit_bytes=VMEM_LIMIT),
        cost_estimate=pl.CostEstimate(
            flops=0, transcendentals=0, bytes_accessed=4 * slow * fast * rows * cols
        ),
        name="order_rows",
    )(lax.axis_index("fsdp")[None], *pieces)
    return out.reshape(-1, cols)


def low_bits(count):
    bit = 1
    while bit < count:
        yield bit
        bit *= 2


def reduce_blocks(send, keep, first, waits):
    bits = [first] + [b for b in low_bits(lax.axis_size("fsdp")) if b != first]
    total = None
    for i, bit in enumerate(bits):
        got = flip(send, "fsdp", bit)
        total = keep.astype(F32) + got.astype(F32)
        if bit != bits[-1]:
            send = after(total[1::2].astype(BF16), *waits[min(i, len(waits) - 1)])
            keep = total[0::2]
    return total[0]


def join_columns_kernel(me_ref, *refs, groups, span):
    count = len(refs) - (1 if span * groups == refs[0].shape[1] else 2)
    tail = 0.0
    for k in range(count):
        for g in range(groups):
            start = pl.multiple_of((g * count + (me_ref[0] ^ k)) * span, span)
            refs[count][:, pl.ds(start, span)] = refs[k][:, g * span : (g + 1) * span].astype(F32)
        if refs[count + 1 :]:
            tail = tail + refs[k][:, groups * span :].astype(F32)
    for ref in refs[count + 1 :]:
        ref[...] = tail


def exchange_columns(blocks, groups, span):
    count, rows, cols = blocks.shape
    got = [blocks[0]] + [flip(blocks[k].astype(BF16), "seq", k) for k in range(1, count)]
    if span % LANES:
        me = lax.axis_index("seq")
        joined = jnp.zeros((rows, groups, count, span), F32)
        for k in range(count):
            part = got[k].astype(F32).reshape(rows, groups, 1, span)
            joined = lax.dynamic_update_slice_in_dim(joined, part, me ^ k, axis=2)
        return (joined.reshape(rows, -1),)
    out_shape = [jax.ShapeDtypeStruct((rows, count * groups * span), F32)]
    if cols > groups * span:
        out_shape.append(jax.ShapeDtypeStruct((rows, cols - groups * span), F32))
    return pl.pallas_call(
        partial(join_columns_kernel, groups=groups, span=span),
        grid_spec=pltpu.PrefetchScalarGridSpec(
            num_scalar_prefetch=1,
            grid=(1,),
            in_specs=[pl.BlockSpec((rows, cols), lambda i, *_: (0, 0))] * count,
            out_specs=[pl.BlockSpec(o.shape, lambda i, *_: (0, 0)) for o in out_shape],
        ),
        out_shape=out_shape,
        compiler_params=pltpu.CompilerParams(vmem_limit_bytes=VMEM_LIMIT),
        name="join_columns",
    )(lax.axis_index("seq")[None], *got)


GRAD_TILE = 512


def store_blocks(product, tail, column, place_ref, per, fsdps, first, refs):
    whole = product.astype(BF16)
    cols = product.shape[1]
    pieces = product.shape[0] // per
    for t in range(pieces):
        piece = column * pieces + t
        block = lax.rem(piece, fsdps)
        part = lax.div(piece, fsdps) ^ place_ref[1]
        rows = slice(t * per, (t + 1) * per)

        def store(ref, slot):
            ref[slot, part, :, :cols] = whole[rows]
            if tail is not None:
                ref[slot, part, :, cols:] = tail[rows]

        if first is None:
            store(refs[0], block)
            continue
        block = block ^ place_ref[0]
        slot = lax.div(block, 2 * first) * first + lax.rem(block, first)
        sent = lax.rem(lax.div(block, first), 2)
        pl.when(sent == 1)(partial(store, refs[0], slot))
        pl.when(sent == 0)(partial(store, refs[1], slot))


def weight_grad_kernel(place_ref, a_ref, b_ref, *refs, per, fsdps, first, gain_lane, with_logits, tail_out):
    column = pl.program_id(0)
    product = mm(a_ref[...], b_ref[...], TN)
    refs = list(refs)
    tail = None
    if gain_lane is not None:
        w_ref, vec_ref, other_ref = refs[:3]
        refs = refs[3:]
        lane = lax.broadcasted_iota(jnp.int32, (product.shape[0], LANES), 1)
        gain = vec_ref[...].astype(F32)[:, gain_lane : gain_lane + 1]
        gain_grad = jnp.sum(product * w_ref[...].astype(F32), axis=1, keepdims=True) / gain
        tail = jnp.where(lane == gain_lane, gain_grad, 0.0) + other_ref[...]
    if with_logits:
        x_ref, logit_ref = refs[:2]
        refs = refs[2:]
        tail = tail + mm(x_ref[...], logit_ref[...], TN)
    if tail_out:
        refs.pop()[...] = tail
    tail = tail.astype(BF16) if with_logits else None
    store_blocks(product, tail, column, place_ref, per, fsdps, first, refs)


def weight_grad(place, a, b, parts, first, gain=None, logits=None):
    rows, total = a.shape
    cols = b.shape[1]
    fsdps = lax.axis_size("fsdp")
    per = total // (parts * fsdps)
    tile = min(GRAD_TILE, total)
    wide = cols + (LANES if logits is not None else 0)
    columns = lambda n: pl.BlockSpec((n, tile), lambda c, *_: (0, c))
    lines = lambda n, at=0: pl.BlockSpec((tile, n), lambda c, *_: (c, at))
    whole = lambda *dims: pl.BlockSpec(dims, lambda c, *_: (0,) * len(dims))
    args, in_specs = [a, b], [columns(rows), whole(rows, cols)]
    copies = 1 if first is None else 2
    block = (fsdps // copies, parts, per, wide)
    out_shape = [jax.ShapeDtypeStruct(block, BF16)] * copies
    out_specs = [whole(*block)] * copies
    lane = None
    if gain is not None:
        weight, vectors, at, lane, other = gain
        args += [weight, vectors, other]
        in_specs += [lines(cols), lines(LANES, at), lines(LANES)]
    tail_out = gain is not None and logits is None
    if tail_out:
        out_shape = out_shape + [jax.ShapeDtypeStruct((total, LANES), F32)]
        out_specs = out_specs + [lines(LANES)]
    if logits is not None:
        args += list(logits)
        in_specs += [columns(logits[0].shape[0]), whole(*logits[1].shape)]
    return pl.pallas_call(
        partial(
            weight_grad_kernel,
            per=per,
            fsdps=fsdps,
            first=first,
            gain_lane=lane,
            with_logits=logits is not None,
            tail_out=tail_out,
        ),
        grid_spec=pltpu.PrefetchScalarGridSpec(
            num_scalar_prefetch=1,
            grid=(total // tile,),
            in_specs=in_specs,
            out_specs=out_specs,
        ),
        out_shape=out_shape,
        compiler_params=pltpu.CompilerParams(vmem_limit_bytes=VMEM_LIMIT),
        cost_estimate=pl.CostEstimate(
            flops=2 * rows * total * cols,
            transcendentals=0,
            bytes_accessed=2 * (rows * total + rows * cols + total * wide),
        ),
        name="weight_grad",
    )(place, *args)


def hidden_grads_kernel(
    place_ref, act_ref, carried_ref, norm_ref, pre_ref, w_ref, vec_ref, both_ref, tail_ref, *, per, down_per, fsdps, gain_lane
):
    column = pl.program_id(0)
    down = mm(act_ref[...], carried_ref[...], TN).astype(BF16)
    for t in range(down.shape[0] // down_per):
        both_ref[column * (down.shape[0] // down_per) + t, 1] = down[t * down_per : (t + 1) * down_per]
    product = mm(norm_ref[...], pre_ref[...], TN)
    lane = lax.broadcasted_iota(jnp.int32, (product.shape[0], LANES), 1)
    gain = vec_ref[...].astype(F32)[:, gain_lane : gain_lane + 1]
    gain_grad = jnp.sum(product * w_ref[...].astype(F32), axis=1, keepdims=True) / gain
    tail_ref[...] = jnp.where(lane == gain_lane, gain_grad, 0.0)
    up = product.astype(BF16)
    pieces = product.shape[0] // per
    for t in range(pieces):
        piece = column * pieces + t
        part = lax.div(piece, fsdps) ^ place_ref[1]
        line = pl.multiple_of(part * per, per)
        both_ref[lax.rem(piece, fsdps), 0, pl.ds(line, per), :] = up[t * per : (t + 1) * per]


def hidden_grads(place, activated, carried_b, normal_m, grad_pre, w_up, vectors, at, lane):
    rows, total = activated.shape
    cols = carried_b.shape[1]
    fsdps = lax.axis_size("fsdp")
    seqs = lax.axis_size("seq")
    tile = min(GRAD_TILE, total)
    columns = pl.BlockSpec((rows, tile), lambda c, *_: (0, c))
    lines = lambda n, at=0: pl.BlockSpec((tile, n), lambda c, *_: (c, at))
    whole = lambda *dims: pl.BlockSpec(dims, lambda c, *_: (0,) * len(dims))
    both = (fsdps, 2, total // fsdps, cols)
    return pl.pallas_call(
        partial(
            hidden_grads_kernel,
            per=total // (seqs * fsdps),
            down_per=total // fsdps,
            fsdps=fsdps,
            gain_lane=lane,
        ),
        grid_spec=pltpu.PrefetchScalarGridSpec(
            num_scalar_prefetch=1,
            grid=(total // tile,),
            in_specs=[columns, whole(rows, cols), columns, whole(rows, cols), lines(cols), lines(LANES, at)],
            out_specs=[whole(*both), lines(LANES)],
        ),
        out_shape=[jax.ShapeDtypeStruct(both, BF16), jax.ShapeDtypeStruct((total, LANES), F32)],
        compiler_params=pltpu.CompilerParams(vmem_limit_bytes=VMEM_LIMIT),
        cost_estimate=pl.CostEstimate(
            flops=4 * rows * total * cols,
            transcendentals=0,
            bytes_accessed=4 * (rows * total + rows * cols + total * cols),
        ),
        name="hidden_grads",
    )(place, activated, carried_b, normal_m, grad_pre, w_up, vectors)


def order_out_kernel(place_ref, *refs):
    out_ref = refs[-1]
    group, seqs = out_ref.shape[1:3]
    for k in range(seqs):
        for block in range(refs[k].shape[0]):
            shard = place_ref[0] ^ block
            at = lax.div(shard, group) ^ place_ref[1]
            out_ref[at, lax.rem(shard, group), place_ref[1] ^ k] = refs[k][block]


def order_out(place, blocks):
    seqs = len(blocks)
    fsdps, per, width = blocks[0].shape
    full = (seqs, fsdps // seqs, seqs, per, width)
    whole = lambda shape: pl.BlockSpec(shape, lambda i, *_: (0,) * len(shape))
    out = pl.pallas_call(
        order_out_kernel,
        grid_spec=pltpu.PrefetchScalarGridSpec(
            num_scalar_prefetch=1,
            grid=(1,),
            in_specs=[whole(blocks[0].shape)] * seqs,
            out_specs=whole(full),
        ),
        out_shape=jax.ShapeDtypeStruct(full, BF16),
        compiler_params=pltpu.CompilerParams(vmem_limit_bytes=VMEM_LIMIT),
        cost_estimate=pl.CostEstimate(flops=0, transcendentals=0, bytes_accessed=4 * width * width),
        name="order_out",
    )(place, *blocks)
    return out.reshape(-1, width)


ROW_TILE = 512


def pick_rows_kernel(ids_ref, from_ref, to_ref, total):
    chunk = pl.program_id(0)
    ids = ids_ref[...] - chunk * ROW_TILE
    hit = ids == lax.broadcasted_iota(jnp.int32, (ids.shape[0], ROW_TILE), 1)
    found = mm(jnp.where(hit, 1.0, 0.0).astype(BF16), from_ref[...], NN)

    @pl.when(chunk == 0)
    def _():
        total[...] = found

    @pl.when(chunk > 0)
    def _():
        total[...] += found

    to_ref[...] = total[...].astype(BF16)


def pick_rows(source, ids):
    length, width = source.shape
    rows = ids.shape[0]
    return pl.pallas_call(
        pick_rows_kernel,
        grid=(length // ROW_TILE,),
        in_specs=[
            pl.BlockSpec((rows, 1), lambda c: (0, 0)),
            pl.BlockSpec((ROW_TILE, width), lambda c: (c, 0)),
        ],
        out_specs=pl.BlockSpec((rows, width), lambda c: (0, 0)),
        out_shape=jax.ShapeDtypeStruct((rows, width), BF16),
        scratch_shapes=[pltpu.VMEM((rows, width), F32)],
        compiler_params=pltpu.CompilerParams(vmem_limit_bytes=VMEM_LIMIT),
        cost_estimate=pl.CostEstimate(
            flops=2 * rows * length * width, transcendentals=0, bytes_accessed=2 * length * width
        ),
        name="pick_rows",
    )(ids[:, None], source)


def place_rows_kernel(ids_ref, new_ref, from_ref, to_ref):
    ids = ids_ref[...] - pl.program_id(0) * ROW_TILE
    hit = ids == lax.broadcasted_iota(jnp.int32, (ROW_TILE, ids.shape[1]), 0)
    ones = jnp.where(hit, 1.0, 0.0)
    routed = jnp.max(ones, axis=1, keepdims=True) > 0.0
    new = mm(ones.astype(BF16), new_ref[...], NN).astype(BF16)
    to_ref[...] = jnp.where(routed, new, from_ref[...])


def place_rows(source, ids, new):
    length, width = source.shape
    rows = ids.shape[0]
    tiles = pl.BlockSpec((ROW_TILE, width), lambda c: (c, 0))
    return pl.pallas_call(
        place_rows_kernel,
        grid=(length // ROW_TILE,),
        in_specs=[
            pl.BlockSpec((1, rows), lambda c: (0, 0)),
            pl.BlockSpec((rows, width), lambda c: (0, 0)),
            tiles,
        ],
        out_specs=tiles,
        out_shape=jax.ShapeDtypeStruct((length, width), BF16),
        compiler_params=pltpu.CompilerParams(vmem_limit_bytes=VMEM_LIMIT),
        cost_estimate=pl.CostEstimate(
            flops=2 * rows * length * width, transcendentals=0, bytes_accessed=4 * length * width
        ),
        name="place_rows",
    )(ids[None, :], new, source)


def half_lanes(values, half):
    lane = lax.broadcasted_iota(jnp.int32, values.shape, 1)
    keep = lane < HD if half == 0 else lane >= HD
    return jnp.where(keep, values, jnp.zeros_like(values))


def allowed_tile(keys_ref, where, pos_row, start_row):
    keys = keys_ref[where]
    return (keys <= pos_row) & (keys >= start_row)


def attention_forward_kernel(
    window_ref, place_ref, first_ref, q_ref, k_ref, v_ref, pos_ref, start_ref, keys_ref, o_ref, lse_ref
):
    block = pl.program_id(0)
    tile, width = q_ref.shape
    heads = width // HD
    pos_row, start_row = pos_ref[0], start_ref[0]
    last = window_ref[block]
    count = last - first_ref[block] + 1
    lanes = [slice(h // 2 * PAIR, (h // 2 + 1) * PAIR) for h in range(heads)]
    scale = jnp.asarray(HD**-0.5, BF16)
    queries = [half_lanes(q_ref[:, lanes[h]] * scale, h % 2) for h in range(heads)]

    def step(i, carry):
        where = place_ref[last - i]
        allowed = allowed_tile(keys_ref, where, pos_row, start_row)
        new = []
        for h, (top, total, acc) in enumerate(carry):
            scores = jnp.where(allowed, mm(k_ref[where, :, lanes[h]], queries[h], NT), NEG_FILL)
            new_top = jnp.maximum(top, jnp.max(scores, axis=0, keepdims=True))
            shrink = jnp.exp(top - new_top)
            exponent = jnp.exp(scores - new_top)
            total = total * shrink + jnp.sum(exponent, axis=0, keepdims=True)
            acc = acc * shrink + mm(v_ref[where, :, lanes[h]], exponent.astype(BF16), TN)
            new.append((new_top, total, acc))
        return tuple(new)

    empty = (jnp.full((1, tile), NEG_FILL, F32), jnp.zeros((1, tile), F32), jnp.zeros((PAIR, tile), F32))
    done = lax.fori_loop(0, count, step, (empty,) * heads)
    for h in range(0, heads, 2):
        pair = [acc * (1.0 / total) for _, total, acc in done[h : h + 2]]
        joined = jnp.concatenate([pair[0][:HD], pair[1][HD:]], axis=0)
        o_ref[:, lanes[h]] = joined.T.astype(BF16)
    row = lax.broadcasted_iota(jnp.int32, (8, tile), 0)
    lse = jnp.zeros((8, tile), F32)
    for h, (top, total, _) in enumerate(done):
        lse = jnp.where(row == h, top + jnp.log(total), lse)
    lse_ref[...] = lse


def attention_backward_kernel(
    window_ref,
    place_ref,
    first_ref,
    q_ref,
    k_ref,
    v_ref,
    g_ref,
    o_ref,
    lse_ref,
    pos_ref,
    start_ref,
    keys_ref,
    dq_ref,
    dkv_ref,
    dk_sum,
    dv_sum,
):
    block = pl.program_id(0)
    tile, width = q_ref.shape
    heads = width // HD
    pos_row, start_row = pos_ref[0], start_ref[0]
    last = window_ref[block]
    count = last - first_ref[block] + 1
    lanes = [slice(h // 2 * PAIR, (h // 2 + 1) * PAIR) for h in range(heads)]
    scale = HD**-0.5

    @pl.when(block == 0)
    def _():
        dk_sum[...] = jnp.zeros_like(dk_sum)
        dv_sum[...] = jnp.zeros_like(dv_sum)

    queries = [half_lanes(q_ref[:, lanes[h]] * jnp.asarray(scale, BF16), h % 2) for h in range(heads)]
    grads = [half_lanes(g_ref[:, lanes[h]], h % 2) for h in range(heads)]
    inner = []
    for h in range(0, heads, 2):
        both = (g_ref[:, lanes[h]].astype(F32) * o_ref[:, lanes[h]].astype(F32)).T
        inner += [jnp.sum(part, axis=0, keepdims=True) for part in (both[:HD], both[HD:])]

    def step(i, carry):
        where = place_ref[last - i]
        allowed = allowed_tile(keys_ref, where, pos_row, start_row)
        new = []
        for h, acc in enumerate(carry):
            keys = k_ref[where, :, lanes[h]]
            scores = mm(keys, queries[h], NT)
            prob = jnp.where(allowed, jnp.exp(scores - lse_ref[h : h + 1, :]), 0.0)
            grad_prob = mm(v_ref[where, :, lanes[h]], grads[h], NT)
            grad_scores = (prob * (grad_prob - inner[h])).astype(BF16)
            dv_sum[where, :, lanes[h]] += mm(prob.astype(BF16), grads[h], NN)
            dk_sum[where, :, lanes[h]] += mm(grad_scores, queries[h], NN)
            new.append(acc + mm(keys, grad_scores, TN))
        return tuple(new)

    done = lax.fori_loop(0, count, step, (jnp.zeros((PAIR, tile), F32),) * heads)
    for h in range(0, heads, 2):
        joined = jnp.concatenate([done[h][:HD], done[h + 1][HD:]], axis=0) * scale
        dq_ref[:, lanes[h]] = joined.T.astype(BF16)

    @pl.when(block == pl.num_programs(0) - 1)
    def _():
        dkv_ref[:, :, :width] = dk_sum[...].astype(BF16)
        dkv_ref[:, :, width:] = dv_sum[...].astype(BF16)


def attention_specs(blocks, tile, width):
    by_rows = pl.BlockSpec((tile, width), lambda b, *_: (b, 0))
    keys = lambda at: pl.BlockSpec((blocks, tile, width), lambda b, *_: (0, 0, at))
    row = pl.BlockSpec((1, 1, tile), lambda b, *_: (b, 0, 0))
    lse = pl.BlockSpec((8, tile), lambda b, *_: (0, b))
    return by_rows, keys, row, lse, pl.BlockSpec((blocks, tile, 1), lambda b, *_: (0, 0, 0))


def attention_forward(tables, q, kv, pos, start, tile):
    rows, width = q.shape
    blocks = rows // tile
    by_rows, keys, row, lse, cols = attention_specs(blocks, tile, width)
    return pl.pallas_call(
        attention_forward_kernel,
        grid_spec=pltpu.PrefetchScalarGridSpec(
            num_scalar_prefetch=3,
            grid=(blocks,),
            in_specs=[by_rows, keys(0), keys(1), row, row, cols],
            out_specs=[by_rows, lse],
        ),
        out_shape=[jax.ShapeDtypeStruct((rows, width), BF16), jax.ShapeDtypeStruct((8, rows), F32)],
        compiler_params=pltpu.CompilerParams(vmem_limit_bytes=VMEM_LIMIT),
        cost_estimate=pl.CostEstimate(
            flops=2 * rows * rows * width,
            transcendentals=rows * rows * width // HD // 2,
            bytes_accessed=8 * rows * width,
        ),
        name="attention_forward",
    )(
        *tables,
        q,
        kv.reshape(blocks, tile, 2 * width),
        kv.reshape(blocks, tile, 2 * width),
        pos.reshape(blocks, 1, tile),
        start.reshape(blocks, 1, tile),
        pos.reshape(blocks, tile, 1),
    )


def attention_backward(tables, q, kv, grad, out, lse_rows, pos, start, tile):
    rows, width = q.shape
    blocks = rows // tile
    by_rows, keys, row, lse, cols = attention_specs(blocks, tile, width)
    dq, dkv = pl.pallas_call(
        attention_backward_kernel,
        grid_spec=pltpu.PrefetchScalarGridSpec(
            num_scalar_prefetch=3,
            grid=(blocks,),
            in_specs=[by_rows, keys(0), keys(1), by_rows, by_rows, lse, row, row, cols],
            out_specs=[by_rows, pl.BlockSpec((blocks, tile, 2 * width), lambda b, *_: (0, 0, 0))],
            scratch_shapes=[pltpu.VMEM((blocks, tile, width), F32)] * 2,
        ),
        out_shape=[
            jax.ShapeDtypeStruct((rows, width), BF16),
            jax.ShapeDtypeStruct((blocks, tile, 2 * width), BF16),
        ],
        compiler_params=pltpu.CompilerParams(vmem_limit_bytes=VMEM_LIMIT),
        cost_estimate=pl.CostEstimate(
            flops=5 * rows * rows * width,
            transcendentals=rows * rows * width // HD // 2,
            bytes_accessed=14 * rows * width,
        ),
        name="attention_backward",
    )(
        *tables,
        q,
        kv.reshape(blocks, tile, 2 * width),
        kv.reshape(blocks, tile, 2 * width),
        grad,
        out,
        lse_rows,
        pos.reshape(blocks, 1, tile),
        start.reshape(blocks, 1, tile),
        pos.reshape(blocks, tile, 1),
    )
    return dq, dkv.reshape(rows, 2 * width)


def whole_spec(shape):
    return pl.BlockSpec(shape, lambda i, *_: (0,) * len(shape))


def one_step(kernel, name, place, args, out_shape, flops):
    size = lambda x: x.size * x.dtype.itemsize
    return pl.pallas_call(
        kernel,
        grid_spec=pltpu.PrefetchScalarGridSpec(
            num_scalar_prefetch=1,
            grid=(1,),
            in_specs=[whole_spec(x.shape) for x in args],
            out_specs=[whole_spec(x.shape) for x in out_shape],
        ),
        out_shape=out_shape,
        compiler_params=pltpu.CompilerParams(vmem_limit_bytes=VMEM_LIMIT),
        cost_estimate=pl.CostEstimate(
            flops=flops, transcendentals=0, bytes_accessed=sum(size(x) for x in (*args, *out_shape))
        ),
        name=name,
    )(place, *args)


def norm_scale(values):
    return lax.rsqrt(jnp.mean(values * values, axis=1, keepdims=True) + EPS)


def project_kernel(place_ref, *refs, seqs, slow, fast):
    x_refs, pieces = refs[:seqs], refs[seqs:-6]
    w_ref, vec_ref, normal_ref, q_ref, kv_ref, rate_ref = refs[-6:]
    per, cols = pieces[0].shape[1:]
    span = q_ref.shape[1]
    done = 0
    for ref in pieces:
        for i in range(ref.shape[0]):
            shard = place_ref[0] ^ (done % slow * fast + done // slow)
            w_ref[pl.ds(pl.multiple_of(shard * per, per), per), :] = ref[i]
            done += 1
    tails = w_ref[:, 3 * span :]
    vec = tails.astype(F32).T
    vec_ref[...] = vec[:8]
    gain = vec[1:2]
    weight = w_ref[:, : 3 * span]
    rows = x_refs[0].shape[0]
    for k in range(seqs):
        here = slice(k * rows, (k + 1) * rows)
        x = x_refs[k][...]
        x_f = x.astype(F32)
        normal = (x_f * norm_scale(x_f) * gain).astype(BF16)
        normal_ref[here, :] = normal
        proj = mm(normal, weight, NN).astype(BF16)
        kv_ref[here, :] = proj[:, : 2 * span]
        q_ref[here, :] = proj[:, 2 * span :]
        rate_ref[here, :] = jax.nn.sigmoid(mm(x, tails, NN)[:, :1])


def project(place, x_blocks, pieces, span):
    slow, fast = fsdp_sizes()
    rows, width = x_blocks[0].shape
    total = rows * len(x_blocks)
    cols = pieces[0].shape[2]
    out_shape = [
        jax.ShapeDtypeStruct((width, cols), BF16),
        jax.ShapeDtypeStruct((8, width), F32),
        jax.ShapeDtypeStruct((total, width), BF16),
        jax.ShapeDtypeStruct((total, span), BF16),
        jax.ShapeDtypeStruct((total, 2 * span), BF16),
        jax.ShapeDtypeStruct((total, 1), F32),
    ]
    kernel = partial(project_kernel, seqs=len(x_blocks), slow=slow, fast=fast)
    return one_step(
        kernel, "project", place, [*x_blocks, *pieces], out_shape, 2 * total * width * cols
    )


def branch_kernel(place_ref, *refs, seqs):
    x_refs, g_refs, att_refs = (refs[i * seqs : (i + 1) * seqs] for i in range(3))
    w_ref, vec_ref, rate_ref, branch_ref, normal_ref, carried_ref = refs[3 * seqs :]
    rows = x_refs[0].shape[0]
    span = att_refs[0].shape[1]
    gain = vec_ref[2:3, :]
    for j in range(seqs):
        here = slice(j * rows, (j + 1) * rows)
        branch = 0.0
        for b in range(seqs):
            there = slice((j ^ b) * rows, ((j ^ b) + 1) * rows)
            branch = branch + mm(att_refs[b][there, :], w_ref[b * span : (b + 1) * span, :], NN)
        if j == 0:
            branch_ref[...] = branch
        middle = x_refs[j][...].astype(F32) + branch
        normal_ref[here, :] = (middle * norm_scale(middle) * gain).astype(BF16)
        carried_ref[here, :] = (rate_ref[here, :] * g_refs[j][...].astype(F32)).astype(BF16)


def attention_branch(place, x_blocks, g_blocks, att_blocks, w_out, vectors, rate):
    rows, width = x_blocks[0].shape
    seqs = len(x_blocks)
    out_shape = [
        jax.ShapeDtypeStruct((rows, width), F32),
        jax.ShapeDtypeStruct((rows * seqs, width), BF16),
        jax.ShapeDtypeStruct((rows * seqs, width), BF16),
    ]
    args = [*x_blocks, *g_blocks, *att_blocks, w_out, vectors, rate]
    return one_step(
        partial(branch_kernel, seqs=seqs),
        "attention_branch",
        place,
        args,
        out_shape,
        2 * rows * seqs * width * width,
    )


def attention_grad_kernel(place_ref, *refs, seqs):
    w_ref, joined_ref, out_ref = refs[seqs:]
    rows = refs[0].shape[0]
    for j in range(seqs):
        here = slice(j * rows, (j + 1) * rows)
        block = refs[j][...]
        joined_ref[here, :] = block
        out_ref[here, :] = mm(block, w_ref[...], NT).astype(BF16)


def attention_grad(place, blocks, w_out):
    rows, width = blocks[0].shape
    total = rows * len(blocks)
    span = w_out.shape[0]
    out_shape = [jax.ShapeDtypeStruct((total, width), BF16), jax.ShapeDtypeStruct((total, span), BF16)]
    return one_step(
        partial(attention_grad_kernel, seqs=len(blocks)),
        "attention_grad",
        place,
        [*blocks, w_out],
        out_shape,
        2 * total * width * span,
    )


def norm_back(values, scale, gain, grad):
    weighted = grad * gain
    inner = jnp.mean(weighted * values, axis=1, keepdims=True)
    return scale * weighted - values * (scale * scale * scale) * inner


def shards(
    inputs,
    cotangent,
    routed,
    doc_starts,
    router,
    attn_gain,
    qkv_weight,
    out_weight,
    mlp_gain,
    up_weight,
    down_weight,
):
    seqs = lax.axis_size("seq")
    fsdps = lax.axis_size("fsdp")
    me = lax.axis_index("seq")
    width = inputs.shape[2]
    tok_count = inputs.shape[1]
    own_windows = tok_count // WIN
    windows = routed.shape[1]
    tile = routed.shape[2]
    own_rows = own_windows * tile
    rows = windows * tile
    heads_width = width // seqs
    hidden = up_weight.shape[1]
    own_hidden = hidden // seqs

    order = jnp.arange(seqs, dtype=jnp.int32) ^ me
    window_of = (order[:, None] * own_windows + jnp.arange(own_windows, dtype=jnp.int32)).reshape(-1)
    stream_pos = jnp.arange(windows, dtype=jnp.int32)[:, None] * WIN + routed[0]
    pos = stream_pos[window_of].reshape(-1)
    starts = doc_starts[0]
    start = jnp.max(jnp.where(starts[None, :] <= pos[:, None], starts[None, :], 0), axis=1)
    first_window = start.reshape(windows, tile)[:, 0] // WIN
    place_of = jnp.zeros((windows,), jnp.int32).at[window_of].set(jnp.arange(windows, dtype=jnp.int32))
    tables = (window_of, place_of, first_window)

    own_routes = lax.dynamic_slice_in_dim(routed[0], me * own_windows, own_windows, 0)
    row_ids = ((jnp.arange(own_windows, dtype=jnp.int32) * WIN)[:, None] + own_routes).reshape(-1)
    stream_in = inputs[0]
    grad_in = cotangent[0]

    place = jnp.stack([lax.axis_index("fsdp"), me])
    heads = lambda i: lax.dynamic_slice_in_dim(qkv_weight, i * width + me * heads_width, heads_width, 1)
    vectors = jnp.stack([router, attn_gain, mlp_gain], axis=1)
    tails = jnp.pad(vectors, ((0, 0), (0, LANES - vectors.shape[1])))
    qkv_own = jnp.concatenate([heads(1), heads(2), heads(0), tails], axis=1)
    qkv_slow = gather_slow(qkv_own)
    x_own = pick_rows(stream_in, after(row_ids, qkv_own))
    x_blocks = gather_blocks(x_own, "seq")

    span = down_weight.shape[0] // seqs
    up_late = after(up_weight, x_own)
    up_own = jnp.concatenate(
        [
            lax.dynamic_slice_in_dim(up_late, (i * seqs + me) * span, span, 1)
            for i in range(fsdps)
        ],
        axis=1,
    )
    down_own = lax.dynamic_slice_in_dim(down_weight, me * span, span, 0)
    square = own_hidden == width
    shard_rows = up_weight.shape[0]
    if square:
        hidden_own = jnp.concatenate([up_own, down_own], axis=0)
        up_own = hidden_own
        hidden_all = lax.all_gather(after(hidden_own, *qkv_slow[1:]), "fsdp", axis=0)
        w_up = hidden_all[:, :shard_rows].reshape(width, own_hidden)
        w_down = hidden_all[:, shard_rows:].reshape(own_hidden, width)
    else:
        w_up = lax.all_gather(up_own, "fsdp", axis=0, tiled=True)
        w_down = lax.all_gather(down_own, "fsdp", axis=0, tiled=True)

    out_piece = width // (seqs * fsdps)
    out_own = lax.dynamic_slice_in_dim(out_weight, me * out_piece, out_piece, 0)
    out_slow = gather_slow(out_own, *qkv_slow[1:])
    qkv_pieces = gather_fast([qkv_slow[0], *after(tuple(qkv_slow[1:]), up_own)], False)
    out_part = jnp.stack(gather_fast(out_slow, True), axis=1).reshape(fsdps, out_piece, width)

    w_qkv, vectors, normal_a, q, kv, rate = project(place, x_blocks, qkv_pieces, heads_width)
    router_w, gain_a, gain_m = vectors[0:1], vectors[1:2], vectors[2:3]
    w_kv = w_qkv[:, : 2 * heads_width]
    w_q = w_qkv[:, 2 * heads_width :]
    tail_at = heads_width // LANES
    out_blocks = gather_blocks(after(out_part, q), "seq")
    g_own = pick_rows(grad_in, after(row_ids, q))
    g_blocks = gather_blocks(g_own, "seq")
    att_own, lse = attention_forward(tables, q, kv, pos, start, tile)
    att_blocks = gather_blocks(att_own, "seq")
    out_ordered = order_out(place, out_blocks)
    w_out = out_ordered[:heads_width]
    branch_o, normal_m, carried_b = attention_branch(
        place, x_blocks, g_blocks, att_blocks, out_ordered, vectors, rate
    )
    pre_act = mm(normal_m, w_up, NN)
    cdf = 0.5 * (1.0 + lax.erf(pre_act * (0.5**0.5)))
    activated = (pre_act * cdf).astype(BF16)
    slope = cdf + pre_act * (jnp.exp(-0.5 * pre_act * pre_act) * (2.0 * jnp.pi) ** -0.5)

    grad_act = mm(carried_b, w_down, NT)
    grad_pre = (grad_act * slope).astype(BF16)
    cut = lambda a, b: a[b * own_rows : (b + 1) * own_rows]
    normal_grads = [mm(cut(grad_pre, b), w_up, NT) for b in range(seqs)]
    grad_normal_m = scatter_blocks(normal_grads, "seq")
    flat = place * jnp.array([1, 0], jnp.int32)
    scatter = lambda g: lax.psum_scatter(g, "fsdp", scatter_dimension=0)
    activated_late = after(activated, *normal_grads)
    if square:
        both, gains = hidden_grads(
            place, activated_late, carried_b, normal_m, grad_pre, w_up, w_q, tail_at, 2
        )
        grad_normal_m = after(grad_normal_m, both)
        both = scatter(both)
        up_part, down_part = both[0].reshape(seqs, -1, own_hidden), both[1]
    else:
        (down_grad,) = weight_grad(flat, activated_late, carried_b, 1, None)
        up_grad, gains = weight_grad(
            place,
            normal_m,
            grad_pre,
            seqs,
            None,
            (w_up, w_q, tail_at, 2, jnp.zeros((width, LANES), F32)),
        )
        up_part, down_part = scatter(up_grad), scatter(down_grad)[0]

    x_o = x_blocks[0].astype(F32)
    g_o = g_blocks[0].astype(F32)
    rate_o = cut(rate, 0)
    middle_o = x_o + branch_o
    grad_middle = norm_back(middle_o, norm_scale(middle_o), gain_m, grad_normal_m)
    grad_a_own = (rate_o * g_o + grad_middle).astype(BF16)
    grad_a_blocks = gather_blocks(grad_a_own, "seq")
    branch_parts = [mm(cut(after(activated, grad_a_own), b), w_down, NN) for b in range(seqs)]
    branch_f = scatter_blocks(branch_parts, "seq")
    grad_a, grad_att = attention_grad(place, grad_a_blocks, w_out)
    fast = 1
    slow = fsdp_sizes()[1]
    out_send, out_keep = weight_grad(flat, att_own, after(grad_a, *branch_parts), 1, fast)
    dq, dkv = attention_backward(
        tables, q, kv, after(grad_att, out_send), att_own, lse, pos, start, tile
    )
    kv_send, kv_keep, gains = weight_grad(
        place, normal_a, dkv, seqs, fast, (w_kv, w_q, tail_at, 1, gains)
    )
    branch_sum = branch_o + branch_f
    result = x_o + rate_o * branch_sum
    grad_logit = jnp.sum(g_o * branch_sum, axis=1, keepdims=True) * rate_o * (1.0 - rate_o)
    logit_high = grad_logit.astype(BF16)
    logit_low = (grad_logit - logit_high.astype(F32)).astype(BF16)
    lane = jnp.arange(LANES)[None, :]
    logits = jnp.where(lane == 0, logit_high, jnp.where(lane == 3, logit_low, jnp.zeros((), BF16)))
    q_send, q_keep = weight_grad(
        place, after(normal_a, kv_send), dq, seqs, slow, (w_q, w_q, tail_at, 1, gains), (x_own, logits)
    )
    out_sum = reduce_blocks(out_send, out_keep, fast, [(q_send,)])[0]
    kv_part = reduce_blocks(kv_send, kv_keep, fast, [()])
    q_part = reduce_blocks(q_send, q_keep, slow, [()])
    dq_late, dkv_late = after((dq, dkv), q_send)
    grad_normal_a = scatter_blocks(
        [
            mm(cut(dkv_late, b), w_kv, NT) + mm(cut(dq_late, b), w_q[:, :heads_width], NT)
            for b in range(seqs)
        ],
        "seq",
    )
    output = place_rows(stream_in, row_ids, after(result.astype(BF16), q_send))
    grad_norm_x = norm_back(x_o, norm_scale(x_o), gain_a, grad_normal_a)
    grad_picked = g_o + grad_middle + grad_norm_x + grad_logit * router_w
    input_grad = place_rows(grad_in, row_ids, grad_picked.astype(BF16))
    qkv_sum, tiny = exchange_columns(
        jnp.concatenate([q_part[:, :, :heads_width], kv_part, q_part[:, :, heads_width:]], axis=2),
        3,
        heads_width,
    )
    down_sum = lax.ppermute(
        down_part,
        ("seq", "fsdp"),
        [(s * fsdps + f, f * seqs + s) for s in range(seqs) for f in range(fsdps)],
    ).astype(F32)
    up_sum = exchange_columns(up_part, fsdps, span)[0]
    return (
        output[None],
        input_grad[None],
        tiny[:, 0] + tiny[:, 3],
        tiny[:, 1],
        qkv_sum,
        out_sum,
        tiny[:, 2],
        up_sum,
        down_sum,
    )


def solution(mesh):
    return jax.shard_map(
        shards,
        mesh=mesh,
        in_specs=(
            P("fsdp", "seq", None),
            P("fsdp", "seq", None),
            P("fsdp", None, None),
            P("fsdp", None),
            P("fsdp"),
            P("fsdp"),
            P("fsdp", None),
            P("fsdp", None),
            P("fsdp"),
            P("fsdp", None),
            P("fsdp", None),
        ),
        out_specs=(
            P("fsdp", "seq", None),
            P("fsdp", "seq", None),
            P(("seq", "fsdp")),
            P(("seq", "fsdp")),
            P(("seq", "fsdp"), None),
            P(("seq", "fsdp"), None),
            P(("seq", "fsdp")),
            P(("seq", "fsdp"), None),
            P(("seq", "fsdp"), None),
        ),
        check_vma=False,
    )
```

time: 587 us -> 322 us (0.55)
  waiting for transfers between devices: 345 us -> 93.9 us
  matrix products: 62.9 us -> 24.1 us
  Pallas kernels: 39.4 us -> 71.6 us
  starting transfers between devices: 31.8 us -> 60 us
  local copies, waits for them, and re-layouts: 62 us -> 39.3 us
  other arithmetic: 19.4 us -> 11.6 us
    reduce_scatter x3 -> x1, waiting for transfers between devices: 166 us -> 0.02 us  [shards(): scatter = lambda g: lax.psum_scatter(g, 'fsdp', scatter_dimension=0)]
    all_gather x4 -> x1, waiting for transfers between devices: 88.5 us -> 0.01 us  [shards(): lax.all_gather(after(hidden_own, *qkv_slow[1:]), 'fsdp', axis=0)]
    pallas_call x0 -> x14, Pallas kernels: none -> 50.5 us  [the longest x3 15.2 us: one_step(): pl.pallas_call(kernel, grid_spec=pltpu.PrefetchScalarGridSpec(num_scalar_...]
    ppermute x18 -> x50, starting transfers between devices: 18.7 us -> 57.5 us  [flip(): return lax.ppermute(values, axis, [(j, j ^ bit) for j in range(count)])]
    dot_general x22 -> x18, matrix products: 62.9 us -> 24.1 us  [mm(): return lax.dot_general(a, b, (dims, ((), ())), preferred_element_type=F32)]
    ppermute x18 -> x50, waiting for transfers between devices: 66.3 us -> 91.7 us  [flip(): return lax.ppermute(values, axis, [(j, j ^ bit) for j in range(count)])]
    unnamed x9 -> x2, waiting for transfers between devices: 18.3 us -> 0.03 us
    unnamed x132 -> x120, local copies, waits for them, and re-layouts: 10.6 us -> 24.1 us
  transfers between devices with their start and end apart: 29 -> 53, of which waited for: 13 -> 22; matrix products, arithmetic and copies ran while one was open for 21% -> 12% of each run, Pallas kernels for 7% -> 23%
where the time goes in v2:
time: 322 us; the launch traced here: 316 us
  waiting for transfers between devices  93.9 us (29%)
  Pallas kernels  71.6 us (22%)
  starting transfers between devices  60 us (19%)
  local copies, waits for them, and re-layouts  39.3 us (12%)
  matrix products  24.1 us (7%)
  between operations  15.6 us (5%)
  other arithmetic  11.6 us (4%)
    ppermute x50, waiting for transfers between devices, flip(): return lax.ppermute(values, axis, [(j, j ^ bit) for j in range(count)])  91.7 us
    ppermute x50, starting transfers between devices, flip(): return lax.ppermute(values, axis, [(j, j ^ bit) for j in range(count)])  57.5 us
    unnamed x120, local copies, waits for them, and re-layouts  24.1 us
    dot_general x18, matrix products, mm(): return lax.dot_general(a, b, (dims, ((), ())), preferred_element_type=F32)  24.1 us
    pallas_call x3, Pallas kernels, one_step(): pl.pallas_call(kernel, grid_spec=pltpu.PrefetchScalarGridSpec(num_scalar_...  15.2 us
    pallas_call x1, Pallas kernels, attention_forward(): pl.pallas_call(attention_forward_kernel, grid_spec=pltpu.PrefetchScalarGr...  10.8 us
    pallas_call x1, Pallas kernels, hidden_grads(): pl.pallas_call(partial(hidden_grads_kernel, per=total // (seqs * fsdps),...  10.7 us
    pallas_call x1, Pallas kernels, attention_backward(): pl.pallas_call(attention_backward_kernel, grid_spec=pltpu.PrefetchScalarG...  10.3 us
  transfers between devices with their start and end apart: 53, of which 22 were waited for; matrix products, arithmetic and copies ran while one was open for 12% of the time, Pallas kernels for 23%

profile of v2, /device:TPU:1, one launch (start us, length us, event | category | flops | bytes accessed | tf_op | source)
XLA Modules:
  0.0 316.0 jit_solution(8237600718445230028)
XLA Ops:
  9.1 3.2 %collective-permute-start.4 = (bf16[128,896]{1,0:T(8,128)(2,1)S(1)}, bf16[128,896]{1,0:T(8,128)(2,1)S(1)}, u32[]{:S(2)}, u32[]{:S(2)}) collective-permute-start(bf16[128,896]{1,0:T(8,128)(2,1)S(1)} %fusion.53), channel_id=1, source_target_pairs={{0,4},{1,5},{2,6},{3,7},{4,0},{5,1},{6,2},{7,3},{8,12},{9,13},{10,... | collective-permute-start | bytes 688136 | tf_op jit(solution)/shard_map/ppermute | solution.py:33
  35.5 3.9 %collective-permute-start.17 = (bf16[32,1024]{1,0:T(8,128)(2,1)S(1)}, bf16[32,1024]{1,0:T(8,128)(2,1)S(1)}, u32[]{:S(2)}, u32[]{:S(2)}) collective-permute-start(bf16[32,1024]{1,0:T(8,128)(2,1)S(1)} %constant_dynamic-slice_fusion), channel_id=1, source_target_pairs={{0,4},{1,5},{2,6},{3,7},{4,0},{5,1},{6,2},{7,3},{8,12},{9,13},{10,... | collective-permute-start | bytes 196616 | tf_op jit(solution)/shard_map/ppermute | solution.py:33
  41.0 3.2 %collective-permute-done.17 = bf16[32,1024]{1,0:T(8,128)(2,1)S(1)} collective-permute-done((bf16[32,1024]{1,0:T(8,128)(2,1)S(1)}, bf16[32,1024]{1,0:T(8,128)(2,1)S(1)}, u32[]{:S(2)}, u32[]{:S(2)}) %collective-permute-start.17) | collective-permute-done | bytes 65568 | tf_op jit(solution)/shard_map/ppermute | solution.py:33
  50.9 6.8 %collective-permute-done.19 = bf16[4,32,1024]{2,1,0:T(8,128)(2,1)} collective-permute-done((bf16[4,32,1024]{2,1,0:T(8,128)(2,1)}, bf16[4,32,1024]{2,1,0:T(8,128)(2,1)}, u32[]{:S(2)}, u32[]{:S(2)}) %collective-permute-start.19) | collective-permute-done | bytes 262176 | tf_op jit(solution)/shard_map/ppermute | solution.py:33
  62.6 4.9 %collective-permute-done.7.refs_9_ = bf16[1,128,896]{2,1,0:T(8,128)(2,1)} collective-permute-done((bf16[1,128,896]{2,1,0:T(8,128)(2,1)S(1)}, bf16[1,128,896]{2,1,0:T(8,128)(2,1)}, u32[]{:S(2)}, u32[]{:S(2)}) %collective-permute-start.7) | collective-permute-done | bytes 229408 | tf_op jit(solution)/shard_map/ppermute | solution.py:33
  67.6 5.2 %collective-permute-done.9.refs_11_ = bf16[1,128,896]{2,1,0:T(8,128)(2,1)} collective-permute-done((bf16[1,128,896]{2,1,0:T(8,128)(2,1)}, bf16[1,128,896]{2,1,0:T(8,128)(2,1)}, u32[]{:S(2)}, u32[]{:S(2)}) %collective-permute-start.9) | collective-permute-done | bytes 229408 | tf_op jit(solution)/shard_map/ppermute | solution.py:33
  75.9 4.7 %project.1 = (bf16[1024,896]{1,0:T(8,128)(2,1)}, f32[8,1024]{1,0:T(8,128)S(1)}, bf16[1024,1024]{1,0:T(8,128)(2,1)}, bf16[1024,256]{1,0:T(8,128)(2,1)S(1)}, bf16[...) custom-call(s32[2]{0:T(128)S(1)} %get-tuple-element.111.place_ref, bf16[256,1024]{1,0:T(8,128)(2,1)S(1)} %pick_rows.2.refs_0_.refs_3_, ...), custom_call_target="tpu_custom_call" | custom-call | flops 1879048192 | bytes 9474048 | tf_op jit(solution)/shard_map/project/pallas_call | solution.py:639
  82.8 2.8 collective-permute-start.20
  87.9 2.7 pick_rows.3.refs_4_
  92.4 10.8 %attention_forward.1 = (bf16[1024,256]{1,0:T(8,128)(2,1)S(1)}, f32[8,1024]{1,0:T(8,128)S(1)}) custom-call(s32[4]{0:T(128)S(1)} %get-tuple-element.149.window_ref, s32[4]{0:T(128)S(1)} %scatter_custom_fusion.place_ref, s32[4]{0:T(128)S(1)} %get-tuple-element.148.first_ref, bf16[1024,256]{1,0:T(8,128)(2,1)S(1)} %copy-done.36, ...), custom_call_target="tpu_custom_call" | custom-call | flops 536870912 | bytes 2097152 | tf_op jit(solution)/shard_map/attention_forward/pallas_call | solution.py:567
  105.0 4.5 %collective-permute-start.13 = (bf16[1024,256]{1,0:T(8,128)(2,1)S(1)}, bf16[1024,256]{1,0:T(8,128)(2,1)S(1)}, u32[]{:S(2)}, u32[]{:S(2)}) collective-permute-start(bf16[1024,256]{1,0:T(8,128)(2,1)S(1)} %get-tuple-element.64.refs_8_.a_ref.o_ref), channel_id=1, source_target_pairs={{0,8},{8,0},{16,24},{24,16},{1,9},{9,1},{17,25},{25,17},{2,10},{10... | collective-permute-start | bytes 1572872 | tf_op jit(solution)/shard_map/ppermute | solution.py:33
  110.4 6.9 %collective-permute-done.14.refs_10_ = bf16[1024,256]{1,0:T(8,128)(2,1)S(1)} collective-permute-done((bf16[1024,256]{1,0:T(8,128)(2,1)S(1)}, bf16[1024,256]{1,0:T(8,128)(2,1)S(1)}, u32[]{:S(2)}, u32[]{:S(2)}) %collective-permute-start.14) | collective-permute-done | bytes 524320 | tf_op jit(solution)/shard_map/ppermute | solution.py:33
  125.7 7.4 %attention_branch.1 = (f32[256,1024]{1,0:T(8,128)}, bf16[1024,1024]{1,0:T(8,128)(2,1)}, bf16[1024,1024]{1,0:T(8,128)(2,1)}) custom-call(s32[2]{0:T(128)S(1)} %get-tuple-element.111.place_ref, bf16[256,1024]{1,0:T(8,128)(2,1)S(1)} %pick_rows.2.refs_0_.refs_3_, bf16[256,1024]{1,0:T(8,128)(2,1)S(1)} %copy-done.14, ...), custom_call_target="tpu_custom_call" | custom-call | flops 2147483648 | bytes 13668352 | tf_op jit(solution)/shard_map/attention_branch/pallas_call | solution.py:639
  133.1 3.0 fusion.75
  136.1 2.9 multiply_convert_fusion
  139.2 3.6 %fusion.5.pre_ref = bf16[1024,1024]{1,0:T(8,128)(2,1)S(1)} fusion(f32[1024,1024]{1,0:T(8,128)S(1)} %get-tuple-element.142, bf16[1024,1024]{1,0:T(8,128)(2,1)S(1)} %copy-done.25, bf16[1024,1024]{1,0:T(8,128)(2,1)S(1)} %bitcast.108), kind=kOutput, calls=%fused_computation.8 | convolution fusion | flops 2157969408 | bytes 10485760 | tf_op jit(solution)/shard_map/dot_general | solution.py:23
  147.5 10.7 %hidden_grads.1 = (bf16[8,2,128,1024]{3,2,1,0:T(8,128)(2,1)}, f32[1024,128]{1,0:T(8,128)S(1)}) custom-call(s32[2]{0:T(128)S(1)} %get-tuple-element.111.place_ref, bf16[1024,1024]{1,0:T(8,128)(2,1)S(1)} %get-tuple-element.76.act_ref, bf16[1024,1024]{1,0:T(8,128)(2,1)S(1)} %copy-done.25, bf16[1024,1024]{1,0:T(8,128)(2,1)} %get-tuple-element.69.norm_ref, ...), custom_call_target="tpu_custom_call" | custom-call | flops 4294967296 | bytes 12582912 | tf_op jit(solution)/shard_map/hidden_grads/pallas_call | solution.py:311
  163.8 2.6 fusion.31
  167.3 2.6 fusion.35
  176.6 7.2 %collective-permute-done.30.refs_2_ = bf16[256,1024]{1,0:T(8,128)(2,1)} collective-permute-done((bf16[256,1024]{1,0:T(8,128)(2,1)}, bf16[256,1024]{1,0:T(8,128)(2,1)}, u32[]{:S(2)}, u32[]{:S(2)}) %collective-permute-start.30) | collective-permute-done | bytes 524320 | tf_op jit(solution)/shard_map/ppermute | solution.py:33
  185.8 9.3 %collective-permute-done.28 = bf16[256,1024]{1,0:T(8,128)(2,1)S(1)} collective-permute-done((bf16[256,1024]{1,0:T(8,128)(2,1)S(1)}, bf16[256,1024]{1,0:T(8,128)(2,1)S(1)}, u32[]{:S(2)}, u32[]{:S(2)}) %collective-permute-start.28) | collective-permute-done | bytes 524320 | tf_op jit(solution)/shard_map/ppermute | solution.py:33
  197.6 3.0 attention_grad.1
  204.2 10.3 %attention_backward.1 = (bf16[1024,256]{1,0:T(8,128)(2,1)S(1)}, bf16[4,256,512]{2,1,0:T(8,128)(2,1)S(1)}) custom-call(s32[4]{0:T(128)S(1)} %get-tuple-element.149.window_ref, s32[4]{0:T(128)S(1)} %scatter_custom_fusion.place_ref, s32[4]{0:T(128)S(1)} %get-tuple-element.148.first_ref, bf16[1024,256]{1,0:T(8,128)(2,1)S(1)} %copy-done.37, ...), custom_call_target="tpu_custom_call" | custom-call | flops 1342177280 | bytes 3670016 | tf_op jit(solution)/shard_map/attention_backward/pallas_call | solution.py:598
  214.6 5.1 %weight_grad.4 = (bf16[4,4,32,512]{3,2,1,0:T(8,128)(2,1)S(1)}, bf16[4,4,32,512]{3,2,1,0:T(8,128)(2,1)S(1)}, f32[1024,128]{1,0:T(8,128)S(1)}) custom-call(s32[2]{0:T(128)S(1)} %get-tuple-element.111.place_ref, bf16[1024,1024]{1,0:T(8,128)(2,1)} %get-tuple-element.87.a_ref, bf16[1024,512]{1,0:T(8,128)(2,1)S(1)} %bitcast.89, ...), custom_call_target="tpu_custom_call" | custom-call | flops 1073741824 | bytes 4194304 | tf_op jit(solution)/shard_map/weight_grad/pallas_call | solution.py:253
  220.0 3.0 weight_grad.5
  223.0 3.8 %collective-permute-start.35 = (bf16[4,4,32,384]{3,2,1,0:T(8,128)(2,1)S(1)}, bf16[4,4,32,384]{3,2,1,0:T(8,128)(2,1)S(1)}, u32[]{:S(2)}, u32[]{:S(2)}) collective-permute-start(bf16[4,4,32,384]{3,2,1,0:T(8,128)(2,1)S(1)} %get-tuple-element.90), channel_id=1, source_target_pairs={{0,2},{1,3},{2,0},{3,1},{4,6},{5,7},{6,4},{7,5},{8,10},{9,11},{10,... | collective-permute-start | bytes 1179656 | tf_op jit(solution)/shard_map/ppermute | solution.py:33
  232.7 3.3 %place_rows.2 = bf16[2048,1024]{1,0:T(8,128)(2,1)} custom-call(s32[1,256]{1,0:T(1,128)S(1)} %fusion.90.ids_ref, bf16[256,1024]{1,0:T(8,128)(2,1)S(1)} %get-tuple-element.91.new_ref, bf16[2048,1024]{1,0:T(8,128)(2,1)S(1)} %bitcast.85), custom_call_target="tpu_custom_call" | custom-call | flops 1073741824 | bytes 8388608 | tf_op jit(solution)/shard_map/place_rows/pallas_call | solution.py:421
  248.5 16.8 %collective-permute-done.39 = bf16[2,4,32,512]{3,2,1,0:T(8,128)(2,1)S(1)} collective-permute-done((bf16[2,4,32,512]{3,2,1,0:T(8,128)(2,1)S(1)}, bf16[2,4,32,512]{3,2,1,0:T(8,128)(2,1)S(1)}, u32[]{:S(2)}, u32[]{:S(2)}) %collective-permute-start.39) | collective-permute-done | bytes 262176 | tf_op jit(solution)/shard_map/ppermute | solution.py:33
  265.5 9.6 %collective-permute-done.40 = bf16[1,4,32,512]{3,2,1,0:T(8,128)(2,1)S(1)} collective-permute-done((bf16[1,4,32,512]{3,2,1,0:T(8,128)(2,1)S(1)}, bf16[1,4,32,512]{3,2,1,0:T(8,128)(2,1)S(1)}, u32[]{:S(2)}, u32[]{:S(2)}) %collective-permute-start.40) | collective-permute-done | bytes 131104 | tf_op jit(solution)/shard_map/ppermute | solution.py:33
  275.2 2.5 collective-permute-start.43
  294.6 3.3 %place_rows.3 = bf16[2048,1024]{1,0:T(8,128)(2,1)} custom-call(s32[1,256]{1,0:T(1,128)S(1)} %fusion.90.ids_ref, bf16[256,1024]{1,0:T(8,128)(2,1)S(1)} %fusion.17.new_ref, bf16[2048,1024]{1,0:T(8,128)(2,1)S(1)} %bitcast.87), custom_call_target="tpu_custom_call" | custom-call | flops 1073741824 | bytes 8388608 | tf_op jit(solution)/shard_map/place_rows/pallas_call | solution.py:421
  297.9 7.1 %collective-permute-done.48.refs_2_ = bf16[32,1024]{1,0:T(8,128)(2,1)S(1)} collective-permute-done((bf16[32,1024]{1,0:T(8,128)(2,1)S(1)}, bf16[32,1024]{1,0:T(8,128)(2,1)S(1)}, u32[]{:S(2)}, u32[]{:S(2)}) %collective-permute-start.48) | collective-permute-done | bytes 65568 | tf_op jit(solution)/shard_map/ppermute | solution.py:33
  (305 shorter events, 123.7 us)
Async XLA Ops:
  7.2 125.9 %all-gather.3.cloned.1.call-start = ((), (), s32[]{:S(2)}) async-start(), calls=%async_computation.2 | async-start | bytes 4718592 | tf_op jit(solution)/shard_map/all_gather | solution.py:843
  9.1 17.1 %collective-permute-start.4 = (bf16[128,896]{1,0:T(8,128)(2,1)S(1)}, bf16[128,896]{1,0:T(8,128)(2,1)S(1)}, u32[]{:S(2)}, u32[]{:S(2)}) collective-permute-start(bf16[128,896]{1,0:T(8,128)(2,1)S(1)} %fusion.53), channel_id=1, source_target_pairs={{0,4},{1,5},{2,6},{3,7},{4,0},{5,1},{6,2},{7,3},{8,12},{9,13},{10,... | collective-permute-start | bytes 688136 | tf_op jit(solution)/shard_map/ppermute | solution.py:33
  13.6 14.8 %collective-permute-start.5 = (bf16[128,896]{1,0:T(8,128)(2,1)S(1)}, bf16[128,896]{1,0:T(8,128)(2,1)}, u32[]{:S(2)}, u32[]{:S(2)}) collective-permute-start(bf16[128,896]{1,0:T(8,128)(2,1)S(1)} %fusion.53), channel_id=1, source_target_pairs={{0,6},{1,7},{2,4},{3,5},{4,2},{5,3},{6,0},{7,1},{8,14},{9,15},{10,... | collective-permute-start | bytes 688136 | tf_op jit(solution)/shard_map/ppermute | solution.py:33
  28.5 257.4 %reduce-scatter.2.cloned.1.call-start = ((), (), s32[]{:S(2)}) async-start(), calls=%async_computation.1 | async-start | bytes 4718592 | tf_op jit(solution)/shard_map/reduce_scatter | solution.py:882
  28.5 18.3 %collective-permute-start.1 = (bf16[256,1024]{1,0:T(8,128)(2,1)S(1)}, bf16[256,1024]{1,0:T(8,128)(2,1)S(1)}, u32[]{:S(2)}, u32[]{:S(2)}) collective-permute-start(bf16[256,1024]{1,0:T(8,128)(2,1)S(1)} %pick_rows.2.refs_0_.refs_3_), channel_id=1, source_target_pairs={{0,16},{8,24},{16,0},{24,8},{1,17},{9,25},{17,1},{25,9},{2,18},{10... | collective-permute-start | bytes 1572872 | tf_op jit(solution)/shard_map/ppermute | solution.py:33
  29.8 43.0 %collective-permute-start = (bf16[256,1024]{1,0:T(8,128)(2,1)S(1)}, bf16[256,1024]{1,0:T(8,128)(2,1)S(1)}, u32[]{:S(2)}, u32[]{:S(2)}) collective-permute-start(bf16[256,1024]{1,0:T(8,128)(2,1)S(1)} %pick_rows.2.refs_0_.refs_3_), channel_id=1, source_target_pairs={{0,8},{8,0},{16,24},{24,16},{1,9},{9,1},{17,25},{25,17},{2,10},{10... | collective-permute-start | bytes 1572872 | tf_op jit(solution)/shard_map/ppermute | solution.py:33
  46.8 26.0 %collective-permute-start.2 = (bf16[256,1024]{1,0:T(8,128)(2,1)S(1)}, bf16[256,1024]{1,0:T(8,128)(2,1)S(1)}, u32[]{:S(2)}, u32[]{:S(2)}) collective-permute-start(bf16[256,1024]{1,0:T(8,128)(2,1)S(1)} %collective-permute-done.1.refs_2_), channel_id=1, source_target_pairs={{0,8},{8,0},{16,24},{24,16},{1,9},{9,1},{17,25},{25,17},{2,10},{10... | collective-permute-start | bytes 1572872 | tf_op jit(solution)/shard_map/ppermute | solution.py:33
  47.6 15.0 %collective-permute-start.8 = (bf16[1,128,896]{2,1,0:T(8,128)(2,1)S(1)}, bf16[1,128,896]{2,1,0:T(8,128)(2,1)}, u32[]{:S(2)}, u32[]{:S(2)}) collective-permute-start(bf16[1,128,896]{2,1,0:T(8,128)(2,1)S(1)} %bitcast.100), channel_id=1, source_target_pairs={{0,1},{1,0},{2,3},{3,2},{4,5},{5,4},{6,7},{7,6},{8,9},{9,8},{10,11... | collective-permute-start | bytes 688136 | tf_op jit(solution)/shard_map/ppermute | solution.py:33
  48.6 19.0 %collective-permute-start.7 = (bf16[1,128,896]{2,1,0:T(8,128)(2,1)S(1)}, bf16[1,128,896]{2,1,0:T(8,128)(2,1)}, u32[]{:S(2)}, u32[]{:S(2)}) collective-permute-start(bf16[1,128,896]{2,1,0:T(8,128)(2,1)S(1)} %bitcast.102), channel_id=1, source_target_pairs={{0,1},{1,0},{2,3},{3,2},{4,5},{5,4},{6,7},{7,6},{8,9},{9,8},{10,11... | collective-permute-start | bytes 688136 | tf_op jit(solution)/shard_map/ppermute | solution.py:33
  57.7 15.0 %collective-permute-start.9 = (bf16[1,128,896]{2,1,0:T(8,128)(2,1)}, bf16[1,128,896]{2,1,0:T(8,128)(2,1)}, u32[]{:S(2)}, u32[]{:S(2)}) collective-permute-start(bf16[1,128,896]{2,1,0:T(8,128)(2,1)} %bitcast.12.refs_7_), channel_id=1, source_target_pairs={{0,1},{1,0},{2,3},{3,2},{4,5},{5,4},{6,7},{7,6},{8,9},{9,8},{10,11... | collective-permute-start | bytes 688136 | tf_op jit(solution)/shard_map/ppermute | solution.py:33
  82.4 21.2 %collective-permute-start.21 = (bf16[8,32,1024]{2,1,0:T(8,128)(2,1)S(1)}, bf16[8,32,1024]{2,1,0:T(8,128)(2,1)}, u32[]{:S(2)}, u32[]{:S(2)}) collective-permute-start(bf16[8,32,1024]{2,1,0:T(8,128)(2,1)S(1)} %bitcast.94), channel_id=1, source_target_pairs={{0,16},{8,24},{16,0},{24,8},{1,17},{9,25},{17,1},{25,9},{2,18},{10... | collective-permute-start | bytes 1572872 | tf_op jit(solution)/shard_map/ppermute | solution.py:33
  82.8 26.8 %collective-permute-start.20 = (bf16[8,32,1024]{2,1,0:T(8,128)(2,1)S(1)}, bf16[8,32,1024]{2,1,0:T(8,128)(2,1)S(1)}, u32[]{:S(2)}, u32[]{:S(2)}) collective-permute-start(bf16[8,32,1024]{2,1,0:T(8,128)(2,1)S(1)} %bitcast.95), channel_id=1, source_target_pairs={{0,8},{8,0},{16,24},{24,16},{1,9},{9,1},{17,25},{25,17},{2,10},{10... | collective-permute-start | bytes 1572872 | tf_op jit(solution)/shard_map/ppermute | solution.py:33
  90.6 14.5 %collective-permute-start.11 = (bf16[256,1024]{1,0:T(8,128)(2,1)S(1)}, bf16[256,1024]{1,0:T(8,128)(2,1)S(1)}, u32[]{:S(2)}, u32[]{:S(2)}) collective-permute-start(bf16[256,1024]{1,0:T(8,128)(2,1)S(1)} %pick_rows.3.refs_4_), channel_id=1, source_target_pairs={{0,16},{8,24},{16,0},{24,8},{1,17},{9,25},{17,1},{25,9},{2,18},{10... | collective-permute-start | bytes 1572872 | tf_op jit(solution)/shard_map/ppermute | solution.py:33
  103.2 14.1 %collective-permute-start.14 = (bf16[1024,256]{1,0:T(8,128)(2,1)S(1)}, bf16[1024,256]{1,0:T(8,128)(2,1)S(1)}, u32[]{:S(2)}, u32[]{:S(2)}) collective-permute-start(bf16[1024,256]{1,0:T(8,128)(2,1)S(1)} %get-tuple-element.64.refs_8_.a_ref.o_ref), channel_id=1, source_target_pairs={{0,16},{8,24},{16,0},{24,8},{1,17},{9,25},{17,1},{25,9},{2,18},{10... | collective-permute-start | bytes 1572872 | tf_op jit(solution)/shard_map/ppermute | solution.py:33
  103.3 21.5 %collective-permute-start.10 = (bf16[256,1024]{1,0:T(8,128)(2,1)S(1)}, bf16[256,1024]{1,0:T(8,128)(2,1)S(1)}, u32[]{:S(2)}, u32[]{:S(2)}) collective-permute-start(bf16[256,1024]{1,0:T(8,128)(2,1)S(1)} %pick_rows.3.refs_4_), channel_id=1, source_target_pairs={{0,8},{8,0},{16,24},{24,16},{1,9},{9,1},{17,25},{25,17},{2,10},{10... | collective-permute-start | bytes 1572872 | tf_op jit(solution)/shard_map/ppermute | solution.py:33
  103.7 17.0 %collective-permute-start.22 = (bf16[8,32,1024]{2,1,0:T(8,128)(2,1)}, bf16[8,32,1024]{2,1,0:T(8,128)(2,1)S(1)}, u32[]{:S(2)}, u32[]{:S(2)}) collective-permute-start(bf16[8,32,1024]{2,1,0:T(8,128)(2,1)} %collective-permute-done.21.refs_2_), channel_id=1, source_target_pairs={{0,8},{8,0},{16,24},{24,16},{1,9},{9,1},{17,25},{25,17},{2,10},{10... | collective-permute-start | bytes 1572872 | tf_op jit(solution)/shard_map/ppermute | solution.py:33
  105.0 19.8 %collective-permute-start.13 = (bf16[1024,256]{1,0:T(8,128)(2,1)S(1)}, bf16[1024,256]{1,0:T(8,128)(2,1)S(1)}, u32[]{:S(2)}, u32[]{:S(2)}) collective-permute-start(bf16[1024,256]{1,0:T(8,128)(2,1)S(1)} %get-tuple-element.64.refs_8_.a_ref.o_ref), channel_id=1, source_target_pairs={{0,8},{8,0},{16,24},{24,16},{1,9},{9,1},{17,25},{25,17},{2,10},{10... | collective-permute-start | bytes 1572872 | tf_op jit(solution)/shard_map/ppermute | solution.py:33
  110.4 14.4 %collective-permute-start.12 = (bf16[256,1024]{1,0:T(8,128)(2,1)S(1)}, bf16[256,1024]{1,0:T(8,128)(2,1)S(1)}, u32[]{:S(2)}, u32[]{:S(2)}) collective-permute-start(bf16[256,1024]{1,0:T(8,128)(2,1)S(1)} %collective-permute-done.11.refs_6_), channel_id=1, source_target_pairs={{0,8},{8,0},{16,24},{24,16},{1,9},{9,1},{17,25},{25,17},{2,10},{10... | collective-permute-start | bytes 1572872 | tf_op jit(solution)/shard_map/ppermute | solution.py:33
  170.3 15.4 %collective-permute-start.26 = (bf16[256,1024]{1,0:T(8,128)(2,1)S(1)}, bf16[256,1024]{1,0:T(8,128)(2,1)S(1)}, u32[]{:S(2)}, u32[]{:S(2)}) collective-permute-start(bf16[256,1024]{1,0:T(8,128)(2,1)S(1)} %fusion.35), channel_id=1, source_target_pairs={{0,8},{8,0},{16,24},{24,16},{1,9},{9,1},{17,25},{25,17},{2,10},{10... | collective-permute-start | bytes 1572872 | tf_op jit(solution)/shard_map/ppermute | solution.py:33
  172.9 22.2 %collective-permute-start.28 = (bf16[256,1024]{1,0:T(8,128)(2,1)S(1)}, bf16[256,1024]{1,0:T(8,128)(2,1)S(1)}, u32[]{:S(2)}, u32[]{:S(2)}) collective-permute-start(bf16[256,1024]{1,0:T(8,128)(2,1)S(1)} %add_convert_fusion), channel_id=1, source_target_pairs={{0,16},{8,24},{16,0},{24,8},{1,17},{9,25},{17,1},{25,9},{2,18},{10... | collective-permute-start | bytes 1572872 | tf_op jit(solution)/shard_map/ppermute | solution.py:33
  176.1 20.3 %collective-permute-start.29 = (bf16[256,1024]{1,0:T(8,128)(2,1)}, bf16[256,1024]{1,0:T(8,128)(2,1)}, u32[]{:S(2)}, u32[]{:S(2)}) collective-permute-start(bf16[256,1024]{1,0:T(8,128)(2,1)} %fusion.13.refs_0_), channel_id=1, source_target_pairs={{0,8},{8,0},{16,24},{24,16},{1,9},{9,1},{17,25},{25,17},{2,10},{10... | collective-permute-start | bytes 1572872 | tf_op jit(solution)/shard_map/ppermute | solution.py:33
  202.0 29.2 %collective-permute-start.44 = (bf16[4,1,32,1024]{3,2,1,0:T(8,128)(2,1)S(1)}, bf16[4,1,32,1024]{3,2,1,0:T(8,128)(2,1)S(1)}, u32[]{:S(2)}, u32[]{:S(2)}) collective-permute-start(bf16[4,1,32,1024]{3,2,1,0:T(8,128)(2,1)S(1)} %get-tuple-element.81), channel_id=1, source_target_pairs={{0,1},{1,0},{2,3},{3,2},{4,5},{5,4},{6,7},{7,6},{8,9},{9,8},{10,11... | collective-permute-start | bytes 786440 | tf_op jit(solution)/shard_map/ppermute | solution.py:33
  223.0 17.1 %collective-permute-start.35 = (bf16[4,4,32,384]{3,2,1,0:T(8,128)(2,1)S(1)}, bf16[4,4,32,384]{3,2,1,0:T(8,128)(2,1)S(1)}, u32[]{:S(2)}, u32[]{:S(2)}) collective-permute-start(bf16[4,4,32,384]{3,2,1,0:T(8,128)(2,1)S(1)} %get-tuple-element.90), channel_id=1, source_target_pairs={{0,2},{1,3},{2,0},{3,1},{4,6},{5,7},{6,4},{7,5},{8,10},{9,11},{10,... | collective-permute-start | bytes 1179656 | tf_op jit(solution)/shard_map/ppermute | solution.py:33
  226.8 16.1 %collective-permute-start.38 = (bf16[4,4,32,512]{3,2,1,0:T(8,128)(2,1)S(1)}, bf16[4,4,32,512]{3,2,1,0:T(8,128)(2,1)S(1)}, u32[]{:S(2)}, u32[]{:S(2)}) collective-permute-start(bf16[4,4,32,512]{3,2,1,0:T(8,128)(2,1)S(1)} %get-tuple-element.86), channel_id=1, source_target_pairs={{0,1},{1,0},{2,3},{3,2},{4,5},{5,4},{6,7},{7,6},{8,9},{9,8},{10,11... | collective-permute-start | bytes 1572872 | tf_op jit(solution)/shard_map/ppermute | solution.py:33
  227.6 16.8 %collective-permute-start.33 = (bf16[256,1024]{1,0:T(8,128)(2,1)S(1)}, bf16[256,1024]{1,0:T(8,128)(2,1)}, u32[]{:S(2)}, u32[]{:S(2)}) collective-permute-start(bf16[256,1024]{1,0:T(8,128)(2,1)S(1)} %fusion.11), channel_id=1, source_target_pairs={{0,8},{8,0},{16,24},{24,16},{1,9},{9,1},{17,25},{25,17},{2,10},{10... | collective-permute-start | bytes 1572872 | tf_op jit(solution)/shard_map/ppermute | solution.py:33
  230.5 52.7 %collective-permute-start.32 = (bf16[256,1024]{1,0:T(8,128)(2,1)}, bf16[256,1024]{1,0:T(8,128)(2,1)}, u32[]{:S(2)}, u32[]{:S(2)}) collective-permute-start(bf16[256,1024]{1,0:T(8,128)(2,1)} %fusion.9), channel_id=1, source_target_pairs={{0,8},{8,0},{16,24},{24,16},{1,9},{9,1},{17,25},{25,17},{2,10},{10... | collective-permute-start | bytes 1572872 | tf_op jit(solution)/shard_map/ppermute | solution.py:33
  243.1 22.1 %collective-permute-start.39 = (bf16[2,4,32,512]{3,2,1,0:T(8,128)(2,1)S(1)}, bf16[2,4,32,512]{3,2,1,0:T(8,128)(2,1)S(1)}, u32[]{:S(2)}, u32[]{:S(2)}) collective-permute-start(bf16[2,4,32,512]{3,2,1,0:T(8,128)(2,1)S(1)} %slice.229), channel_id=1, source_target_pairs={{0,2},{1,3},{2,0},{3,1},{4,6},{5,7},{6,4},{7,5},{8,10},{9,11},{10,... | collective-permute-start | bytes 786440 | tf_op jit(solution)/shard_map/ppermute | solution.py:33
  245.9 37.3 %collective-permute-start.34 = (bf16[256,1024]{1,0:T(8,128)(2,1)S(1)}, bf16[256,1024]{1,0:T(8,128)(2,1)S(1)}, u32[]{:S(2)}, u32[]{:S(2)}) collective-permute-start(bf16[256,1024]{1,0:T(8,128)(2,1)S(1)} %fusion.10), channel_id=1, source_target_pairs={{0,16},{8,24},{16,0},{24,8},{1,17},{9,25},{17,1},{25,9},{2,18},{10... | collective-permute-start | bytes 1572872 | tf_op jit(solution)/shard_map/ppermute | solution.py:33
  246.4 19.0 %collective-permute-start.37 = (bf16[1,4,32,384]{3,2,1,0:T(8,128)(2,1)S(1)}, bf16[1,4,32,384]{3,2,1,0:T(8,128)(2,1)S(1)}, u32[]{:S(2)}, u32[]{:S(2)}) collective-permute-start(bf16[1,4,32,384]{3,2,1,0:T(8,128)(2,1)S(1)} %slice.363), channel_id=1, source_target_pairs={{0,4},{1,5},{2,6},{3,7},{4,0},{5,1},{6,2},{7,3},{8,12},{9,13},{10,... | collective-permute-start | bytes 294920 | tf_op jit(solution)/shard_map/ppermute | solution.py:33
  286.9 21.0 %collective-permute-start.50 = (bf16[128,1024]{1,0:T(8,128)(2,1)S(1)}, bf16[128,1024]{1,0:T(8,128)(2,1)S(1)}, u32[]{:S(2)}, u32[]{:S(2)}) collective-permute-start(bf16[128,1024]{1,0:T(8,128)(2,1)S(1)} %slice_bitcast_fusion), channel_id=1, source_target_pairs={{0,0},{1,4},{2,8},{3,12},{4,16},{5,20},{6,24},{7,28},{8,1},{9,5},{... | collective-permute-start | bytes 786440 | tf_op jit(solution)/shard_map/ppermute | solution.py:952
  290.7 14.3 %collective-permute-start.48 = (bf16[32,1024]{1,0:T(8,128)(2,1)S(1)}, bf16[32,1024]{1,0:T(8,128)(2,1)S(1)}, u32[]{:S(2)}, u32[]{:S(2)}) collective-permute-start(bf16[32,1024]{1,0:T(8,128)(2,1)S(1)} %get-tuple-element.124), channel_id=1, source_target_pairs={{0,16},{8,24},{16,0},{24,8},{1,17},{9,25},{17,1},{25,9},{2,18},{10... | collective-permute-start | bytes 196616 | tf_op jit(solution)/shard_map/ppermute | solution.py:33
  290.7 14.3 %collective-permute-start.47 = (bf16[32,1024]{1,0:T(8,128)(2,1)S(1)}, bf16[32,1024]{1,0:T(8,128)(2,1)S(1)}, u32[]{:S(2)}, u32[]{:S(2)}) collective-permute-start(bf16[32,1024]{1,0:T(8,128)(2,1)S(1)} %get-tuple-element.125), channel_id=1, source_target_pairs={{0,8},{8,0},{16,24},{24,16},{1,9},{9,1},{17,25},{25,17},{2,10},{10... | collective-permute-start | bytes 196616 | tf_op jit(solution)/shard_map/ppermute | solution.py:33
  (77 other events, 605.4 us)
Sparse Core Ops, SparseCore 0:
  28.6 83.2 all-gather.2
  167.4 103.4 reduce-scatter.1

commit v3 on v2

--- a/solution.py
+++ b/solution.py
@@ -40,20 +40,23 @@
         bit //= 2
 
 
-def gather_blocks(own, axis):
+def gather_blocks(own, axis, *waits):
     blocks = {0: own}
+    top = lax.axis_size(axis) // 2
     for bit in bits_down(lax.axis_size(axis)):
         for key in list(blocks):
-            blocks[key ^ bit] = flip(blocks[key], axis, bit)
+            block = blocks[key] if bit == top else after(blocks[key], *waits)
+            blocks[key ^ bit] = flip(block, axis, bit)
     return [blocks[key] for key in sorted(blocks)]
 
 
-def scatter_blocks(blocks, axis):
+def scatter_blocks(blocks, axis, *waits):
     parts = dict(enumerate(blocks))
     bit = 1
     while bit < lax.axis_size(axis):
         for key in [k for k in parts if k & bit]:
-            got = flip(parts.pop(key).astype(BF16), axis, bit)
+            part = parts.pop(key).astype(BF16)
+            got = flip(part if bit == 1 else after(part, *waits), axis, bit)
             parts[key ^ bit] = parts[key ^ bit] + got.astype(F32)
         bit *= 2
     return parts[0]
@@ -76,42 +79,18 @@
     return [own_late] + [flip(own_late, "fsdp", k * fast) for k in range(1, slow)]
 
 
-def gather_fast(held, joined):
+def own_fast(own):
     _, fast = fsdp_sizes()
-    held = [jnp.stack(held)] if joined else [h[None] for h in held]
-    return held + [flip(h, "fsdp", k) for k in range(1, fast) for h in held]
-
-
-def order_rows_kernel(me_ref, *refs, fast):
-    slow = refs[-1].shape[0] // fast
-    done = 0
-    for ref in refs[:-1]:
-        for i in range(ref.shape[0]):
-            block = lax.rem(done, slow) * fast + lax.div(done, slow)
-            refs[-1][me_ref[0] ^ block] = ref[i]
-            done += 1
-
-
-def order_rows(pieces):
-    slow, fast = fsdp_sizes()
-    rows, cols = pieces[0].shape[1:]
-    whole = lambda shape: pl.BlockSpec(shape, lambda i, *_: (0,) * len(shape))
-    out = pl.pallas_call(
-        partial(order_rows_kernel, fast=fast),
-        grid_spec=pltpu.PrefetchScalarGridSpec(
-            num_scalar_prefetch=1,
-            grid=(1,),
-            in_specs=[whole(p.shape) for p in pieces],
-            out_specs=whole((slow * fast, rows, cols)),
-        ),
-        out_shape=jax.ShapeDtypeStruct((slow * fast, rows, cols), BF16),
-        compiler_params=pltpu.CompilerParams(vmem_limit_bytes=VMEM_LIMIT),
-        cost_estimate=pl.CostEstimate(
-            flops=0, transcendentals=0, bytes_accessed=4 * slow * fast * rows * cols
-        ),
-        name="order_rows",
-    )(lax.axis_index("fsdp")[None], *pieces)
-    return out.reshape(-1, cols)
+    return [flip(own[None], "fsdp", k) for k in range(1, fast)]
+
+
+def gather_fast(own, others, own_got):
+    _, fast = fsdp_sizes()
+    others = jnp.stack(others)
+    pieces = [own[None], others]
+    for k in range(1, fast):
+        pieces += [own_got[k - 1], flip(others, "fsdp", k)]
+    return pieces
 
 
 def low_bits(count):
@@ -133,41 +112,52 @@
     return total[0]
 
 
-def join_columns_kernel(me_ref, *refs, groups, span):
-    count = len(refs) - (1 if span * groups == refs[0].shape[1] else 2)
+def join_columns_kernel(me_ref, *refs, up_span, span):
+    up_ref, qkv_ref, tail_ref = refs[-3:]
+    count = len(refs) - 3
+    own_hidden = up_ref.shape[1] // count
     tail = 0.0
     for k in range(count):
-        for g in range(groups):
-            start = pl.multiple_of((g * count + (me_ref[0] ^ k)) * span, span)
-            refs[count][:, pl.ds(start, span)] = refs[k][:, g * span : (g + 1) * span].astype(F32)
-        if refs[count + 1 :]:
-            tail = tail + refs[k][:, groups * span :].astype(F32)
-    for ref in refs[count + 1 :]:
-        ref[...] = tail
-
-
-def exchange_columns(blocks, groups, span):
-    count, rows, cols = blocks.shape
-    got = [blocks[0]] + [flip(blocks[k].astype(BF16), "seq", k) for k in range(1, count)]
-    if span % LANES:
+        block = refs[k][...].astype(F32)
+        at = me_ref[0] ^ k
+        for ref, first, groups, cols in ((up_ref, 0, own_hidden // up_span, up_span), (qkv_ref, own_hidden, 3, span)):
+            for g in range(groups):
+                start = pl.multiple_of((g * count + at) * cols, cols)
+                ref[:, pl.ds(start, cols)] = block[:, first + g * cols : first + (g + 1) * cols]
+        tail = tail + block[:, own_hidden + 3 * span :]
+    tail_ref[...] = tail
+
+
+def exchange_columns(up, qkv, up_span, span):
+    count, rows, own_hidden = up.shape
+    both = jnp.concatenate([up.astype(BF16), qkv.astype(BF16)], axis=2)
+    got = [both[0]] + [flip(both[k], "seq", k) for k in range(1, count)]
+    shapes = [(rows, count * own_hidden), (rows, 3 * count * span), (rows, LANES)]
+    if up_span % LANES:
         me = lax.axis_index("seq")
-        joined = jnp.zeros((rows, groups, count, span), F32)
+        groups = own_hidden // up_span
+        joined = jnp.zeros((rows, groups, count, up_span), F32)
         for k in range(count):
-            part = got[k].astype(F32).reshape(rows, groups, 1, span)
+            part = got[k][:, :own_hidden].astype(F32).reshape(rows, groups, 1, up_span)
             joined = lax.dynamic_update_slice_in_dim(joined, part, me ^ k, axis=2)
-        return (joined.reshape(rows, -1),)
-    out_shape = [jax.ShapeDtypeStruct((rows, count * groups * span), F32)]
-    if cols > groups * span:
-        out_shape.append(jax.ShapeDtypeStruct((rows, cols - groups * span), F32))
+        alone = [g[:, own_hidden:] for g in got]
+        zero = [jnp.concatenate([jnp.zeros((rows, LANES), BF16), a], axis=1) for a in alone]
+        rest = join_columns(zero, [(rows, count * LANES), *shapes[1:]], LANES, span)
+        return (joined.reshape(rows, -1), *rest[1:])
+    return join_columns(got, shapes, up_span, span)
+
+
+def join_columns(got, shapes, up_span, span):
+    whole = lambda shape: pl.BlockSpec(shape, lambda i, *_: (0, 0))
     return pl.pallas_call(
-        partial(join_columns_kernel, groups=groups, span=span),
+        partial(join_columns_kernel, up_span=up_span, span=span),
         grid_spec=pltpu.PrefetchScalarGridSpec(
             num_scalar_prefetch=1,
             grid=(1,),
-            in_specs=[pl.BlockSpec((rows, cols), lambda i, *_: (0, 0))] * count,
-            out_specs=[pl.BlockSpec(o.shape, lambda i, *_: (0, 0)) for o in out_shape],
-        ),
-        out_shape=out_shape,
+            in_specs=[whole(got[0].shape)] * len(got),
+            out_specs=[whole(shape) for shape in shapes],
+        ),
+        out_shape=[jax.ShapeDtypeStruct(shape, F32) for shape in shapes],
         compiler_params=pltpu.CompilerParams(vmem_limit_bytes=VMEM_LIMIT),
         name="join_columns",
     )(lax.axis_index("seq")[None], *got)
@@ -223,9 +213,9 @@
     store_blocks(product, tail, column, place_ref, per, fsdps, first, refs)
 
 
-def weight_grad(place, a, b, parts, first, gain=None, logits=None):
+def weight_grad(place, a, b, parts, first, gain=None, logits=None, cols=None, at_b=0):
     rows, total = a.shape
-    cols = b.shape[1]
+    cols = cols or b.shape[1]
     fsdps = lax.axis_size("fsdp")
     per = total // (parts * fsdps)
     tile = min(GRAD_TILE, total)
@@ -233,16 +223,16 @@
     columns = lambda n: pl.BlockSpec((n, tile), lambda c, *_: (0, c))
     lines = lambda n, at=0: pl.BlockSpec((tile, n), lambda c, *_: (c, at))
     whole = lambda *dims: pl.BlockSpec(dims, lambda c, *_: (0,) * len(dims))
-    args, in_specs = [a, b], [columns(rows), whole(rows, cols)]
+    args, in_specs = [a, b], [columns(rows), pl.BlockSpec((rows, cols), lambda c, *_: (0, at_b))]
     copies = 1 if first is None else 2
     block = (fsdps // copies, parts, per, wide)
     out_shape = [jax.ShapeDtypeStruct(block, BF16)] * copies
     out_specs = [whole(*block)] * copies
     lane = None
     if gain is not None:
-        weight, vectors, at, lane, other = gain
+        weight, weight_at, vectors, at, lane, other = gain
         args += [weight, vectors, other]
-        in_specs += [lines(cols), lines(LANES, at), lines(LANES)]
+        in_specs += [lines(cols, weight_at), lines(LANES, at), lines(LANES)]
     tail_out = gain is not None and logits is None
     if tail_out:
         out_shape = out_shape + [jax.ShapeDtypeStruct((total, LANES), F32)]
@@ -463,16 +453,18 @@
     def step(i, carry):
         where = place_ref[last - i]
         allowed = allowed_tile(keys_ref, where, pos_row, start_row)
-        new = []
-        for h, (top, total, acc) in enumerate(carry):
-            scores = jnp.where(allowed, mm(k_ref[where, :, lanes[h]], queries[h], NT), NEG_FILL)
-            new_top = jnp.maximum(top, jnp.max(scores, axis=0, keepdims=True))
-            shrink = jnp.exp(top - new_top)
-            exponent = jnp.exp(scores - new_top)
-            total = total * shrink + jnp.sum(exponent, axis=0, keepdims=True)
-            acc = acc * shrink + mm(v_ref[where, :, lanes[h]], exponent.astype(BF16), TN)
-            new.append((new_top, total, acc))
-        return tuple(new)
+        each = range(heads)
+        raw = [mm(k_ref[where, :, lanes[h]], queries[h], NT) for h in each]
+        scores = [jnp.where(allowed, raw[h], NEG_FILL) for h in each]
+        tops = [jnp.maximum(carry[h][0], jnp.max(scores[h], axis=0, keepdims=True)) for h in each]
+        exponents = [jnp.exp(scores[h] - tops[h]) for h in each]
+        values = [mm(v_ref[where, :, lanes[h]], exponents[h].astype(BF16), TN) for h in each]
+        shrinks = [jnp.exp(carry[h][0] - tops[h]) for h in each]
+        sums = [jnp.sum(exponents[h], axis=0, keepdims=True) for h in each]
+        return tuple(
+            (tops[h], carry[h][1] * shrinks[h] + sums[h], carry[h][2] * shrinks[h] + values[h])
+            for h in each
+        )
 
     empty = (jnp.full((1, tile), NEG_FILL, F32), jnp.zeros((1, tile), F32), jnp.zeros((PAIR, tile), F32))
     done = lax.fori_loop(0, count, step, (empty,) * heads)
@@ -500,8 +492,7 @@
     pos_ref,
     start_ref,
     keys_ref,
-    dq_ref,
-    dkv_ref,
+    grad_ref,
     dk_sum,
     dv_sum,
 ):
@@ -529,27 +520,29 @@
     def step(i, carry):
         where = place_ref[last - i]
         allowed = allowed_tile(keys_ref, where, pos_row, start_row)
-        new = []
-        for h, acc in enumerate(carry):
-            keys = k_ref[where, :, lanes[h]]
-            scores = mm(keys, queries[h], NT)
-            prob = jnp.where(allowed, jnp.exp(scores - lse_ref[h : h + 1, :]), 0.0)
-            grad_prob = mm(v_ref[where, :, lanes[h]], grads[h], NT)
-            grad_scores = (prob * (grad_prob - inner[h])).astype(BF16)
-            dv_sum[where, :, lanes[h]] += mm(prob.astype(BF16), grads[h], NN)
-            dk_sum[where, :, lanes[h]] += mm(grad_scores, queries[h], NN)
-            new.append(acc + mm(keys, grad_scores, TN))
-        return tuple(new)
+        each = range(heads)
+        keys = [k_ref[where, :, lanes[h]] for h in each]
+        scores = [mm(keys[h], queries[h], NT) for h in each]
+        grad_prob = [mm(v_ref[where, :, lanes[h]], grads[h], NT) for h in each]
+        prob = [jnp.where(allowed, jnp.exp(scores[h] - lse_ref[h : h + 1, :]), 0.0) for h in each]
+        grad_scores = [(prob[h] * (grad_prob[h] - inner[h])).astype(BF16) for h in each]
+        values = [mm(prob[h].astype(BF16), grads[h], NN) for h in each]
+        moved = [mm(grad_scores[h], queries[h], NN) for h in each]
+        for h in range(0, heads, 2):
+            dv_sum[where, :, lanes[h]] += values[h] + values[h + 1]
+            dk_sum[where, :, lanes[h]] += moved[h] + moved[h + 1]
+        return tuple(carry[h] + mm(keys[h], grad_scores[h], TN) for h in each)
 
     done = lax.fori_loop(0, count, step, (jnp.zeros((PAIR, tile), F32),) * heads)
     for h in range(0, heads, 2):
         joined = jnp.concatenate([done[h][:HD], done[h + 1][HD:]], axis=0) * scale
-        dq_ref[:, lanes[h]] = joined.T.astype(BF16)
+        at = 2 * width + h * HD
+        grad_ref[block, :, at : at + PAIR] = joined.T.astype(BF16)
 
     @pl.when(block == pl.num_programs(0) - 1)
     def _():
-        dkv_ref[:, :, :width] = dk_sum[...].astype(BF16)
-        dkv_ref[:, :, width:] = dv_sum[...].astype(BF16)
+        grad_ref[:, :, :width] = dk_sum[...].astype(BF16)
+        grad_ref[:, :, width : 2 * width] = dv_sum[...].astype(BF16)
 
 
 def attention_specs(blocks, tile, width):
@@ -595,19 +588,16 @@
     rows, width = q.shape
     blocks = rows // tile
     by_rows, keys, row, lse, cols = attention_specs(blocks, tile, width)
-    dq, dkv = pl.pallas_call(
+    grads = pl.pallas_call(
         attention_backward_kernel,
         grid_spec=pltpu.PrefetchScalarGridSpec(
             num_scalar_prefetch=3,
             grid=(blocks,),
             in_specs=[by_rows, keys(0), keys(1), by_rows, by_rows, lse, row, row, cols],
-            out_specs=[by_rows, pl.BlockSpec((blocks, tile, 2 * width), lambda b, *_: (0, 0, 0))],
+            out_specs=pl.BlockSpec((blocks, tile, 3 * width), lambda b, *_: (0, 0, 0)),
             scratch_shapes=[pltpu.VMEM((blocks, tile, width), F32)] * 2,
         ),
-        out_shape=[
-            jax.ShapeDtypeStruct((rows, width), BF16),
-            jax.ShapeDtypeStruct((blocks, tile, 2 * width), BF16),
-        ],
+        out_shape=jax.ShapeDtypeStruct((blocks, tile, 3 * width), BF16),
         compiler_params=pltpu.CompilerParams(vmem_limit_bytes=VMEM_LIMIT),
         cost_estimate=pl.CostEstimate(
             flops=5 * rows * rows * width,
@@ -627,7 +617,7 @@
         start.reshape(blocks, 1, tile),
         pos.reshape(blocks, tile, 1),
     )
-    return dq, dkv.reshape(rows, 2 * width)
+    return grads.reshape(rows, 3 * width)
 
 
 def whole_spec(shape):
@@ -657,16 +647,84 @@
     return lax.rsqrt(jnp.mean(values * values, axis=1, keepdims=True) + EPS)
 
 
+def first_shard_kernel(place_ref, q_ref, k_ref, v_ref, tails_ref, out_ref, own_ref):
+    span = q_ref.shape[1]
+    for i, ref in enumerate((k_ref, v_ref, q_ref)):
+        own_ref[:, i * span : (i + 1) * span] = ref[...]
+    own_ref[:, 3 * span : 3 * span + LANES] = tails_ref[...]
+    lines = out_ref.shape[1]
+    for j in range(out_ref.shape[2] // span):
+        own_ref[j * lines : (j + 1) * lines, 3 * span + LANES :] = out_ref[0, :, j * span : (j + 1) * span]
+
+
+def first_shard(place, qkv, tails, out, span):
+    rows, width = out.shape
+    seqs = width // span
+    out = out.reshape(seqs, rows // seqs, width)
+    heads = lambda i: pl.BlockSpec((rows, span), lambda g, at: (0, i * seqs + at[1]))
+    cols = 4 * span + LANES
+    return pl.pallas_call(
+        first_shard_kernel,
+        grid_spec=pltpu.PrefetchScalarGridSpec(
+            num_scalar_prefetch=1,
+            grid=(1,),
+            in_specs=[
+                heads(0),
+                heads(1),
+                heads(2),
+                pl.BlockSpec((rows, LANES), lambda g, at: (0, 0)),
+                pl.BlockSpec((1, rows // seqs, width), lambda g, at: (at[1], 0, 0)),
+            ],
+            out_specs=pl.BlockSpec((rows, cols), lambda g, at: (0, 0)),
+        ),
+        out_shape=jax.ShapeDtypeStruct((rows, cols), BF16),
+        compiler_params=pltpu.CompilerParams(vmem_limit_bytes=VMEM_LIMIT),
+        cost_estimate=pl.CostEstimate(flops=0, transcendentals=0, bytes_accessed=4 * rows * cols),
+        name="first_shard",
+    )(place, qkv, qkv, qkv, tails, out)
+
+
+def hidden_shard_kernel(place_ref, up_ref, down_ref, both_ref):
+    rows = up_ref.shape[0]
+    both_ref[:rows, :] = up_ref[...]
+    both_ref[rows:, :] = down_ref[...]
+
+
+def hidden_shard(place, up, down, span):
+    rows, width = up.shape[0], down.shape[1]
+    seqs = lax.axis_size("seq")
+    return pl.pallas_call(
+        hidden_shard_kernel,
+        grid_spec=pltpu.PrefetchScalarGridSpec(
+            num_scalar_prefetch=1,
+            grid=(width // span,),
+            in_specs=[
+                pl.BlockSpec((rows, span), lambda i, at: (0, i * seqs + at[1])),
+                pl.BlockSpec((span, span), lambda i, at: (at[1], i)),
+            ],
+            out_specs=pl.BlockSpec((rows + span, span), lambda i, at: (0, i)),
+        ),
+        out_shape=jax.ShapeDtypeStruct((rows + span, width), BF16),
+        compiler_params=pltpu.CompilerParams(vmem_limit_bytes=VMEM_LIMIT),
+        cost_estimate=pl.CostEstimate(flops=0, transcendentals=0, bytes_accessed=8 * rows * width),
+        name="hidden_shard",
+    )(place, up, down)
+
+
 def project_kernel(place_ref, *refs, seqs, slow, fast):
-    x_refs, pieces = refs[:seqs], refs[seqs:-6]
-    w_ref, vec_ref, normal_ref, q_ref, kv_ref, rate_ref = refs[-6:]
-    per, cols = pieces[0].shape[1:]
+    x_refs, pieces = refs[:seqs], refs[seqs:-7]
+    out_ref, w_ref, vec_ref, normal_ref, q_ref, kv_ref, rate_ref = refs[-7:]
+    per, cols = pieces[0].shape[1], w_ref.shape[1]
     span = q_ref.shape[1]
+    lines = out_ref.shape[1]
     done = 0
     for ref in pieces:
         for i in range(ref.shape[0]):
-            shard = place_ref[0] ^ (done % slow * fast + done // slow)
-            w_ref[pl.ds(pl.multiple_of(shard * per, per), per), :] = ref[i]
+            block = done % slow * fast + done // slow
+            shard = place_ref[0] ^ block
+            w_ref[pl.ds(pl.multiple_of(shard * per, per), per), :] = ref[i, :, :cols]
+            for j in range(seqs):
+                out_ref[block, :, j * span : (j + 1) * span] = ref[i, j * lines : (j + 1) * lines, cols:]
             done += 1
     tails = w_ref[:, 3 * span :]
     vec = tails.astype(F32).T
@@ -690,8 +748,9 @@
     slow, fast = fsdp_sizes()
     rows, width = x_blocks[0].shape
     total = rows * len(x_blocks)
-    cols = pieces[0].shape[2]
+    cols = pieces[0].shape[2] - span
     out_shape = [
+        jax.ShapeDtypeStruct((slow * fast, width // (slow * fast * len(x_blocks)), width), BF16),
         jax.ShapeDtypeStruct((width, cols), BF16),
         jax.ShapeDtypeStruct((8, width), F32),
         jax.ShapeDtypeStruct((total, width), BF16),
@@ -817,53 +876,42 @@
     grad_in = cotangent[0]
 
     place = jnp.stack([lax.axis_index("fsdp"), me])
-    heads = lambda i: lax.dynamic_slice_in_dim(qkv_weight, i * width + me * heads_width, heads_width, 1)
     vectors = jnp.stack([router, attn_gain, mlp_gain], axis=1)
     tails = jnp.pad(vectors, ((0, 0), (0, LANES - vectors.shape[1])))
-    qkv_own = jnp.concatenate([heads(1), heads(2), heads(0), tails], axis=1)
-    qkv_slow = gather_slow(qkv_own)
-    x_own = pick_rows(stream_in, after(row_ids, qkv_own))
+    first_own = first_shard(place, qkv_weight, tails, out_weight, heads_width)
+    first_slow = gather_slow(first_own)
+    first_got = own_fast(first_slow[0])
+    x_own = pick_rows(stream_in, after(row_ids, first_own))
     x_blocks = gather_blocks(x_own, "seq")
 
     span = down_weight.shape[0] // seqs
-    up_late = after(up_weight, x_own)
-    up_own = jnp.concatenate(
-        [
-            lax.dynamic_slice_in_dim(up_late, (i * seqs + me) * span, span, 1)
-            for i in range(fsdps)
-        ],
-        axis=1,
-    )
-    down_own = lax.dynamic_slice_in_dim(down_weight, me * span, span, 0)
-    square = own_hidden == width
+    square = own_hidden == width and span % LANES == 0
     shard_rows = up_weight.shape[0]
     if square:
-        hidden_own = jnp.concatenate([up_own, down_own], axis=0)
-        up_own = hidden_own
-        hidden_all = lax.all_gather(after(hidden_own, *qkv_slow[1:]), "fsdp", axis=0)
+        hidden_own = hidden_shard(place, after(up_weight, x_own, *first_got), down_weight, span)
+        hidden_late = after(hidden_own, *first_slow[1:])
+        hidden_all = lax.all_gather(hidden_late, "fsdp", axis=0)
         w_up = hidden_all[:, :shard_rows].reshape(width, own_hidden)
         w_down = hidden_all[:, shard_rows:].reshape(own_hidden, width)
     else:
-        w_up = lax.all_gather(up_own, "fsdp", axis=0, tiled=True)
+        hidden_own = lax.dynamic_index_in_dim(
+            up_weight.reshape(-1, fsdps, seqs, span), me, axis=2, keepdims=False
+        ).reshape(-1, own_hidden)
+        down_own = lax.dynamic_slice_in_dim(down_weight, me * span, span, 0)
+        w_up = lax.all_gather(hidden_own, "fsdp", axis=0, tiled=True)
         w_down = lax.all_gather(down_own, "fsdp", axis=0, tiled=True)
-
-    out_piece = width // (seqs * fsdps)
-    out_own = lax.dynamic_slice_in_dim(out_weight, me * out_piece, out_piece, 0)
-    out_slow = gather_slow(out_own, *qkv_slow[1:])
-    qkv_pieces = gather_fast([qkv_slow[0], *after(tuple(qkv_slow[1:]), up_own)], False)
-    out_part = jnp.stack(gather_fast(out_slow, True), axis=1).reshape(fsdps, out_piece, width)
-
-    w_qkv, vectors, normal_a, q, kv, rate = project(place, x_blocks, qkv_pieces, heads_width)
+    first_pieces = gather_fast(first_slow[0], after(tuple(first_slow[1:]), hidden_own), first_got)
+    g_own = pick_rows(grad_in, after(row_ids, x_blocks[seqs // 2]))
+    g_blocks = gather_blocks(g_own, "seq")
+    out_part, w_qkv, vectors, normal_a, q, kv, rate = project(
+        place, x_blocks, first_pieces, heads_width
+    )
     router_w, gain_a, gain_m = vectors[0:1], vectors[1:2], vectors[2:3]
-    w_kv = w_qkv[:, : 2 * heads_width]
-    w_q = w_qkv[:, 2 * heads_width :]
-    tail_at = heads_width // LANES
-    out_blocks = gather_blocks(after(out_part, q), "seq")
-    g_own = pick_rows(grad_in, after(row_ids, q))
-    g_blocks = gather_blocks(g_own, "seq")
+    tail_at = 3 * heads_width // LANES
     att_own, lse = attention_forward(tables, q, kv, pos, start, tile)
-    att_blocks = gather_blocks(att_own, "seq")
+    out_blocks = gather_blocks(out_part, "seq", att_own)
     out_ordered = order_out(place, out_blocks)
+    att_blocks = gather_blocks(att_own, "seq", out_ordered)
     w_out = out_ordered[:heads_width]
     branch_o, normal_m, carried_b = attention_branch(
         place, x_blocks, g_blocks, att_blocks, out_ordered, vectors, rate
@@ -883,7 +931,7 @@
     activated_late = after(activated, *normal_grads)
     if square:
         both, gains = hidden_grads(
-            place, activated_late, carried_b, normal_m, grad_pre, w_up, w_q, tail_at, 2
+            place, activated_late, carried_b, normal_m, grad_pre, w_up, w_qkv, tail_at, 2
         )
         grad_normal_m = after(grad_normal_m, both)
         both = scatter(both)
@@ -896,7 +944,7 @@
             grad_pre,
             seqs,
             None,
-            (w_up, w_q, tail_at, 2, jnp.zeros((width, LANES), F32)),
+            (w_up, 0, w_qkv, tail_at, 2, jnp.zeros((width, LANES), F32)),
         )
         up_part, down_part = scatter(up_grad), scatter(down_grad)[0]
 
@@ -907,17 +955,23 @@
     grad_middle = norm_back(middle_o, norm_scale(middle_o), gain_m, grad_normal_m)
     grad_a_own = (rate_o * g_o + grad_middle).astype(BF16)
     grad_a_blocks = gather_blocks(grad_a_own, "seq")
-    branch_parts = [mm(cut(after(activated, grad_a_own), b), w_down, NN) for b in range(seqs)]
-    branch_f = scatter_blocks(branch_parts, "seq")
+    branch_parts = [mm(cut(after(activated, grad_a_blocks[1]), b), w_down, NN) for b in range(seqs)]
+    branch_f = scatter_blocks(branch_parts, "seq", grad_a_blocks[-1])
     grad_a, grad_att = attention_grad(place, grad_a_blocks, w_out)
     fast = 1
     slow = fsdp_sizes()[1]
     out_send, out_keep = weight_grad(flat, att_own, after(grad_a, *branch_parts), 1, fast)
-    dq, dkv = attention_backward(
+    grad_proj = attention_backward(
         tables, q, kv, after(grad_att, out_send), att_own, lse, pos, start, tile
     )
     kv_send, kv_keep, gains = weight_grad(
-        place, normal_a, dkv, seqs, fast, (w_kv, w_q, tail_at, 1, gains)
+        place,
+        normal_a,
+        grad_proj,
+        seqs,
+        fast,
+        (w_qkv, 0, w_qkv, tail_at, 1, gains),
+        cols=2 * heads_width,
     )
     branch_sum = branch_o + branch_f
     result = x_o + rate_o * branch_sum
@@ -927,34 +981,35 @@
     lane = jnp.arange(LANES)[None, :]
     logits = jnp.where(lane == 0, logit_high, jnp.where(lane == 3, logit_low, jnp.zeros((), BF16)))
     q_send, q_keep = weight_grad(
-        place, after(normal_a, kv_send), dq, seqs, slow, (w_q, w_q, tail_at, 1, gains), (x_own, logits)
+        place,
+        after(normal_a, kv_send),
+        grad_proj,
+        seqs,
+        slow,
+        (w_qkv, 2, w_qkv, tail_at, 1, gains),
+        (x_own, logits),
+        cols=heads_width,
+        at_b=2,
     )
     out_sum = reduce_blocks(out_send, out_keep, fast, [(q_send,)])[0]
     kv_part = reduce_blocks(kv_send, kv_keep, fast, [()])
     q_part = reduce_blocks(q_send, q_keep, slow, [()])
-    dq_late, dkv_late = after((dq, dkv), q_send)
-    grad_normal_a = scatter_blocks(
-        [
-            mm(cut(dkv_late, b), w_kv, NT) + mm(cut(dq_late, b), w_q[:, :heads_width], NT)
-            for b in range(seqs)
-        ],
-        "seq",
-    )
+    proj_late = after(grad_proj, q_send)
+    w_proj = w_qkv[:, : 3 * heads_width]
+    grad_normal_a = scatter_blocks([mm(cut(proj_late, b), w_proj, NT) for b in range(seqs)], "seq")
     output = place_rows(stream_in, row_ids, after(result.astype(BF16), q_send))
     grad_norm_x = norm_back(x_o, norm_scale(x_o), gain_a, grad_normal_a)
     grad_picked = g_o + grad_middle + grad_norm_x + grad_logit * router_w
     input_grad = place_rows(grad_in, row_ids, grad_picked.astype(BF16))
-    qkv_sum, tiny = exchange_columns(
-        jnp.concatenate([q_part[:, :, :heads_width], kv_part, q_part[:, :, heads_width:]], axis=2),
-        3,
-        heads_width,
-    )
     down_sum = lax.ppermute(
         down_part,
         ("seq", "fsdp"),
         [(s * fsdps + f, f * seqs + s) for s in range(seqs) for f in range(fsdps)],
     ).astype(F32)
-    up_sum = exchange_columns(up_part, fsdps, span)[0]
+    qkv_part = jnp.concatenate(
+        [q_part[:, :, :heads_width], kv_part, q_part[:, :, heads_width:]], axis=2
+    )
+    up_sum, qkv_sum, tiny = exchange_columns(up_part, qkv_part, span, heads_width)
     return (
         output[None],
         input_grad[None],

time: 322 us -> 289 us (0.90); the launches traced: 316 us -> 288 us
  starting transfers between devices: 60 us -> 46.8 us
  local copies, waits for them, and re-layouts: 39.3 us -> 27 us
  other arithmetic: 11.6 us -> 18 us
  matrix products: 24.1 us -> 19.3 us
    ppermute x50 -> x41, starting transfers between devices: 57.5 us -> 43.5 us  [flip(): return lax.ppermute(values, axis, [(j, j ^ bit) for j in range(count)])]
    unnamed x120 -> x123, local copies, waits for them, and re-layouts: 24.1 us -> 15.9 us
    dot_general x18 -> x14, matrix products: 24.1 us -> 19.3 us  [mm(): return lax.dot_general(a, b, (dims, ((), ())), preferred_element_type=F32)]
    pallas_call x1, Pallas kernels: 10.8 us -> 6.33 us  [attention_forward(): pl.pallas_call(attention_forward_kernel, grid_spec=pltpu.PrefetchScalarGr...]
    ppermute x50 -> x41, waiting for transfers between devices: 91.7 us -> 87.4 us  [flip(): return lax.ppermute(values, axis, [(j, j ^ bit) for j in range(count)])]
    reduce_scatter x1, waiting for transfers between devices: 0.02 us -> 3.29 us  [shards(): scatter = lambda g: lax.psum_scatter(g, 'fsdp', scatter_dimension=0)]
    pallas_call x2 -> x3, Pallas kernels: 1.63 us -> 4.86 us  [the longest x1 3.27 us: hidden_shard(): pl.pallas_call(hidden_shard_kernel, grid_spec=pltpu.PrefetchScalarGridSpe...]
  transfers between devices with their start and end apart: 53 -> 44, of which waited for: 22 -> 17; matrix products, arithmetic and copies ran while one was open for 12% -> 12% of each run, Pallas kernels for 23% -> 24%
where the time goes in v3:
time: 289 us; the launch traced here: 288 us
  waiting for transfers between devices  90.7 us (31%)
  Pallas kernels  70.7 us (24%)
  starting transfers between devices  46.8 us (16%)
  local copies, waits for them, and re-layouts  27 us (9%)
  matrix products  19.3 us (7%)
  other arithmetic  18 us (6%)
  between operations  15 us (5%)
    ppermute x41, waiting for transfers between devices, flip(): return lax.ppermute(values, axis, [(j, j ^ bit) for j in range(count)])  87.4 us
    ppermute x41, starting transfers between devices, flip(): return lax.ppermute(values, axis, [(j, j ^ bit) for j in range(count)])  43.5 us
    dot_general x14, matrix products, mm(): return lax.dot_general(a, b, (dims, ((), ())), preferred_element_type=F32)  19.3 us
    unnamed x123, local copies, waits for them, and re-layouts  15.9 us
    pallas_call x3, Pallas kernels, one_step(): pl.pallas_call(kernel, grid_spec=pltpu.PrefetchScalarGridSpec(num_scalar_...  15.2 us
    pallas_call x1, Pallas kernels, hidden_grads(): pl.pallas_call(partial(hidden_grads_kernel, per=total // (seqs * fsdps),...  11.3 us
    pallas_call x3, Pallas kernels, weight_grad(): pl.pallas_call(partial(weight_grad_kernel, per=per, fsdps=fsdps, first=fi...  11 us
    pallas_call x1, Pallas kernels, attention_backward(): pl.pallas_call(attention_backward_kernel, grid_spec=pltpu.PrefetchScalarG...  8.47 us
  transfers between devices with their start and end apart: 44, of which 17 were waited for; matrix products, arithmetic and copies ran while one was open for 12% of the time, Pallas kernels for 24%

profile of v3, /device:TPU:1, one launch (start us, length us, event | category | flops | bytes accessed | tf_op | source)
XLA Modules:
  0.0 287.5 jit_solution(5836149921023165194)
XLA Ops:
  13.6 3.3 %collective-permute-start.5 = (bf16[128,1152]{1,0:T(8,128)(2,1)S(1)}, bf16[128,1152]{1,0:T(8,128)(2,1)S(1)}, u32[]{:S(2)}, u32[]{:S(2)}) collective-permute-start(bf16[128,1152]{1,0:T(8,128)(2,1)S(1)} %first_shard.1), channel_id=1, source_target_pairs={{0,6},{1,7},{2,4},{3,5},{4,2},{5,3},{6,0},{7,1},{8,14},{9,15},{10,... | collective-permute-start | bytes 884744 | tf_op jit(solution)/shard_map/ppermute | solution.py:33
  19.6 2.5 pick_rows.2.refs_0_.refs_3_
  22.8 3.3 %hidden_shard.1 = bf16[256,1024]{1,0:T(8,128)(2,1)} custom-call(s32[2]{0:T(128)S(1)} %get-tuple-element.115.place_ref, bf16[128,4096]{1,0:T(8,128)(2,1)S(1)} %copy-done.15, bf16[512,1024]{1,0:T(8,128)(2,1)S(1)} %copy-done.16), custom_call_target="tpu_custom_call" | custom-call | bytes 1048576 | tf_op jit(solution)/shard_map/hidden_shard/pallas_call | solution.py:696
  26.1 15.5 %collective-permute-done.4 = bf16[128,1152]{1,0:T(8,128)(2,1)S(1)} collective-permute-done((bf16[128,1152]{1,0:T(8,128)(2,1)S(1)}, bf16[128,1152]{1,0:T(8,128)(2,1)S(1)}, u32[]{:S(2)}, u32[]{:S(2)}) %collective-permute-start.4) | collective-permute-done | bytes 294944 | tf_op jit(solution)/shard_map/ppermute | solution.py:33
  46.4 7.5 %collective-permute-done.1.refs_2_ = bf16[256,1024]{1,0:T(8,128)(2,1)S(1)} collective-permute-done((bf16[256,1024]{1,0:T(8,128)(2,1)S(1)}, bf16[256,1024]{1,0:T(8,128)(2,1)S(1)}, u32[]{:S(2)}, u32[]{:S(2)}) %collective-permute-start.1) | collective-permute-done | bytes 524320 | tf_op jit(solution)/shard_map/ppermute | solution.py:33
  57.7 11.8 %collective-permute-done.7.refs_7_ = bf16[3,128,1152]{2,1,0:T(8,128)(2,1)} collective-permute-done((bf16[3,128,1152]{2,1,0:T(8,128)(2,1)S(1)}, bf16[3,128,1152]{2,1,0:T(8,128)(2,1)}, u32[]{:S(2)}, u32[]{:S(2)}) %collective-permute-start.7) | collective-permute-done | bytes 884768 | tf_op jit(solution)/shard_map/ppermute | solution.py:33
  70.4 6.4 %project.1 = (bf16[8,32,1024]{2,1,0:T(8,128)(2,1)}, bf16[1024,896]{1,0:T(8,128)(2,1)}, f32[8,1024]{1,0:T(8,128)S(1)}, bf16[1024,1024]{1,0:T(8,128)(2,1)}, bf16[1...) custom-call(s32[2]{0:T(128)S(1)} %get-tuple-element.115.place_ref, ...), custom_call_target="tpu_custom_call" | custom-call | flops 1879048192 | bytes 10522624 | tf_op jit(solution)/shard_map/project/pallas_call | solution.py:629
  82.9 2.5 pick_rows.3.refs_4_
  86.0 6.3 %attention_forward.1 = (bf16[1024,256]{1,0:T(8,128)(2,1)S(1)}, f32[8,1024]{1,0:T(8,128)S(1)}) custom-call(s32[4]{0:T(128)S(1)} %get-tuple-element.145.window_ref, s32[4]{0:T(128)S(1)} %scatter_custom_fusion.place_ref, s32[4]{0:T(128)S(1)} %get-tuple-element.144.first_ref, bf16[1024,256]{1,0:T(8,128)(2,1)S(1)} %copy-done.20, ...), custom_call_target="tpu_custom_call" | custom-call | flops 536870912 | bytes 2097152 | tf_op jit(solution)/shard_map/attention_forward/pallas_call | solution.py:560
  92.4 3.2 %collective-permute-start.11 = (bf16[8,32,1024]{2,1,0:T(8,128)(2,1)}, bf16[8,32,1024]{2,1,0:T(8,128)(2,1)S(1)}, u32[]{:S(2)}, u32[]{:S(2)}) collective-permute-start(bf16[8,32,1024]{2,1,0:T(8,128)(2,1)} %get-tuple-element.68.refs_0_), channel_id=1, source_target_pairs={{0,8},{8,0},{16,24},{24,16},{1,9},{9,1},{17,25},{25,17},{2,10},{10... | collective-permute-start | bytes 1572872 | tf_op jit(solution)/shard_map/ppermute | solution.py:33
  97.1 3.7 %collective-permute-done.9.refs_6_ = bf16[256,1024]{1,0:T(8,128)(2,1)S(1)} collective-permute-done((bf16[256,1024]{1,0:T(8,128)(2,1)S(1)}, bf16[256,1024]{1,0:T(8,128)(2,1)S(1)}, u32[]{:S(2)}, u32[]{:S(2)}) %collective-permute-start.9) | collective-permute-done | bytes 524320 | tf_op jit(solution)/shard_map/ppermute | solution.py:33
  100.7 6.5 %collective-permute-start.10 = (bf16[256,1024]{1,0:T(8,128)(2,1)S(1)}, bf16[256,1024]{1,0:T(8,128)(2,1)S(1)}, u32[]{:S(2)}, u32[]{:S(2)}) collective-permute-start(bf16[256,1024]{1,0:T(8,128)(2,1)S(1)} %collective-permute-done.9.refs_6_), channel_id=1, source_target_pairs={{0,8},{8,0},{16,24},{24,16},{1,9},{9,1},{17,25},{25,17},{2,10},{10... | collective-permute-start | bytes 1572872 | tf_op jit(solution)/shard_map/ppermute | solution.py:33
  112.0 3.4 %collective-permute-start.16 = (bf16[1024,256]{1,0:T(8,128)(2,1)S(1)}, bf16[1024,256]{1,0:T(8,128)(2,1)S(1)}, u32[]{:S(2)}, u32[]{:S(2)}) collective-permute-start(bf16[1024,256]{1,0:T(8,128)(2,1)S(1)} %collective-permute-done.15.refs_10_), channel_id=1, source_target_pairs={{0,8},{8,0},{16,24},{24,16},{1,9},{9,1},{17,25},{25,17},{2,10},{10... | collective-permute-start | bytes 1572872 | tf_op jit(solution)/shard_map/ppermute | solution.py:33
  117.7 7.5 %attention_branch.1 = (f32[256,1024]{1,0:T(8,128)}, bf16[1024,1024]{1,0:T(8,128)(2,1)}, bf16[1024,1024]{1,0:T(8,128)(2,1)}) custom-call(s32[2]{0:T(128)S(1)} %get-tuple-element.115.place_ref, bf16[256,1024]{1,0:T(8,128)(2,1)S(1)} %pick_rows.2.refs_0_.refs_3_, bf16[256,1024]{1,0:T(8,128)(2,1)S(1)} %copy-done.25, bf16[256,1024]{1,0:T(8,128)(2,1)S(1)} %copy-done.23, ...), custom_call_target="tpu_custom_call" | custom-call | flops 2147483648 | bytes 13668352 | tf_op jit(solution)/shard_map/attention_branch/pallas_call | solution.py:629
  125.3 3.0 %fusion.57 = (bf16[8,128,1024]{2,1,0:T(8,128)(2,1)S(1)}, bf16[8,128,1024]{2,1,0:T(8,128)(2,1)S(1)}) fusion(bf16[8,256,1024]{2,1,0:T(8,128)(2,1)} %bitcast.102), kind=kLoop, calls=%fused_computation.130 | loop fusion | bytes 8388608 | tf_op jit(solution)/shard_map/slice | solution.py:894
  128.3 2.9 %multiply_convert_fusion = (bf16[1024,1024]{1,0:T(8,128)(2,1)S(1)}, f32[1024,1024]{1,0:T(8,128)S(1)}) fusion(bf16[1024,1024]{1,0:T(8,128)(2,1)S(1)} %copy-done.59, bf16[1024,1024]{1,0:T(8,128)(2,1)S(1)} %bitcast.95), kind=kOutput, calls=%fused_computation.9 | convolution fusion | flops 2152726528 | bytes 10485760 | tf_op jit(solution)/shard_map/dot_general | solution.py:23
  131.4 3.6 %fusion.5.pre_ref = bf16[1024,1024]{1,0:T(8,128)(2,1)S(1)} fusion(f32[1024,1024]{1,0:T(8,128)S(1)} %get-tuple-element.140, bf16[1024,1024]{1,0:T(8,128)(2,1)S(1)} %copy-done.60, bf16[1024,1024]{1,0:T(8,128)(2,1)S(1)} %bitcast.90), kind=kOutput, calls=%fused_computation.8 | convolution fusion | flops 2157969408 | bytes 10485760 | tf_op jit(solution)/shard_map/dot_general | solution.py:23
  142.1 11.3 %hidden_grads.1 = (bf16[8,2,128,1024]{3,2,1,0:T(8,128)(2,1)}, f32[1024,128]{1,0:T(8,128)S(1)}) custom-call(s32[2]{0:T(128)S(1)} %get-tuple-element.115.place_ref, bf16[1024,1024]{1,0:T(8,128)(2,1)S(1)} %get-tuple-element.81.act_ref, bf16[1024,1024]{1,0:T(8,128)(2,1)} %get-tuple-element.76.carried_ref, bf16[1024,1024]{1,0:T(8,128)(2,1)} %get-tuple-element.74.norm_ref, ...), custom_call_target="tpu_custom_call" | custom-call | flops 4294967296 | bytes 12582912 | tf_op jit(solution)/shard_map/hidden_grads/pallas_call | solution.py:301
  162.5 9.8 %collective-permute-done.23.refs_2_ = bf16[256,1024]{1,0:T(8,128)(2,1)S(1)} collective-permute-done((bf16[256,1024]{1,0:T(8,128)(2,1)S(1)}, bf16[256,1024]{1,0:T(8,128)(2,1)S(1)}, u32[]{:S(2)}, u32[]{:S(2)}) %collective-permute-start.23) | collective-permute-done | bytes 524320 | tf_op jit(solution)/shard_map/ppermute | solution.py:33
  178.7 8.5 %attention_backward.1 = bf16[4,256,768]{2,1,0:T(8,128)(2,1)S(1)} custom-call(s32[4]{0:T(128)S(1)} %get-tuple-element.145.window_ref, s32[4]{0:T(128)S(1)} %scatter_custom_fusion.place_ref, s32[4]{0:T(128)S(1)} %get-tuple-element.144.first_ref, bf16[1024,256]{1,0:T(8,128)(2,1)S(1)} %copy-done.21, bf16[4,256,512]{2,1,0:T(8,128)(2,1)S(1)} %bitcast.82, ...), custom_call_target="tpu_custom_call" | custom-call | flops 1342177280 | bytes 3670016 | tf_op jit(solution)/shard_map/attention_backward/pallas_call | solution.py:591
  187.2 5.6 %weight_grad.4 = (bf16[4,4,32,512]{3,2,1,0:T(8,128)(2,1)}, bf16[4,4,32,512]{3,2,1,0:T(8,128)(2,1)S(1)}, f32[1024,128]{1,0:T(8,128)S(1)}) custom-call(s32[2]{0:T(128)S(1)} %get-tuple-element.115.place_ref, bf16[1024,1024]{1,0:T(8,128)(2,1)} %get-tuple-element.92.a_ref, bf16[1024,768]{1,0:T(8,128)(2,1)S(1)} %bitcast.73, bf16[1024,896]{1,0:T(8,128)(2,1)S(1)} %copy-done, ...), custom_call_target="tpu_custom_call" | custom-call | flops 1073741824 | bytes 4194304 | tf_op jit(solution)/shard_map/weight_grad/pallas_call | solution.py:243
  200.7 4.0 %weight_grad.5 = (bf16[4,4,32,384]{3,2,1,0:T(8,128)(2,1)S(1)}, bf16[4,4,32,384]{3,2,1,0:T(8,128)(2,1)S(1)}) custom-call(s32[2]{0:T(128)S(1)} %get-tuple-element.115.place_ref, bf16[1024,1024]{1,0:T(8,128)(2,1)} %get-tuple-element.92.a_ref, bf16[1024,768]{1,0:T(8,128)(2,1)S(1)} %bitcast.74, bf16[1024,896]{1,0:T(8,128)(2,1)S(1)} %copy-done, ...), custom_call_target="tpu_custom_call" | custom-call | flops 536870912 | bytes 3407872 | tf_op jit(solution)/shard_map/weight_grad/pallas_call | solution.py:243
  209.2 2.9 %collective-permute-done.32 = bf16[4,4,32,512]{3,2,1,0:T(8,128)(2,1)} collective-permute-done((bf16[4,4,32,512]{3,2,1,0:T(8,128)(2,1)}, bf16[4,4,32,512]{3,2,1,0:T(8,128)(2,1)}, u32[]{:S(2)}, u32[]{:S(2)}) %collective-permute-start.32) | collective-permute-done | bytes 524320 | tf_op jit(solution)/shard_map/ppermute | solution.py:33
  217.2 3.4 %place_rows.2 = bf16[2048,1024]{1,0:T(8,128)(2,1)} custom-call(s32[1,256]{1,0:T(1,128)S(1)} %fusion.71.ids_ref, bf16[256,1024]{1,0:T(8,128)(2,1)S(1)} %get-tuple-element.95.new_ref, bf16[2048,1024]{1,0:T(8,128)(2,1)S(1)} %bitcast.70), custom_call_target="tpu_custom_call" | custom-call | flops 1073741824 | bytes 8388608 | tf_op jit(solution)/shard_map/place_rows/pallas_call | solution.py:411
  223.5 2.4 collective-permute-start.34
  227.8 8.5 %collective-permute-done.30 = bf16[2,4,32,384]{3,2,1,0:T(8,128)(2,1)S(1)} collective-permute-done((bf16[2,4,32,384]{3,2,1,0:T(8,128)(2,1)S(1)}, bf16[2,4,32,384]{3,2,1,0:T(8,128)(2,1)S(1)}, u32[]{:S(2)}, u32[]{:S(2)}) %collective-permute-start.30) | collective-permute-done | bytes 196640 | tf_op jit(solution)/shard_map/ppermute | solution.py:33
  236.5 10.6 %collective-permute-done.31 = bf16[1,4,32,384]{3,2,1,0:T(8,128)(2,1)S(1)} collective-permute-done((bf16[1,4,32,384]{3,2,1,0:T(8,128)(2,1)S(1)}, bf16[1,4,32,384]{3,2,1,0:T(8,128)(2,1)S(1)}, u32[]{:S(2)}, u32[]{:S(2)}) %collective-permute-start.31) | collective-permute-done | bytes 98336 | tf_op jit(solution)/shard_map/ppermute | solution.py:33
  251.2 3.3 %reduce-scatter.2.cloned.1.call-done = bf16[1,2,128,1024]{3,2,1,0:T(8,128)(2,1)} async-done(((bf16[8,2,128,1024]{3,2,1,0:T(8,128)(2,1)}), bf16[1,2,128,1024]{3,2,1,0:T(8,128)(2,1)}) %reduce-scatter.2.cloned.1.call-update) | async-done | bytes 524304 | tf_op jit(solution)/shard_map/reduce_scatter | solution.py:930
  255.6 3.2 %collective-permute-start.41 = (bf16[128,1024]{1,0:T(8,128)(2,1)S(1)}, bf16[128,1024]{1,0:T(8,128)(2,1)S(1)}, u32[]{:S(2)}, u32[]{:S(2)}) collective-permute-start(bf16[128,1024]{1,0:T(8,128)(2,1)S(1)} %get-tuple-element.124), channel_id=1, source_target_pairs={{0,0},{1,4},{2,8},{3,12},{4,16},{5,20},{6,24},{7,28},{8,1},{9,5},{... | collective-permute-start | bytes 786440 | tf_op jit(solution)/shard_map/ppermute | solution.py:1004
  264.5 3.3 %place_rows.3 = bf16[2048,1024]{1,0:T(8,128)(2,1)} custom-call(s32[1,256]{1,0:T(1,128)S(1)} %fusion.71.ids_ref, bf16[256,1024]{1,0:T(8,128)(2,1)S(1)} %fusion.13.new_ref, bf16[2048,1024]{1,0:T(8,128)(2,1)S(1)} %bitcast.72), custom_call_target="tpu_custom_call" | custom-call | flops 1073741824 | bytes 8388608 | tf_op jit(solution)/shard_map/place_rows/pallas_call | solution.py:411
  267.8 7.6 %collective-permute-done.37.refs_3_ = bf16[32,1920]{1,0:T(8,128)(2,1)S(1)} collective-permute-done((bf16[32,1920]{1,0:T(8,128)(2,1)S(1)}, bf16[32,1920]{1,0:T(8,128)(2,1)S(1)}, u32[]{:S(2)}, u32[]{:S(2)}) %collective-permute-start.37) | collective-permute-done | bytes 122912 | tf_op jit(solution)/shard_map/ppermute | solution.py:33
  275.5 2.6 collective-permute-done.36.refs_2_
  (275 shorter events, 92.6 us)
Async XLA Ops:
  7.2 118.1 %all-gather.3.cloned.1.call-start = ((), (), s32[]{:S(2)}) async-start(), calls=%async_computation.2 | async-start | bytes 4718592 | tf_op jit(solution)/shard_map/all_gather | solution.py:893
  13.6 12.5 %collective-permute-start.5 = (bf16[128,1152]{1,0:T(8,128)(2,1)S(1)}, bf16[128,1152]{1,0:T(8,128)(2,1)S(1)}, u32[]{:S(2)}, u32[]{:S(2)}) collective-permute-start(bf16[128,1152]{1,0:T(8,128)(2,1)S(1)} %first_shard.1), channel_id=1, source_target_pairs={{0,6},{1,7},{2,4},{3,5},{4,2},{5,3},{6,0},{7,1},{8,14},{9,15},{10,... | collective-permute-start | bytes 884744 | tf_op jit(solution)/shard_map/ppermute | solution.py:33
  16.9 24.7 %collective-permute-start.4 = (bf16[128,1152]{1,0:T(8,128)(2,1)S(1)}, bf16[128,1152]{1,0:T(8,128)(2,1)S(1)}, u32[]{:S(2)}, u32[]{:S(2)}) collective-permute-start(bf16[128,1152]{1,0:T(8,128)(2,1)S(1)} %first_shard.1), channel_id=1, source_target_pairs={{0,4},{1,5},{2,6},{3,7},{4,0},{5,1},{6,2},{7,3},{8,12},{9,13},{10,... | collective-permute-start | bytes 884744 | tf_op jit(solution)/shard_map/ppermute | solution.py:33
  17.0 24.7 %collective-permute-start.3 = (bf16[128,1152]{1,0:T(8,128)(2,1)S(1)}, bf16[128,1152]{1,0:T(8,128)(2,1)S(1)}, u32[]{:S(2)}, u32[]{:S(2)}) collective-permute-start(bf16[128,1152]{1,0:T(8,128)(2,1)S(1)} %first_shard.1), channel_id=1, source_target_pairs={{0,2},{1,3},{2,0},{3,1},{4,6},{5,7},{6,4},{7,5},{8,10},{9,11},{10,... | collective-permute-start | bytes 884744 | tf_op jit(solution)/shard_map/ppermute | solution.py:33
  41.7 212.8 %reduce-scatter.2.cloned.1.call-start = ((), (), s32[]{:S(2)}) async-start(), calls=%async_computation.1 | async-start | bytes 4718592 | tf_op jit(solution)/shard_map/reduce_scatter | solution.py:930
  41.7 12.2 %collective-permute-start.1 = (bf16[256,1024]{1,0:T(8,128)(2,1)S(1)}, bf16[256,1024]{1,0:T(8,128)(2,1)S(1)}, u32[]{:S(2)}, u32[]{:S(2)}) collective-permute-start(bf16[256,1024]{1,0:T(8,128)(2,1)S(1)} %pick_rows.2.refs_0_.refs_3_), channel_id=1, source_target_pairs={{0,16},{8,24},{16,0},{24,8},{1,17},{9,25},{17,1},{25,9},{2,18},{10... | collective-permute-start | bytes 1572872 | tf_op jit(solution)/shard_map/ppermute | solution.py:33
  44.2 25.3 %collective-permute-start.7 = (bf16[3,128,1152]{2,1,0:T(8,128)(2,1)S(1)}, bf16[3,128,1152]{2,1,0:T(8,128)(2,1)}, u32[]{:S(2)}, u32[]{:S(2)}) collective-permute-start(bf16[3,128,1152]{2,1,0:T(8,128)(2,1)S(1)} %pad_maximum_fusion.refs_5_), channel_id=1, source_target_pairs={{0,1},{1,0},{2,3},{3,2},{4,5},{5,4},{6,7},{7,6},{8,9},{9,8},{10,11... | collective-permute-start | bytes 2654216 | tf_op jit(solution)/shard_map/ppermute | solution.py:33
  44.5 12.3 %collective-permute-start = (bf16[256,1024]{1,0:T(8,128)(2,1)S(1)}, bf16[256,1024]{1,0:T(8,128)(2,1)S(1)}, u32[]{:S(2)}, u32[]{:S(2)}) collective-permute-start(bf16[256,1024]{1,0:T(8,128)(2,1)S(1)} %pick_rows.2.refs_0_.refs_3_), channel_id=1, source_target_pairs={{0,8},{8,0},{16,24},{24,16},{1,9},{9,1},{17,25},{25,17},{2,10},{10... | collective-permute-start | bytes 1572872 | tf_op jit(solution)/shard_map/ppermute | solution.py:33
  78.4 17.2 %collective-permute-start.12 = (bf16[8,32,1024]{2,1,0:T(8,128)(2,1)}, bf16[8,32,1024]{2,1,0:T(8,128)(2,1)}, u32[]{:S(2)}, u32[]{:S(2)}) collective-permute-start(bf16[8,32,1024]{2,1,0:T(8,128)(2,1)} %get-tuple-element.68.refs_0_), channel_id=1, source_target_pairs={{0,16},{8,24},{16,0},{24,8},{1,17},{9,25},{17,1},{25,9},{2,18},{10... | collective-permute-start | bytes 1572872 | tf_op jit(solution)/shard_map/ppermute | solution.py:33
  85.4 15.3 %collective-permute-start.9 = (bf16[256,1024]{1,0:T(8,128)(2,1)S(1)}, bf16[256,1024]{1,0:T(8,128)(2,1)S(1)}, u32[]{:S(2)}, u32[]{:S(2)}) collective-permute-start(bf16[256,1024]{1,0:T(8,128)(2,1)S(1)} %pick_rows.3.refs_4_), channel_id=1, source_target_pairs={{0,16},{8,24},{16,0},{24,8},{1,17},{9,25},{17,1},{25,9},{2,18},{10... | collective-permute-start | bytes 1572872 | tf_op jit(solution)/shard_map/ppermute | solution.py:33
  92.4 14.9 %collective-permute-start.11 = (bf16[8,32,1024]{2,1,0:T(8,128)(2,1)}, bf16[8,32,1024]{2,1,0:T(8,128)(2,1)S(1)}, u32[]{:S(2)}, u32[]{:S(2)}) collective-permute-start(bf16[8,32,1024]{2,1,0:T(8,128)(2,1)} %get-tuple-element.68.refs_0_), channel_id=1, source_target_pairs={{0,8},{8,0},{16,24},{24,16},{1,9},{9,1},{17,25},{25,17},{2,10},{10... | collective-permute-start | bytes 1572872 | tf_op jit(solution)/shard_map/ppermute | solution.py:33
  96.2 15.8 %collective-permute-start.15 = (bf16[1024,256]{1,0:T(8,128)(2,1)S(1)}, bf16[1024,256]{1,0:T(8,128)(2,1)S(1)}, u32[]{:S(2)}, u32[]{:S(2)}) collective-permute-start(bf16[1024,256]{1,0:T(8,128)(2,1)S(1)} %get-tuple-element.70.refs_8_.a_ref.o_ref), channel_id=1, source_target_pairs={{0,16},{8,24},{16,0},{24,8},{1,17},{9,25},{17,1},{25,9},{2,18},{10... | collective-permute-start | bytes 1572872 | tf_op jit(solution)/shard_map/ppermute | solution.py:33
  96.8 19.6 %collective-permute-start.8 = (bf16[256,1024]{1,0:T(8,128)(2,1)S(1)}, bf16[256,1024]{1,0:T(8,128)(2,1)S(1)}, u32[]{:S(2)}, u32[]{:S(2)}) collective-permute-start(bf16[256,1024]{1,0:T(8,128)(2,1)S(1)} %pick_rows.3.refs_4_), channel_id=1, source_target_pairs={{0,8},{8,0},{16,24},{24,16},{1,9},{9,1},{17,25},{25,17},{2,10},{10... | collective-permute-start | bytes 1572872 | tf_op jit(solution)/shard_map/ppermute | solution.py:33
  100.7 15.7 %collective-permute-start.10 = (bf16[256,1024]{1,0:T(8,128)(2,1)S(1)}, bf16[256,1024]{1,0:T(8,128)(2,1)S(1)}, u32[]{:S(2)}, u32[]{:S(2)}) collective-permute-start(bf16[256,1024]{1,0:T(8,128)(2,1)S(1)} %collective-permute-done.9.refs_6_), channel_id=1, source_target_pairs={{0,8},{8,0},{16,24},{24,16},{1,9},{9,1},{17,25},{25,17},{2,10},{10... | collective-permute-start | bytes 1572872 | tf_op jit(solution)/shard_map/ppermute | solution.py:33
  137.8 16.5 %collective-permute-start.17 = (bf16[256,1024]{1,0:T(8,128)(2,1)}, bf16[256,1024]{1,0:T(8,128)(2,1)}, u32[]{:S(2)}, u32[]{:S(2)}) collective-permute-start(bf16[256,1024]{1,0:T(8,128)(2,1)} %fusion.27), channel_id=1, source_target_pairs={{0,8},{8,0},{16,24},{24,16},{1,9},{9,1},{17,25},{25,17},{2,10},{10... | collective-permute-start | bytes 1572872 | tf_op jit(solution)/shard_map/ppermute | solution.py:33
  139.4 14.8 %collective-permute-start.19 = (bf16[256,1024]{1,0:T(8,128)(2,1)}, bf16[256,1024]{1,0:T(8,128)(2,1)}, u32[]{:S(2)}, u32[]{:S(2)}) collective-permute-start(bf16[256,1024]{1,0:T(8,128)(2,1)} %add_convert_fusion.1), channel_id=1, source_target_pairs={{0,16},{8,24},{16,0},{24,8},{1,17},{9,25},{17,1},{25,9},{2,18},{10... | collective-permute-start | bytes 1572872 | tf_op jit(solution)/shard_map/ppermute | solution.py:33
  159.0 13.4 %collective-permute-start.23 = (bf16[256,1024]{1,0:T(8,128)(2,1)S(1)}, bf16[256,1024]{1,0:T(8,128)(2,1)S(1)}, u32[]{:S(2)}, u32[]{:S(2)}) collective-permute-start(bf16[256,1024]{1,0:T(8,128)(2,1)S(1)} %fusion.9.refs_0_), channel_id=1, source_target_pairs={{0,16},{8,24},{16,0},{24,8},{1,17},{9,25},{17,1},{25,9},{2,18},{10... | collective-permute-start | bytes 1572872 | tf_op jit(solution)/shard_map/ppermute | solution.py:33
  161.1 34.5 %collective-permute-start.21 = (bf16[256,1024]{1,0:T(8,128)(2,1)}, bf16[256,1024]{1,0:T(8,128)(2,1)S(1)}, u32[]{:S(2)}, u32[]{:S(2)}) collective-permute-start(bf16[256,1024]{1,0:T(8,128)(2,1)} %fusion.35), channel_id=1, source_target_pairs={{0,8},{8,0},{16,24},{24,16},{1,9},{9,1},{17,25},{25,17},{2,10},{10... | collective-permute-start | bytes 1572872 | tf_op jit(solution)/shard_map/ppermute | solution.py:33
  162.4 12.4 %collective-permute-start.22 = (bf16[256,1024]{1,0:T(8,128)(2,1)S(1)}, bf16[256,1024]{1,0:T(8,128)(2,1)S(1)}, u32[]{:S(2)}, u32[]{:S(2)}) collective-permute-start(bf16[256,1024]{1,0:T(8,128)(2,1)S(1)} %fusion.31), channel_id=1, source_target_pairs={{0,8},{8,0},{16,24},{24,16},{1,9},{9,1},{17,25},{25,17},{2,10},{10... | collective-permute-start | bytes 1572872 | tf_op jit(solution)/shard_map/ppermute | solution.py:33
  175.0 20.6 %collective-permute-start.25 = (bf16[256,1024]{1,0:T(8,128)(2,1)S(1)}, bf16[256,1024]{1,0:T(8,128)(2,1)S(1)}, u32[]{:S(2)}, u32[]{:S(2)}) collective-permute-start(bf16[256,1024]{1,0:T(8,128)(2,1)S(1)} %add_convert_fusion), channel_id=1, source_target_pairs={{0,16},{8,24},{16,0},{24,8},{1,17},{9,25},{17,1},{25,9},{2,18},{10... | collective-permute-start | bytes 1572872 | tf_op jit(solution)/shard_map/ppermute | solution.py:33
  178.3 15.7 %collective-permute-start.38 = (bf16[4,1,32,1024]{3,2,1,0:T(8,128)(2,1)S(1)}, bf16[4,1,32,1024]{3,2,1,0:T(8,128)(2,1)S(1)}, u32[]{:S(2)}, u32[]{:S(2)}) collective-permute-start(bf16[4,1,32,1024]{3,2,1,0:T(8,128)(2,1)S(1)} %get-tuple-element.87), channel_id=1, source_target_pairs={{0,1},{1,0},{2,3},{3,2},{4,5},{5,4},{6,7},{7,6},{8,9},{9,8},{10,11... | collective-permute-start | bytes 786440 | tf_op jit(solution)/shard_map/ppermute | solution.py:33
  192.8 19.3 %collective-permute-start.32 = (bf16[4,4,32,512]{3,2,1,0:T(8,128)(2,1)}, bf16[4,4,32,512]{3,2,1,0:T(8,128)(2,1)}, u32[]{:S(2)}, u32[]{:S(2)}) collective-permute-start(bf16[4,4,32,512]{3,2,1,0:T(8,128)(2,1)} %get-tuple-element.91), channel_id=1, source_target_pairs={{0,1},{1,0},{2,3},{3,2},{4,5},{5,4},{6,7},{7,6},{8,9},{9,8},{10,11... | collective-permute-start | bytes 1572872 | tf_op jit(solution)/shard_map/ppermute | solution.py:33
  204.6 21.2 %collective-permute-start.29 = (bf16[4,4,32,384]{3,2,1,0:T(8,128)(2,1)S(1)}, bf16[4,4,32,384]{3,2,1,0:T(8,128)(2,1)S(1)}, u32[]{:S(2)}, u32[]{:S(2)}) collective-permute-start(bf16[4,4,32,384]{3,2,1,0:T(8,128)(2,1)S(1)} %get-tuple-element.94), channel_id=1, source_target_pairs={{0,2},{1,3},{2,0},{3,1},{4,6},{5,7},{6,4},{7,5},{8,10},{9,11},{10,... | collective-permute-start | bytes 1179656 | tf_op jit(solution)/shard_map/ppermute | solution.py:33
  204.7 12.4 %collective-permute-start.39 = (bf16[2,1,32,1024]{3,2,1,0:T(8,128)(2,1)S(1)}, bf16[2,1,32,1024]{3,2,1,0:T(8,128)(2,1)S(1)}, u32[]{:S(2)}, u32[]{:S(2)}) collective-permute-start(bf16[2,1,32,1024]{3,2,1,0:T(8,128)(2,1)S(1)} %copy-done.50), channel_id=1, source_target_pairs={{0,2},{1,3},{2,0},{3,1},{4,6},{5,7},{6,4},{7,5},{8,10},{9,11},{10,... | collective-permute-start | bytes 393224 | tf_op jit(solution)/shard_map/ppermute | solution.py:33
  206.8 41.6 %collective-permute-start.26 = (bf16[256,1024]{1,0:T(8,128)(2,1)S(1)}, bf16[256,1024]{1,0:T(8,128)(2,1)S(1)}, u32[]{:S(2)}, u32[]{:S(2)}) collective-permute-start(bf16[256,1024]{1,0:T(8,128)(2,1)S(1)} %convolution_convert_fusion.1), channel_id=1, source_target_pairs={{0,8},{8,0},{16,24},{24,16},{1,9},{9,1},{17,25},{25,17},{2,10},{10... | collective-permute-start | bytes 1572872 | tf_op jit(solution)/shard_map/ppermute | solution.py:33
  209.1 17.1 %collective-permute-start.27 = (bf16[256,1024]{1,0:T(8,128)(2,1)S(1)}, bf16[256,1024]{1,0:T(8,128)(2,1)S(1)}, u32[]{:S(2)}, u32[]{:S(2)}) collective-permute-start(bf16[256,1024]{1,0:T(8,128)(2,1)S(1)} %convolution_convert_fusion), channel_id=1, source_target_pairs={{0,8},{8,0},{16,24},{24,16},{1,9},{9,1},{17,25},{25,17},{2,10},{10... | collective-permute-start | bytes 1572872 | tf_op jit(solution)/shard_map/ppermute | solution.py:33
  223.5 13.0 %collective-permute-start.34 = (bf16[1,4,32,512]{3,2,1,0:T(8,128)(2,1)S(1)}, bf16[1,4,32,512]{3,2,1,0:T(8,128)(2,1)S(1)}, u32[]{:S(2)}, u32[]{:S(2)}) collective-permute-start(bf16[1,4,32,512]{3,2,1,0:T(8,128)(2,1)S(1)} %slice.293), channel_id=1, source_target_pairs={{0,4},{1,5},{2,6},{3,7},{4,0},{5,1},{6,2},{7,3},{8,12},{9,13},{10,... | collective-permute-start | bytes 393224 | tf_op jit(solution)/shard_map/ppermute | solution.py:33
  226.8 21.6 %collective-permute-start.28 = (bf16[256,1024]{1,0:T(8,128)(2,1)S(1)}, bf16[256,1024]{1,0:T(8,128)(2,1)S(1)}, u32[]{:S(2)}, u32[]{:S(2)}) collective-permute-start(bf16[256,1024]{1,0:T(8,128)(2,1)S(1)} %fusion.7), channel_id=1, source_target_pairs={{0,16},{8,24},{16,0},{24,8},{1,17},{9,25},{17,1},{25,9},{2,18},{10... | collective-permute-start | bytes 1572872 | tf_op jit(solution)/shard_map/ppermute | solution.py:33
  255.6 24.3 %collective-permute-start.41 = (bf16[128,1024]{1,0:T(8,128)(2,1)S(1)}, bf16[128,1024]{1,0:T(8,128)(2,1)S(1)}, u32[]{:S(2)}, u32[]{:S(2)}) collective-permute-start(bf16[128,1024]{1,0:T(8,128)(2,1)S(1)} %get-tuple-element.124), channel_id=1, source_target_pairs={{0,0},{1,4},{2,8},{3,12},{4,16},{5,20},{6,24},{7,28},{8,1},{9,5},{... | collective-permute-start | bytes 786440 | tf_op jit(solution)/shard_map/ppermute | solution.py:1004
  259.7 15.7 %collective-permute-start.37 = (bf16[32,1920]{1,0:T(8,128)(2,1)S(1)}, bf16[32,1920]{1,0:T(8,128)(2,1)S(1)}, u32[]{:S(2)}, u32[]{:S(2)}) collective-permute-start(bf16[32,1920]{1,0:T(8,128)(2,1)S(1)} %get-tuple-element.128), channel_id=1, source_target_pairs={{0,24},{8,16},{16,8},{24,0},{1,25},{9,17},{17,9},{25,1},{2,26},{10... | collective-permute-start | bytes 368648 | tf_op jit(solution)/shard_map/ppermute | solution.py:33
  261.4 16.6 %collective-permute-start.36 = (bf16[32,1920]{1,0:T(8,128)(2,1)S(1)}, bf16[32,1920]{1,0:T(8,128)(2,1)S(1)}, u32[]{:S(2)}, u32[]{:S(2)}) collective-permute-start(bf16[32,1920]{1,0:T(8,128)(2,1)S(1)} %get-tuple-element.129), channel_id=1, source_target_pairs={{0,16},{8,24},{16,0},{24,8},{1,17},{9,25},{17,1},{25,9},{2,18},{10... | collective-permute-start | bytes 368648 | tf_op jit(solution)/shard_map/ppermute | solution.py:33
  261.4 16.6 %collective-permute-start.35 = (bf16[32,1920]{1,0:T(8,128)(2,1)S(1)}, bf16[32,1920]{1,0:T(8,128)(2,1)S(1)}, u32[]{:S(2)}, u32[]{:S(2)}) collective-permute-start(bf16[32,1920]{1,0:T(8,128)(2,1)S(1)} %get-tuple-element.130), channel_id=1, source_target_pairs={{0,8},{8,0},{16,24},{24,16},{1,9},{9,1},{17,25},{25,17},{2,10},{10... | collective-permute-start | bytes 368648 | tf_op jit(solution)/shard_map/ppermute | solution.py:33
  (73 other events, 453.7 us)
Sparse Core Ops, SparseCore 0:
  41.8 75.2 all-gather.2
  154.4 100.0 reduce-scatter.1

commit v4 on v3

--- a/solution.py
+++ b/solution.py
@@ -45,7 +45,7 @@
     top = lax.axis_size(axis) // 2
     for bit in bits_down(lax.axis_size(axis)):
         for key in list(blocks):
-            block = blocks[key] if bit == top else after(blocks[key], *waits)
+            block = after(blocks[key], *waits) if key else blocks[key]
             blocks[key ^ bit] = flip(block, axis, bit)
     return [blocks[key] for key in sorted(blocks)]
 
@@ -166,7 +166,12 @@
 GRAD_TILE = 512
 
 
-def store_blocks(product, tail, column, place_ref, per, fsdps, first, refs):
+def down_slot(shard, fsdps, seqs):
+    group = fsdps // seqs
+    return shard % group * seqs + shard // group
+
+
+def store_blocks(product, tail, column, place_ref, per, fsdps, seqs, first, refs):
     whole = product.astype(BF16)
     cols = product.shape[1]
     pieces = product.shape[0] // per
@@ -182,7 +187,8 @@
                 ref[slot, part, :, cols:] = tail[rows]
 
         if first is None:
-            store(refs[0], block)
+            alone = refs[0].shape[1] == 1
+            store(refs[0], down_slot(block, fsdps, seqs) if alone else block)
             continue
         block = block ^ place_ref[0]
         slot = lax.div(block, 2 * first) * first + lax.rem(block, first)
@@ -191,7 +197,7 @@
         pl.when(sent == 0)(partial(store, refs[1], slot))
 
 
-def weight_grad_kernel(place_ref, a_ref, b_ref, *refs, per, fsdps, first, gain_lane, with_logits, tail_out):
+def weight_grad_kernel(place_ref, a_ref, b_ref, *refs, per, fsdps, seqs, first, gain_lane, with_logits, tail_out):
     column = pl.program_id(0)
     product = mm(a_ref[...], b_ref[...], TN)
     refs = list(refs)
@@ -210,7 +216,7 @@
     if tail_out:
         refs.pop()[...] = tail
     tail = tail.astype(BF16) if with_logits else None
-    store_blocks(product, tail, column, place_ref, per, fsdps, first, refs)
+    store_blocks(product, tail, column, place_ref, per, fsdps, seqs, first, refs)
 
 
 def weight_grad(place, a, b, parts, first, gain=None, logits=None, cols=None, at_b=0):
@@ -245,6 +251,7 @@
             weight_grad_kernel,
             per=per,
             fsdps=fsdps,
+            seqs=lax.axis_size("seq"),
             first=first,
             gain_lane=lane,
             with_logits=logits is not None,
@@ -268,12 +275,13 @@
 
 
 def hidden_grads_kernel(
-    place_ref, act_ref, carried_ref, norm_ref, pre_ref, w_ref, vec_ref, both_ref, tail_ref, *, per, down_per, fsdps, gain_lane
+    place_ref, act_ref, carried_ref, norm_ref, pre_ref, w_ref, vec_ref, both_ref, tail_ref, *, per, down_per, fsdps, seqs, gain_lane
 ):
     column = pl.program_id(0)
     down = mm(act_ref[...], carried_ref[...], TN).astype(BF16)
     for t in range(down.shape[0] // down_per):
-        both_ref[column * (down.shape[0] // down_per) + t, 1] = down[t * down_per : (t + 1) * down_per]
+        slot = down_slot(column * (down.shape[0] // down_per) + t, fsdps, seqs)
+        both_ref[slot, 1] = down[t * down_per : (t + 1) * down_per]
     product = mm(norm_ref[...], pre_ref[...], TN)
     lane = lax.broadcasted_iota(jnp.int32, (product.shape[0], LANES), 1)
     gain = vec_ref[...].astype(F32)[:, gain_lane : gain_lane + 1]
@@ -304,6 +312,7 @@
             per=total // (seqs * fsdps),
             down_per=total // fsdps,
             fsdps=fsdps,
+            seqs=seqs,
             gain_lane=lane,
         ),
         grid_spec=pltpu.PrefetchScalarGridSpec(
@@ -357,42 +366,49 @@
 ROW_TILE = 512
 
 
-def pick_rows_kernel(ids_ref, from_ref, to_ref, total):
+def pick_rows_kernel(ids_ref, *refs):
+    count = len(refs) - 2
+    to_ref, total = refs[count:]
     chunk = pl.program_id(0)
     ids = ids_ref[...] - chunk * ROW_TILE
     hit = ids == lax.broadcasted_iota(jnp.int32, (ids.shape[0], ROW_TILE), 1)
-    found = mm(jnp.where(hit, 1.0, 0.0).astype(BF16), from_ref[...], NN)
-
-    @pl.when(chunk == 0)
-    def _():
-        total[...] = found
-
-    @pl.when(chunk > 0)
-    def _():
-        total[...] += found
-
-    to_ref[...] = total[...].astype(BF16)
-
-
-def pick_rows(source, ids):
-    length, width = source.shape
+    ones = jnp.where(hit, 1.0, 0.0).astype(BF16)
+    for i in range(count):
+        found = mm(ones, refs[i][...], NN)
+
+        @pl.when(chunk == 0)
+        def _():
+            total[i] = found
+
+        @pl.when(chunk > 0)
+        def _():
+            total[i] += found
+
+        @pl.when(chunk == pl.num_programs(0) - 1)
+        def _():
+            to_ref[i] = total[i].astype(BF16)
+
+
+def pick_rows(sources, ids):
+    length, width = sources[0].shape
     rows = ids.shape[0]
+    count = len(sources)
     return pl.pallas_call(
         pick_rows_kernel,
         grid=(length // ROW_TILE,),
-        in_specs=[
-            pl.BlockSpec((rows, 1), lambda c: (0, 0)),
-            pl.BlockSpec((ROW_TILE, width), lambda c: (c, 0)),
-        ],
-        out_specs=pl.BlockSpec((rows, width), lambda c: (0, 0)),
-        out_shape=jax.ShapeDtypeStruct((rows, width), BF16),
-        scratch_shapes=[pltpu.VMEM((rows, width), F32)],
+        in_specs=[pl.BlockSpec((rows, 1), lambda c: (0, 0))]
+        + [pl.BlockSpec((ROW_TILE, width), lambda c: (c, 0))] * count,
+        out_specs=pl.BlockSpec((count, rows, width), lambda c: (0, 0, 0)),
+        out_shape=jax.ShapeDtypeStruct((count, rows, width), BF16),
+        scratch_shapes=[pltpu.VMEM((count, rows, width), F32)],
         compiler_params=pltpu.CompilerParams(vmem_limit_bytes=VMEM_LIMIT),
         cost_estimate=pl.CostEstimate(
-            flops=2 * rows * length * width, transcendentals=0, bytes_accessed=2 * length * width
+            flops=2 * count * rows * length * width,
+            transcendentals=0,
+            bytes_accessed=2 * count * length * width,
         ),
         name="pick_rows",
-    )(ids[:, None], source)
+    )(ids[:, None], *sources)
 
 
 def place_rows_kernel(ids_ref, new_ref, from_ref, to_ref):
@@ -731,10 +747,10 @@
     vec_ref[...] = vec[:8]
     gain = vec[1:2]
     weight = w_ref[:, : 3 * span]
-    rows = x_refs[0].shape[0]
+    rows = x_refs[0].shape[1]
     for k in range(seqs):
         here = slice(k * rows, (k + 1) * rows)
-        x = x_refs[k][...]
+        x = x_refs[k][0]
         x_f = x.astype(F32)
         normal = (x_f * norm_scale(x_f) * gain).astype(BF16)
         normal_ref[here, :] = normal
@@ -746,7 +762,7 @@
 
 def project(place, x_blocks, pieces, span):
     slow, fast = fsdp_sizes()
-    rows, width = x_blocks[0].shape
+    _, rows, width = x_blocks[0].shape
     total = rows * len(x_blocks)
     cols = pieces[0].shape[2] - span
     out_shape = [
@@ -765,9 +781,9 @@
 
 
 def branch_kernel(place_ref, *refs, seqs):
-    x_refs, g_refs, att_refs = (refs[i * seqs : (i + 1) * seqs] for i in range(3))
-    w_ref, vec_ref, rate_ref, branch_ref, normal_ref, carried_ref = refs[3 * seqs :]
-    rows = x_refs[0].shape[0]
+    x_refs, att_refs = refs[:seqs], refs[seqs : 2 * seqs]
+    w_ref, vec_ref, rate_ref, branch_ref, normal_ref, carried_ref = refs[2 * seqs :]
+    rows = x_refs[0].shape[1]
     span = att_refs[0].shape[1]
     gain = vec_ref[2:3, :]
     for j in range(seqs):
@@ -778,20 +794,20 @@
             branch = branch + mm(att_refs[b][there, :], w_ref[b * span : (b + 1) * span, :], NN)
         if j == 0:
             branch_ref[...] = branch
-        middle = x_refs[j][...].astype(F32) + branch
+        middle = x_refs[j][0].astype(F32) + branch
         normal_ref[here, :] = (middle * norm_scale(middle) * gain).astype(BF16)
-        carried_ref[here, :] = (rate_ref[here, :] * g_refs[j][...].astype(F32)).astype(BF16)
-
-
-def attention_branch(place, x_blocks, g_blocks, att_blocks, w_out, vectors, rate):
-    rows, width = x_blocks[0].shape
-    seqs = len(x_blocks)
+        carried_ref[here, :] = (rate_ref[here, :] * x_refs[j][1].astype(F32)).astype(BF16)
+
+
+def attention_branch(place, blocks, att_blocks, w_out, vectors, rate):
+    _, rows, width = blocks[0].shape
+    seqs = len(blocks)
     out_shape = [
         jax.ShapeDtypeStruct((rows, width), F32),
         jax.ShapeDtypeStruct((rows * seqs, width), BF16),
         jax.ShapeDtypeStruct((rows * seqs, width), BF16),
     ]
-    args = [*x_blocks, *g_blocks, *att_blocks, w_out, vectors, rate]
+    args = [*blocks, *att_blocks, w_out, vectors, rate]
     return one_step(
         partial(branch_kernel, seqs=seqs),
         "attention_branch",
@@ -881,14 +897,13 @@
     first_own = first_shard(place, qkv_weight, tails, out_weight, heads_width)
     first_slow = gather_slow(first_own)
     first_got = own_fast(first_slow[0])
-    x_own = pick_rows(stream_in, after(row_ids, first_own))
-    x_blocks = gather_blocks(x_own, "seq")
+    picked = pick_rows([stream_in, grad_in], after(row_ids, first_own))
 
     span = down_weight.shape[0] // seqs
     square = own_hidden == width and span % LANES == 0
     shard_rows = up_weight.shape[0]
     if square:
-        hidden_own = hidden_shard(place, after(up_weight, x_own, *first_got), down_weight, span)
+        hidden_own = hidden_shard(place, after(up_weight, picked, *first_got), down_weight, span)
         hidden_late = after(hidden_own, *first_slow[1:])
         hidden_all = lax.all_gather(hidden_late, "fsdp", axis=0)
         w_up = hidden_all[:, :shard_rows].reshape(width, own_hidden)
@@ -901,10 +916,9 @@
         w_up = lax.all_gather(hidden_own, "fsdp", axis=0, tiled=True)
         w_down = lax.all_gather(down_own, "fsdp", axis=0, tiled=True)
     first_pieces = gather_fast(first_slow[0], after(tuple(first_slow[1:]), hidden_own), first_got)
-    g_own = pick_rows(grad_in, after(row_ids, x_blocks[seqs // 2]))
-    g_blocks = gather_blocks(g_own, "seq")
+    blocks = gather_blocks(picked, "seq", first_pieces[-1])
     out_part, w_qkv, vectors, normal_a, q, kv, rate = project(
-        place, x_blocks, first_pieces, heads_width
+        place, blocks, first_pieces, heads_width
     )
     router_w, gain_a, gain_m = vectors[0:1], vectors[1:2], vectors[2:3]
     tail_at = 3 * heads_width // LANES
@@ -914,7 +928,7 @@
     att_blocks = gather_blocks(att_own, "seq", out_ordered)
     w_out = out_ordered[:heads_width]
     branch_o, normal_m, carried_b = attention_branch(
-        place, x_blocks, g_blocks, att_blocks, out_ordered, vectors, rate
+        place, blocks, att_blocks, out_ordered, vectors, rate
     )
     pre_act = mm(normal_m, w_up, NN)
     cdf = 0.5 * (1.0 + lax.erf(pre_act * (0.5**0.5)))
@@ -948,8 +962,8 @@
         )
         up_part, down_part = scatter(up_grad), scatter(down_grad)[0]
 
-    x_o = x_blocks[0].astype(F32)
-    g_o = g_blocks[0].astype(F32)
+    x_o = picked[0].astype(F32)
+    g_o = picked[1].astype(F32)
     rate_o = cut(rate, 0)
     middle_o = x_o + branch_o
     grad_middle = norm_back(middle_o, norm_scale(middle_o), gain_m, grad_normal_m)
@@ -987,7 +1001,7 @@
         seqs,
         slow,
         (w_qkv, 2, w_qkv, tail_at, 1, gains),
-        (x_own, logits),
+        (picked[0], logits),
         cols=heads_width,
         at_b=2,
     )
@@ -1004,7 +1018,11 @@
     down_sum = lax.ppermute(
         down_part,
         ("seq", "fsdp"),
-        [(s * fsdps + f, f * seqs + s) for s in range(seqs) for f in range(fsdps)],
+        [
+            (s * fsdps + down_slot(f, fsdps, seqs), f * seqs + s)
+            for s in range(seqs)
+            for f in range(fsdps)
+        ],
     ).astype(F32)
     qkv_part = jnp.concatenate(
         [q_part[:, :, :heads_width], kv_part, q_part[:, :, heads_width:]], axis=2

time: 289 us -> 279 us (0.965)
  starting transfers between devices: 46.8 us -> 38.6 us
    ppermute x41 -> x38, starting transfers between devices: 43.5 us -> 35.1 us  [flip(): return lax.ppermute(values, axis, [(j, j ^ bit) for j in range(count)])]
    pallas_call x2 -> x1, Pallas kernels: 4.98 us -> 6 us  [pick_rows(): pl.pallas_call(pick_rows_kernel, grid=(length // ROW_TILE,), in_specs=[pl...]
    ppermute x41 -> x38, waiting for transfers between devices: 87.4 us -> 86.7 us  [flip(): return lax.ppermute(values, axis, [(j, j ^ bit) for j in range(count)])]
    unnamed x123 -> x101, local copies, waits for them, and re-layouts: 15.9 us -> 15.5 us
  transfers between devices with their start and end apart: 44 -> 41, of which waited for: 17 -> 17; matrix products, arithmetic and copies ran while one was open for 12% -> 11% of each run, Pallas kernels for 24% -> 26%
where the time goes in v4:
time: 279 us; the launch traced here: 278 us
  waiting for transfers between devices  92.2 us (33%)
  Pallas kernels  71.8 us (26%)
  starting transfers between devices  38.6 us (14%)
  local copies, waits for them, and re-layouts  25.1 us (9%)
  matrix products  19.4 us (7%)
  other arithmetic  15.8 us (6%)
  between operations  14.9 us (5%)
    ppermute x38, waiting for transfers between devices, flip(): return lax.ppermute(values, axis, [(j, j ^ bit) for j in range(count)])  86.7 us
    ppermute x38, starting transfers between devices, flip(): return lax.ppermute(values, axis, [(j, j ^ bit) for j in range(count)])  35.1 us
    dot_general x14, matrix products, mm(): return lax.dot_general(a, b, (dims, ((), ())), preferred_element_type=F32)  19.4 us
    unnamed x101, local copies, waits for them, and re-layouts  15.5 us
    pallas_call x3, Pallas kernels, one_step(): pl.pallas_call(kernel, grid_spec=pltpu.PrefetchScalarGridSpec(num_scalar_...  15.3 us
    pallas_call x1, Pallas kernels, hidden_grads(): pl.pallas_call(partial(hidden_grads_kernel, per=total // (seqs * fsdps),...  11.3 us
    pallas_call x3, Pallas kernels, weight_grad(): pl.pallas_call(partial(weight_grad_kernel, per=per, fsdps=fsdps, seqs=lax...  11 us
    pallas_call x1, Pallas kernels, attention_backward(): pl.pallas_call(attention_backward_kernel, grid_spec=pltpu.PrefetchScalarG...  8.46 us
  transfers between devices with their start and end apart: 41, of which 17 were waited for; matrix products, arithmetic and copies ran while one was open for 11% of the time, Pallas kernels for 26%

profile of v4, /device:TPU:1, one launch (start us, length us, event | category | flops | bytes accessed | tf_op | source)
XLA Modules:
  0.0 277.8 jit_solution(1421564502251024348)
XLA Ops:
  11.5 4.2 %collective-permute-start.4 = (bf16[128,1152]{1,0:T(8,128)(2,1)S(1)}, bf16[128,1152]{1,0:T(8,128)(2,1)S(1)}, u32[]{:S(2)}, u32[]{:S(2)}) collective-permute-start(bf16[128,1152]{1,0:T(8,128)(2,1)S(1)} %first_shard.1), channel_id=1, source_target_pairs={{0,6},{1,7},{2,4},{3,5},{4,2},{5,3},{6,0},{7,1},{8,14},{9,15},{10,... | collective-permute-start | bytes 884744 | tf_op jit(solution)/shard_map/ppermute | solution.py:33
  17.5 2.2 copy-done.1
  19.7 6.0 %pick_rows.1.refs_0_ = bf16[2,256,1024]{2,1,0:T(8,128)(2,1)S(1)} custom-call(s32[256,1]{1,0:T(8,128)S(1)} %copy.49.ids_ref, bf16[2048,1024]{1,0:T(8,128)(2,1)S(1)} %bitcast.97, bf16[2048,1024]{1,0:T(8,128)(2,1)} %bitcast.99), custom_call_target="tpu_custom_call" | custom-call | flops 2147483648 | bytes 8388608 | tf_op jit(solution)/shard_map/pick_rows/pallas_call | solution.py:396
  25.7 3.3 %hidden_shard.1 = bf16[256,1024]{1,0:T(8,128)(2,1)} custom-call(s32[2]{0:T(128)S(1)} %get-tuple-element.111.place_ref, bf16[128,4096]{1,0:T(8,128)(2,1)S(1)} %copy-done.21, bf16[512,1024]{1,0:T(8,128)(2,1)S(1)} %copy-done.22), custom_call_target="tpu_custom_call" | custom-call | bytes 1048576 | tf_op jit(solution)/shard_map/hidden_shard/pallas_call | solution.py:712
  29.0 11.4 %collective-permute-done.3 = bf16[128,1152]{1,0:T(8,128)(2,1)S(1)} collective-permute-done((bf16[128,1152]{1,0:T(8,128)(2,1)S(1)}, bf16[128,1152]{1,0:T(8,128)(2,1)S(1)}, u32[]{:S(2)}, u32[]{:S(2)}) %collective-permute-start.3) | collective-permute-done | bytes 294944 | tf_op jit(solution)/shard_map/ppermute | solution.py:33
  45.1 18.8 %collective-permute-done.1.refs_2_ = bf16[2,256,1024]{2,1,0:T(8,128)(2,1)S(1)} collective-permute-done((bf16[2,256,1024]{2,1,0:T(8,128)(2,1)S(1)}, bf16[2,256,1024]{2,1,0:T(8,128)(2,1)S(1)}, u32[]{:S(2)}, u32[]{:S(2)}) %collective-permute-start.1) | collective-permute-done | bytes 1048608 | tf_op jit(solution)/shard_map/ppermute | solution.py:33
  64.0 3.1 %collective-permute-done.6.refs_7_ = bf16[3,128,1152]{2,1,0:T(8,128)(2,1)S(1)} collective-permute-done((bf16[3,128,1152]{2,1,0:T(8,128)(2,1)S(1)}, bf16[3,128,1152]{2,1,0:T(8,128)(2,1)S(1)}, u32[]{:S(2)}, u32[]{:S(2)}) %collective-permute-start.6) | collective-permute-done | bytes 884768 | tf_op jit(solution)/shard_map/ppermute | solution.py:33
  67.1 2.6 collective-permute-start.7
  69.7 2.2 collective-permute-done.7.refs_3_
  73.0 6.1 %project.1 = (bf16[8,32,1024]{2,1,0:T(8,128)(2,1)}, bf16[1024,896]{1,0:T(8,128)(2,1)}, f32[8,1024]{1,0:T(8,128)S(1)}, bf16[1024,1024]{1,0:T(8,128)(2,1)}, bf16[1...) custom-call(s32[2]{0:T(128)S(1)} %get-tuple-element.111.place_ref, ...), custom_call_target="tpu_custom_call" | custom-call | flops 1879048192 | bytes 12619776 | tf_op jit(solution)/shard_map/project/pallas_call | solution.py:645
  84.5 6.3 %attention_forward.1 = (bf16[1024,256]{1,0:T(8,128)(2,1)S(1)}, f32[8,1024]{1,0:T(8,128)S(1)}) custom-call(s32[4]{0:T(128)S(1)} %get-tuple-element.141.window_ref, s32[4]{0:T(128)S(1)} %scatter_custom_fusion.place_ref, s32[4]{0:T(128)S(1)} %get-tuple-element.140.first_ref, bf16[1024,256]{1,0:T(8,128)(2,1)S(1)} %copy-done.26, ...), custom_call_target="tpu_custom_call" | custom-call | flops 536870912 | bytes 2097152 | tf_op jit(solution)/shard_map/attention_forward/pallas_call | solution.py:576
  90.9 3.2 %collective-permute-done.11.refs_2_ = bf16[8,32,1024]{2,1,0:T(8,128)(2,1)} collective-permute-done((bf16[8,32,1024]{2,1,0:T(8,128)(2,1)}, bf16[8,32,1024]{2,1,0:T(8,128)(2,1)}, u32[]{:S(2)}, u32[]{:S(2)}) %collective-permute-start.11) | collective-permute-done | bytes 524320 | tf_op jit(solution)/shard_map/ppermute | solution.py:33
  100.3 8.6 %collective-permute-done.9.refs_6_ = bf16[1024,256]{1,0:T(8,128)(2,1)S(1)} collective-permute-done((bf16[1024,256]{1,0:T(8,128)(2,1)S(1)}, bf16[1024,256]{1,0:T(8,128)(2,1)S(1)}, u32[]{:S(2)}, u32[]{:S(2)}) %collective-permute-start.9) | collective-permute-done | bytes 524320 | tf_op jit(solution)/shard_map/ppermute | solution.py:33
  111.2 7.9 %attention_branch.1 = (f32[256,1024]{1,0:T(8,128)S(1)}, bf16[1024,1024]{1,0:T(8,128)(2,1)}, bf16[1024,1024]{1,0:T(8,128)(2,1)}) custom-call(s32[2]{0:T(128)S(1)} %get-tuple-element.111.place_ref, bf16[2,256,1024]{2,1,0:T(8,128)(2,1)S(1)} %pick_rows.1.refs_0_, bf16[2,256,1024]{2,1,0:T(8,128)(2,1)S(1)} %copy-done.20, bf16[2,256,1024]{2,1,0:T(8,128)(2,1)} %copy-done.42, ...), custom_call_target="tpu_custom_call" | custom-call | flops 2147483648 | bytes 13668352 | tf_op jit(solution)/shard_map/attention_branch/pallas_call | solution.py:645
  120.1 3.0 %fusion.58 = (bf16[8,128,1024]{2,1,0:T(8,128)(2,1)S(1)}, bf16[8,128,1024]{2,1,0:T(8,128)(2,1)S(1)}) fusion(bf16[8,256,1024]{2,1,0:T(8,128)(2,1)} %bitcast.130), kind=kLoop, calls=%fused_computation.133 | loop fusion | bytes 8388608 | tf_op jit(solution)/shard_map/slice | solution.py:909
  123.1 2.9 %multiply_convert_fusion = (bf16[1024,1024]{1,0:T(8,128)(2,1)S(1)}, f32[1024,1024]{1,0:T(8,128)S(1)}) fusion(bf16[1024,1024]{1,0:T(8,128)(2,1)S(1)} %copy-done.48, bf16[1024,1024]{1,0:T(8,128)(2,1)S(1)} %bitcast.123), kind=kOutput, calls=%fused_computation.9 | convolution fusion | flops 2152726528 | bytes 10485760 | tf_op jit(solution)/shard_map/dot_general | solution.py:23
  126.2 3.6 %fusion.5.pre_ref = bf16[1024,1024]{1,0:T(8,128)(2,1)S(1)} fusion(f32[1024,1024]{1,0:T(8,128)S(1)} %get-tuple-element.136, bf16[1024,1024]{1,0:T(8,128)(2,1)S(1)} %copy-done.49, bf16[1024,1024]{1,0:T(8,128)(2,1)S(1)} %bitcast.118), kind=kOutput, calls=%fused_computation.8 | convolution fusion | flops 2157969408 | bytes 10485760 | tf_op jit(solution)/shard_map/dot_general | solution.py:23
  136.3 11.3 %hidden_grads.1 = (bf16[8,2,128,1024]{3,2,1,0:T(8,128)(2,1)}, f32[1024,128]{1,0:T(8,128)S(1)}) custom-call(s32[2]{0:T(128)S(1)} %get-tuple-element.111.place_ref, bf16[1024,1024]{1,0:T(8,128)(2,1)S(1)} %get-tuple-element.77.act_ref, bf16[1024,1024]{1,0:T(8,128)(2,1)} %get-tuple-element.72.carried_ref, bf16[1024,1024]{1,0:T(8,128)(2,1)} %get-tuple-element.70.norm_ref, ...), custom_call_target="tpu_custom_call" | custom-call | flops 4294967296 | bytes 12582912 | tf_op jit(solution)/shard_map/hidden_grads/pallas_call | solution.py:309
  158.1 9.6 %collective-permute-done.20.refs_2_ = bf16[256,1024]{1,0:T(8,128)(2,1)S(1)} collective-permute-done((bf16[256,1024]{1,0:T(8,128)(2,1)S(1)}, bf16[256,1024]{1,0:T(8,128)(2,1)S(1)}, u32[]{:S(2)}, u32[]{:S(2)}) %collective-permute-start.20) | collective-permute-done | bytes 524320 | tf_op jit(solution)/shard_map/ppermute | solution.py:33
  175.3 8.5 %attention_backward.1 = bf16[4,256,768]{2,1,0:T(8,128)(2,1)S(1)} custom-call(s32[4]{0:T(128)S(1)} %get-tuple-element.141.window_ref, s32[4]{0:T(128)S(1)} %scatter_custom_fusion.place_ref, s32[4]{0:T(128)S(1)} %get-tuple-element.140.first_ref, bf16[1024,256]{1,0:T(8,128)(2,1)S(1)} %copy-done.27, bf16[4,256,512]{2,1,0:T(8,128)(2,1)S(1)} %bitcast.110, ...), custom_call_target="tpu_custom_call" | custom-call | flops 1342177280 | bytes 3670016 | tf_op jit(solution)/shard_map/attention_backward/pallas_call | solution.py:607
  183.8 5.6 %weight_grad.4 = (bf16[4,4,32,512]{3,2,1,0:T(8,128)(2,1)}, bf16[4,4,32,512]{3,2,1,0:T(8,128)(2,1)S(1)}, f32[1024,128]{1,0:T(8,128)S(1)}) custom-call(s32[2]{0:T(128)S(1)} %get-tuple-element.111.place_ref, bf16[1024,1024]{1,0:T(8,128)(2,1)} %get-tuple-element.88.a_ref, bf16[1024,768]{1,0:T(8,128)(2,1)S(1)} %bitcast.101, bf16[1024,896]{1,0:T(8,128)(2,1)S(1)} %copy-done, ...), custom_call_target="tpu_custom_call" | custom-call | flops 1073741824 | bytes 4194304 | tf_op jit(solution)/shard_map/weight_grad/pallas_call | solution.py:249
  197.4 4.0 %weight_grad.5 = (bf16[4,4,32,384]{3,2,1,0:T(8,128)(2,1)S(1)}, bf16[4,4,32,384]{3,2,1,0:T(8,128)(2,1)S(1)}) custom-call(s32[2]{0:T(128)S(1)} %get-tuple-element.111.place_ref, bf16[1024,1024]{1,0:T(8,128)(2,1)} %get-tuple-element.88.a_ref, bf16[1024,768]{1,0:T(8,128)(2,1)S(1)} %bitcast.102, bf16[1024,896]{1,0:T(8,128)(2,1)S(1)} %copy-done, ...), custom_call_target="tpu_custom_call" | custom-call | flops 536870912 | bytes 3407872 | tf_op jit(solution)/shard_map/weight_grad/pallas_call | solution.py:249
  205.9 2.3 collective-permute-done.29
  211.7 2.1 collective-permute-done.36
  215.1 3.3 %place_rows.2 = bf16[2048,1024]{1,0:T(8,128)(2,1)} custom-call(s32[1,256]{1,0:T(1,128)S(1)} %fusion.72.ids_ref, bf16[256,1024]{1,0:T(8,128)(2,1)S(1)} %get-tuple-element.91.new_ref, bf16[2048,1024]{1,0:T(8,128)(2,1)S(1)} %bitcast.98), custom_call_target="tpu_custom_call" | custom-call | flops 1073741824 | bytes 8388608 | tf_op jit(solution)/shard_map/place_rows/pallas_call | solution.py:427
  220.2 2.4 collective-permute-start.31
  224.9 7.7 %collective-permute-done.27 = bf16[2,4,32,384]{3,2,1,0:T(8,128)(2,1)S(1)} collective-permute-done((bf16[2,4,32,384]{3,2,1,0:T(8,128)(2,1)S(1)}, bf16[2,4,32,384]{3,2,1,0:T(8,128)(2,1)S(1)}, u32[]{:S(2)}, u32[]{:S(2)}) %collective-permute-start.27) | collective-permute-done | bytes 196640 | tf_op jit(solution)/shard_map/ppermute | solution.py:33
  233.5 11.5 %collective-permute-done.28 = bf16[1,4,32,384]{3,2,1,0:T(8,128)(2,1)S(1)} collective-permute-done((bf16[1,4,32,384]{3,2,1,0:T(8,128)(2,1)S(1)}, bf16[1,4,32,384]{3,2,1,0:T(8,128)(2,1)S(1)}, u32[]{:S(2)}, u32[]{:S(2)}) %collective-permute-start.28) | collective-permute-done | bytes 98336 | tf_op jit(solution)/shard_map/ppermute | solution.py:33
  246.8 5.4 %reduce-scatter.2.cloned.1.call-done = bf16[1,2,128,1024]{3,2,1,0:T(8,128)(2,1)} async-done(((bf16[8,2,128,1024]{3,2,1,0:T(8,128)(2,1)}), bf16[1,2,128,1024]{3,2,1,0:T(8,128)(2,1)}) %reduce-scatter.2.cloned.1.call-update) | async-done | bytes 524304 | tf_op jit(solution)/shard_map/reduce_scatter | solution.py:944
  253.3 3.4 %collective-permute-start.38 = (bf16[128,1024]{1,0:T(8,128)(2,1)S(1)}, bf16[128,1024]{1,0:T(8,128)(2,1)S(1)}, u32[]{:S(2)}, u32[]{:S(2)}) collective-permute-start(bf16[128,1024]{1,0:T(8,128)(2,1)S(1)} %get-tuple-element.120), channel_id=1, source_target_pairs={{0,0},{4,4},{1,8},{5,12},{2,16},{6,20},{3,24},{7,28},{8,1},{12,5},... | collective-permute-start | bytes 786440 | tf_op jit(solution)/shard_map/ppermute | solution.py:1018
  262.4 3.3 %place_rows.3 = bf16[2048,1024]{1,0:T(8,128)(2,1)} custom-call(s32[1,256]{1,0:T(1,128)S(1)} %fusion.72.ids_ref, bf16[256,1024]{1,0:T(8,128)(2,1)S(1)} %fusion.14.new_ref, bf16[2048,1024]{1,0:T(8,128)(2,1)S(1)} %bitcast.100), custom_call_target="tpu_custom_call" | custom-call | flops 1073741824 | bytes 8388608 | tf_op jit(solution)/shard_map/place_rows/pallas_call | solution.py:427
  265.7 2.6 collective-permute-done.33.refs_2_
  (246 shorter events, 84.5 us)
Async XLA Ops:
  7.2 112.9 %all-gather.3.cloned.1.call-start = ((), (), s32[]{:S(2)}) async-start(), calls=%async_computation.2 | async-start | bytes 4718592 | tf_op jit(solution)/shard_map/all_gather | solution.py:908
  11.5 17.5 %collective-permute-start.4 = (bf16[128,1152]{1,0:T(8,128)(2,1)S(1)}, bf16[128,1152]{1,0:T(8,128)(2,1)S(1)}, u32[]{:S(2)}, u32[]{:S(2)}) collective-permute-start(bf16[128,1152]{1,0:T(8,128)(2,1)S(1)} %first_shard.1), channel_id=1, source_target_pairs={{0,6},{1,7},{2,4},{3,5},{4,2},{5,3},{6,0},{7,1},{8,14},{9,15},{10,... | collective-permute-start | bytes 884744 | tf_op jit(solution)/shard_map/ppermute | solution.py:33
  15.7 24.7 %collective-permute-start.3 = (bf16[128,1152]{1,0:T(8,128)(2,1)S(1)}, bf16[128,1152]{1,0:T(8,128)(2,1)S(1)}, u32[]{:S(2)}, u32[]{:S(2)}) collective-permute-start(bf16[128,1152]{1,0:T(8,128)(2,1)S(1)} %first_shard.1), channel_id=1, source_target_pairs={{0,4},{1,5},{2,6},{3,7},{4,0},{5,1},{6,2},{7,3},{8,12},{9,13},{10,... | collective-permute-start | bytes 884744 | tf_op jit(solution)/shard_map/ppermute | solution.py:33
  15.7 24.7 %collective-permute-start.2 = (bf16[128,1152]{1,0:T(8,128)(2,1)S(1)}, bf16[128,1152]{1,0:T(8,128)(2,1)S(1)}, u32[]{:S(2)}, u32[]{:S(2)}) collective-permute-start(bf16[128,1152]{1,0:T(8,128)(2,1)S(1)} %first_shard.1), channel_id=1, source_target_pairs={{0,2},{1,3},{2,0},{3,1},{4,6},{5,7},{6,4},{7,5},{8,10},{9,11},{10,... | collective-permute-start | bytes 884744 | tf_op jit(solution)/shard_map/ppermute | solution.py:33
  16.1 9.6 %collective-permute-start.5 = (bf16[1,128,1152]{2,1,0:T(8,128)(2,1)S(1)}, bf16[1,128,1152]{2,1,0:T(8,128)(2,1)S(1)}, u32[]{:S(2)}, u32[]{:S(2)}) collective-permute-start(bf16[1,128,1152]{2,1,0:T(8,128)(2,1)S(1)} %bitcast.113), channel_id=1, source_target_pairs={{0,1},{1,0},{2,3},{3,2},{4,5},{5,4},{6,7},{7,6},{8,9},{9,8},{10,11... | collective-permute-start | bytes 884744 | tf_op jit(solution)/shard_map/ppermute | solution.py:33
  40.5 211.8 %reduce-scatter.2.cloned.1.call-start = ((), (), s32[]{:S(2)}) async-start(), calls=%async_computation.1 | async-start | bytes 4718592 | tf_op jit(solution)/shard_map/reduce_scatter | solution.py:944
  40.5 23.5 %collective-permute-start.1 = (bf16[2,256,1024]{2,1,0:T(8,128)(2,1)S(1)}, bf16[2,256,1024]{2,1,0:T(8,128)(2,1)S(1)}, u32[]{:S(2)}, u32[]{:S(2)}) collective-permute-start(bf16[2,256,1024]{2,1,0:T(8,128)(2,1)S(1)} %pick_rows.1.refs_0_), channel_id=1, source_target_pairs={{0,16},{8,24},{16,0},{24,8},{1,17},{9,25},{17,1},{25,9},{2,18},{10... | collective-permute-start | bytes 3145736 | tf_op jit(solution)/shard_map/ppermute | solution.py:33
  41.9 25.2 %collective-permute-start.6 = (bf16[3,128,1152]{2,1,0:T(8,128)(2,1)S(1)}, bf16[3,128,1152]{2,1,0:T(8,128)(2,1)S(1)}, u32[]{:S(2)}, u32[]{:S(2)}) collective-permute-start(bf16[3,128,1152]{2,1,0:T(8,128)(2,1)S(1)} %pad_maximum_fusion.refs_5_), channel_id=1, source_target_pairs={{0,1},{1,0},{2,3},{3,2},{4,5},{5,4},{6,7},{7,6},{8,9},{9,8},{10,11... | collective-permute-start | bytes 2654216 | tf_op jit(solution)/shard_map/ppermute | solution.py:33
  43.2 26.5 %collective-permute-start = (bf16[2,256,1024]{2,1,0:T(8,128)(2,1)S(1)}, bf16[2,256,1024]{2,1,0:T(8,128)(2,1)S(1)}, u32[]{:S(2)}, u32[]{:S(2)}) collective-permute-start(bf16[2,256,1024]{2,1,0:T(8,128)(2,1)S(1)} %pick_rows.1.refs_0_), channel_id=1, source_target_pairs={{0,8},{8,0},{16,24},{24,16},{1,9},{9,1},{17,25},{25,17},{2,10},{10... | collective-permute-start | bytes 3145736 | tf_op jit(solution)/shard_map/ppermute | solution.py:33
  80.7 13.5 %collective-permute-start.11 = (bf16[8,32,1024]{2,1,0:T(8,128)(2,1)}, bf16[8,32,1024]{2,1,0:T(8,128)(2,1)}, u32[]{:S(2)}, u32[]{:S(2)}) collective-permute-start(bf16[8,32,1024]{2,1,0:T(8,128)(2,1)} %get-tuple-element.65.refs_0_), channel_id=1, source_target_pairs={{0,16},{8,24},{16,0},{24,8},{1,17},{9,25},{17,1},{25,9},{2,18},{10... | collective-permute-start | bytes 1572872 | tf_op jit(solution)/shard_map/ppermute | solution.py:33
  82.8 13.2 %collective-permute-start.10 = (bf16[8,32,1024]{2,1,0:T(8,128)(2,1)}, bf16[8,32,1024]{2,1,0:T(8,128)(2,1)S(1)}, u32[]{:S(2)}, u32[]{:S(2)}) collective-permute-start(bf16[8,32,1024]{2,1,0:T(8,128)(2,1)} %get-tuple-element.65.refs_0_), channel_id=1, source_target_pairs={{0,8},{8,0},{16,24},{24,16},{1,9},{9,1},{17,25},{25,17},{2,10},{10... | collective-permute-start | bytes 1572872 | tf_op jit(solution)/shard_map/ppermute | solution.py:33
  95.3 13.6 %collective-permute-start.9 = (bf16[1024,256]{1,0:T(8,128)(2,1)S(1)}, bf16[1024,256]{1,0:T(8,128)(2,1)S(1)}, u32[]{:S(2)}, u32[]{:S(2)}) collective-permute-start(bf16[1024,256]{1,0:T(8,128)(2,1)S(1)} %get-tuple-element.64.refs_4_.a_ref.o_ref), channel_id=1, source_target_pairs={{0,16},{8,24},{16,0},{24,8},{1,17},{9,25},{17,1},{25,9},{2,18},{10... | collective-permute-start | bytes 1572872 | tf_op jit(solution)/shard_map/ppermute | solution.py:33
  95.6 14.2 %collective-permute-start.8 = (bf16[1024,256]{1,0:T(8,128)(2,1)S(1)}, bf16[1024,256]{1,0:T(8,128)(2,1)S(1)}, u32[]{:S(2)}, u32[]{:S(2)}) collective-permute-start(bf16[1024,256]{1,0:T(8,128)(2,1)S(1)} %get-tuple-element.64.refs_4_.a_ref.o_ref), channel_id=1, source_target_pairs={{0,8},{8,0},{16,24},{24,16},{1,9},{9,1},{17,25},{25,17},{2,10},{10... | collective-permute-start | bytes 1572872 | tf_op jit(solution)/shard_map/ppermute | solution.py:33
  132.6 15.9 %collective-permute-start.14 = (bf16[256,1024]{1,0:T(8,128)(2,1)}, bf16[256,1024]{1,0:T(8,128)(2,1)}, u32[]{:S(2)}, u32[]{:S(2)}) collective-permute-start(bf16[256,1024]{1,0:T(8,128)(2,1)} %fusion.28), channel_id=1, source_target_pairs={{0,8},{8,0},{16,24},{24,16},{1,9},{9,1},{17,25},{25,17},{2,10},{10... | collective-permute-start | bytes 1572872 | tf_op jit(solution)/shard_map/ppermute | solution.py:33
  134.3 14.2 %collective-permute-start.16 = (bf16[256,1024]{1,0:T(8,128)(2,1)}, bf16[256,1024]{1,0:T(8,128)(2,1)}, u32[]{:S(2)}, u32[]{:S(2)}) collective-permute-start(bf16[256,1024]{1,0:T(8,128)(2,1)} %add_convert_fusion.1), channel_id=1, source_target_pairs={{0,16},{8,24},{16,0},{24,8},{1,17},{9,25},{17,1},{25,9},{2,18},{10... | collective-permute-start | bytes 1572872 | tf_op jit(solution)/shard_map/ppermute | solution.py:33
  153.9 13.7 %collective-permute-start.20 = (bf16[256,1024]{1,0:T(8,128)(2,1)S(1)}, bf16[256,1024]{1,0:T(8,128)(2,1)S(1)}, u32[]{:S(2)}, u32[]{:S(2)}) collective-permute-start(bf16[256,1024]{1,0:T(8,128)(2,1)S(1)} %fusion.10.refs_0_), channel_id=1, source_target_pairs={{0,16},{8,24},{16,0},{24,8},{1,17},{9,25},{17,1},{25,9},{2,18},{10... | collective-permute-start | bytes 1572872 | tf_op jit(solution)/shard_map/ppermute | solution.py:33
  156.8 34.5 %collective-permute-start.18 = (bf16[256,1024]{1,0:T(8,128)(2,1)}, bf16[256,1024]{1,0:T(8,128)(2,1)S(1)}, u32[]{:S(2)}, u32[]{:S(2)}) collective-permute-start(bf16[256,1024]{1,0:T(8,128)(2,1)} %fusion.36), channel_id=1, source_target_pairs={{0,8},{8,0},{16,24},{24,16},{1,9},{9,1},{17,25},{25,17},{2,10},{10... | collective-permute-start | bytes 1572872 | tf_op jit(solution)/shard_map/ppermute | solution.py:33
  157.8 12.0 %collective-permute-start.19 = (bf16[256,1024]{1,0:T(8,128)(2,1)S(1)}, bf16[256,1024]{1,0:T(8,128)(2,1)S(1)}, u32[]{:S(2)}, u32[]{:S(2)}) collective-permute-start(bf16[256,1024]{1,0:T(8,128)(2,1)S(1)} %fusion.32), channel_id=1, source_target_pairs={{0,8},{8,0},{16,24},{24,16},{1,9},{9,1},{17,25},{25,17},{2,10},{10... | collective-permute-start | bytes 1572872 | tf_op jit(solution)/shard_map/ppermute | solution.py:33
  170.0 21.3 %collective-permute-start.22 = (bf16[256,1024]{1,0:T(8,128)(2,1)S(1)}, bf16[256,1024]{1,0:T(8,128)(2,1)S(1)}, u32[]{:S(2)}, u32[]{:S(2)}) collective-permute-start(bf16[256,1024]{1,0:T(8,128)(2,1)S(1)} %add_convert_fusion), channel_id=1, source_target_pairs={{0,16},{8,24},{16,0},{24,8},{1,17},{9,25},{17,1},{25,9},{2,18},{10... | collective-permute-start | bytes 1572872 | tf_op jit(solution)/shard_map/ppermute | solution.py:33
  174.0 15.7 %collective-permute-start.35 = (bf16[4,1,32,1024]{3,2,1,0:T(8,128)(2,1)S(1)}, bf16[4,1,32,1024]{3,2,1,0:T(8,128)(2,1)S(1)}, u32[]{:S(2)}, u32[]{:S(2)}) collective-permute-start(bf16[4,1,32,1024]{3,2,1,0:T(8,128)(2,1)S(1)} %get-tuple-element.83), channel_id=1, source_target_pairs={{0,1},{1,0},{2,3},{3,2},{4,5},{5,4},{6,7},{7,6},{8,9},{9,8},{10,11... | collective-permute-start | bytes 786440 | tf_op jit(solution)/shard_map/ppermute | solution.py:33
  189.4 18.8 %collective-permute-start.29 = (bf16[4,4,32,512]{3,2,1,0:T(8,128)(2,1)}, bf16[4,4,32,512]{3,2,1,0:T(8,128)(2,1)}, u32[]{:S(2)}, u32[]{:S(2)}) collective-permute-start(bf16[4,4,32,512]{3,2,1,0:T(8,128)(2,1)} %get-tuple-element.87), channel_id=1, source_target_pairs={{0,1},{1,0},{2,3},{3,2},{4,5},{5,4},{6,7},{7,6},{8,9},{9,8},{10,11... | collective-permute-start | bytes 1572872 | tf_op jit(solution)/shard_map/ppermute | solution.py:33
  201.3 21.2 %collective-permute-start.26 = (bf16[4,4,32,384]{3,2,1,0:T(8,128)(2,1)S(1)}, bf16[4,4,32,384]{3,2,1,0:T(8,128)(2,1)S(1)}, u32[]{:S(2)}, u32[]{:S(2)}) collective-permute-start(bf16[4,4,32,384]{3,2,1,0:T(8,128)(2,1)S(1)} %get-tuple-element.90), channel_id=1, source_target_pairs={{0,2},{1,3},{2,0},{3,1},{4,6},{5,7},{6,4},{7,5},{8,10},{9,11},{10,... | collective-permute-start | bytes 1179656 | tf_op jit(solution)/shard_map/ppermute | solution.py:33
  201.4 12.3 %collective-permute-start.36 = (bf16[2,1,32,1024]{3,2,1,0:T(8,128)(2,1)S(1)}, bf16[2,1,32,1024]{3,2,1,0:T(8,128)(2,1)S(1)}, u32[]{:S(2)}, u32[]{:S(2)}) collective-permute-start(bf16[2,1,32,1024]{3,2,1,0:T(8,128)(2,1)S(1)} %copy-done.45), channel_id=1, source_target_pairs={{0,2},{1,3},{2,0},{3,1},{4,6},{5,7},{6,4},{7,5},{8,10},{9,11},{10,... | collective-permute-start | bytes 393224 | tf_op jit(solution)/shard_map/ppermute | solution.py:33
  203.5 41.5 %collective-permute-start.23 = (bf16[256,1024]{1,0:T(8,128)(2,1)S(1)}, bf16[256,1024]{1,0:T(8,128)(2,1)S(1)}, u32[]{:S(2)}, u32[]{:S(2)}) collective-permute-start(bf16[256,1024]{1,0:T(8,128)(2,1)S(1)} %convolution_convert_fusion.1), channel_id=1, source_target_pairs={{0,8},{8,0},{16,24},{24,16},{1,9},{9,1},{17,25},{25,17},{2,10},{10... | collective-permute-start | bytes 1572872 | tf_op jit(solution)/shard_map/ppermute | solution.py:33
  205.8 18.2 %collective-permute-start.24 = (bf16[256,1024]{1,0:T(8,128)(2,1)S(1)}, bf16[256,1024]{1,0:T(8,128)(2,1)S(1)}, u32[]{:S(2)}, u32[]{:S(2)}) collective-permute-start(bf16[256,1024]{1,0:T(8,128)(2,1)S(1)} %convolution_convert_fusion), channel_id=1, source_target_pairs={{0,8},{8,0},{16,24},{24,16},{1,9},{9,1},{17,25},{25,17},{2,10},{10... | collective-permute-start | bytes 1572872 | tf_op jit(solution)/shard_map/ppermute | solution.py:33
  209.7 10.4 %collective-permute-start.30 = (bf16[2,4,32,512]{3,2,1,0:T(8,128)(2,1)S(1)}, bf16[2,4,32,512]{3,2,1,0:T(8,128)(2,1)S(1)}, u32[]{:S(2)}, u32[]{:S(2)}) collective-permute-start(bf16[2,4,32,512]{3,2,1,0:T(8,128)(2,1)S(1)} %slice.192), channel_id=1, source_target_pairs={{0,2},{1,3},{2,0},{3,1},{4,6},{5,7},{6,4},{7,5},{8,10},{9,11},{10,... | collective-permute-start | bytes 786440 | tf_op jit(solution)/shard_map/ppermute | solution.py:33
  220.2 12.6 %collective-permute-start.31 = (bf16[1,4,32,512]{3,2,1,0:T(8,128)(2,1)S(1)}, bf16[1,4,32,512]{3,2,1,0:T(8,128)(2,1)S(1)}, u32[]{:S(2)}, u32[]{:S(2)}) collective-permute-start(bf16[1,4,32,512]{3,2,1,0:T(8,128)(2,1)S(1)} %slice.330), channel_id=1, source_target_pairs={{0,4},{1,5},{2,6},{3,7},{4,0},{5,1},{6,2},{7,3},{8,12},{9,13},{10,... | collective-permute-start | bytes 393224 | tf_op jit(solution)/shard_map/ppermute | solution.py:33
  222.7 9.9 %collective-permute-start.27 = (bf16[2,4,32,384]{3,2,1,0:T(8,128)(2,1)S(1)}, bf16[2,4,32,384]{3,2,1,0:T(8,128)(2,1)S(1)}, u32[]{:S(2)}, u32[]{:S(2)}) collective-permute-start(bf16[2,4,32,384]{3,2,1,0:T(8,128)(2,1)S(1)} %slice.187), channel_id=1, source_target_pairs={{0,1},{1,0},{2,3},{3,2},{4,5},{5,4},{6,7},{7,6},{8,9},{9,8},{10,11... | collective-permute-start | bytes 589832 | tf_op jit(solution)/shard_map/ppermute | solution.py:33
  224.7 20.4 %collective-permute-start.25 = (bf16[256,1024]{1,0:T(8,128)(2,1)S(1)}, bf16[256,1024]{1,0:T(8,128)(2,1)S(1)}, u32[]{:S(2)}, u32[]{:S(2)}) collective-permute-start(bf16[256,1024]{1,0:T(8,128)(2,1)S(1)} %fusion.8), channel_id=1, source_target_pairs={{0,16},{8,24},{16,0},{24,8},{1,17},{9,25},{17,1},{25,9},{2,18},{10... | collective-permute-start | bytes 1572872 | tf_op jit(solution)/shard_map/ppermute | solution.py:33
  232.7 12.2 %collective-permute-start.28 = (bf16[1,4,32,384]{3,2,1,0:T(8,128)(2,1)S(1)}, bf16[1,4,32,384]{3,2,1,0:T(8,128)(2,1)S(1)}, u32[]{:S(2)}, u32[]{:S(2)}) collective-permute-start(bf16[1,4,32,384]{3,2,1,0:T(8,128)(2,1)S(1)} %slice.331), channel_id=1, source_target_pairs={{0,4},{1,5},{2,6},{3,7},{4,0},{5,1},{6,2},{7,3},{8,12},{9,13},{10,... | collective-permute-start | bytes 294920 | tf_op jit(solution)/shard_map/ppermute | solution.py:33
  253.3 16.8 %collective-permute-start.38 = (bf16[128,1024]{1,0:T(8,128)(2,1)S(1)}, bf16[128,1024]{1,0:T(8,128)(2,1)S(1)}, u32[]{:S(2)}, u32[]{:S(2)}) collective-permute-start(bf16[128,1024]{1,0:T(8,128)(2,1)S(1)} %get-tuple-element.120), channel_id=1, source_target_pairs={{0,0},{4,4},{1,8},{5,12},{2,16},{6,20},{3,24},{7,28},{8,1},{12,5},... | collective-permute-start | bytes 786440 | tf_op jit(solution)/shard_map/ppermute | solution.py:1018
  258.1 10.2 %collective-permute-start.33 = (bf16[32,1920]{1,0:T(8,128)(2,1)S(1)}, bf16[32,1920]{1,0:T(8,128)(2,1)S(1)}, u32[]{:S(2)}, u32[]{:S(2)}) collective-permute-start(bf16[32,1920]{1,0:T(8,128)(2,1)S(1)} %get-tuple-element.125), channel_id=1, source_target_pairs={{0,16},{8,24},{16,0},{24,8},{1,17},{9,25},{17,1},{25,9},{2,18},{10... | collective-permute-start | bytes 368648 | tf_op jit(solution)/shard_map/ppermute | solution.py:33
  (59 other events, 304.2 us)
Sparse Core Ops, SparseCore 0:
  40.6 76.1 all-gather.2
  148.6 103.5 reduce-scatter.1

commit v5 on v4

--- a/solution.py
+++ b/solution.py
@@ -17,6 +17,7 @@
 BF16 = jnp.bfloat16
 F32 = jnp.float32
 VMEM_LIMIT = 48 * 1024 * 1024
+GRAD_LIMIT = 28 * 1024 * 1024
 
 
 def mm(a, b, dims):
@@ -264,7 +265,7 @@
             out_specs=out_specs,
         ),
         out_shape=out_shape,
-        compiler_params=pltpu.CompilerParams(vmem_limit_bytes=VMEM_LIMIT),
+        compiler_params=pltpu.CompilerParams(vmem_limit_bytes=GRAD_LIMIT),
         cost_estimate=pl.CostEstimate(
             flops=2 * rows * total * cols,
             transcendentals=0,
@@ -322,7 +323,7 @@
             out_specs=[whole(*both), lines(LANES)],
         ),
         out_shape=[jax.ShapeDtypeStruct(both, BF16), jax.ShapeDtypeStruct((total, LANES), F32)],
-        compiler_params=pltpu.CompilerParams(vmem_limit_bytes=VMEM_LIMIT),
+        compiler_params=pltpu.CompilerParams(vmem_limit_bytes=GRAD_LIMIT),
         cost_estimate=pl.CostEstimate(
             flops=4 * rows * total * cols,
             transcendentals=0,
@@ -663,22 +664,23 @@
     return lax.rsqrt(jnp.mean(values * values, axis=1, keepdims=True) + EPS)
 
 
-def first_shard_kernel(place_ref, q_ref, k_ref, v_ref, tails_ref, out_ref, own_ref):
-    span = q_ref.shape[1]
+def first_shard_kernel(place_ref, q_ref, k_ref, v_ref, vec_ref, out_ref, own_ref):
+    rows, span = q_ref.shape
     for i, ref in enumerate((k_ref, v_ref, q_ref)):
-        own_ref[:, i * span : (i + 1) * span] = ref[...]
-    own_ref[:, 3 * span : 3 * span + LANES] = tails_ref[...]
+        own_ref[:rows, i * span : (i + 1) * span] = ref[...]
     lines = out_ref.shape[1]
     for j in range(out_ref.shape[2] // span):
-        own_ref[j * lines : (j + 1) * lines, 3 * span + LANES :] = out_ref[0, :, j * span : (j + 1) * span]
-
-
-def first_shard(place, qkv, tails, out, span):
+        own_ref[j * lines : (j + 1) * lines, 3 * span :] = out_ref[0, :, j * span : (j + 1) * span]
+    own_ref[rows:, :] = jnp.zeros((own_ref.shape[0] - rows, own_ref.shape[1]), BF16)
+    own_ref[rows:, : vec_ref.shape[1]] = vec_ref[...]
+
+
+def first_shard(place, qkv, vectors, out, span):
     rows, width = out.shape
     seqs = width // span
     out = out.reshape(seqs, rows // seqs, width)
     heads = lambda i: pl.BlockSpec((rows, span), lambda g, at: (0, i * seqs + at[1]))
-    cols = 4 * span + LANES
+    shape = (rows + vectors.shape[0], 4 * span)
     return pl.pallas_call(
         first_shard_kernel,
         grid_spec=pltpu.PrefetchScalarGridSpec(
@@ -688,16 +690,18 @@
                 heads(0),
                 heads(1),
                 heads(2),
-                pl.BlockSpec((rows, LANES), lambda g, at: (0, 0)),
+                pl.BlockSpec(vectors.shape, lambda g, at: (0, 0)),
                 pl.BlockSpec((1, rows // seqs, width), lambda g, at: (at[1], 0, 0)),
             ],
-            out_specs=pl.BlockSpec((rows, cols), lambda g, at: (0, 0)),
-        ),
-        out_shape=jax.ShapeDtypeStruct((rows, cols), BF16),
+            out_specs=pl.BlockSpec(shape, lambda g, at: (0, 0)),
+        ),
+        out_shape=jax.ShapeDtypeStruct(shape, BF16),
         compiler_params=pltpu.CompilerParams(vmem_limit_bytes=VMEM_LIMIT),
-        cost_estimate=pl.CostEstimate(flops=0, transcendentals=0, bytes_accessed=4 * rows * cols),
+        cost_estimate=pl.CostEstimate(
+            flops=0, transcendentals=0, bytes_accessed=4 * shape[0] * shape[1]
+        ),
         name="first_shard",
-    )(place, qkv, qkv, qkv, tails, out)
+    )(place, qkv, qkv, qkv, vectors, out)
 
 
 def hidden_shard_kernel(place_ref, up_ref, down_ref, both_ref):
@@ -730,17 +734,21 @@
 def project_kernel(place_ref, *refs, seqs, slow, fast):
     x_refs, pieces = refs[:seqs], refs[seqs:-7]
     out_ref, w_ref, vec_ref, normal_ref, q_ref, kv_ref, rate_ref = refs[-7:]
-    per, cols = pieces[0].shape[1], w_ref.shape[1]
     span = q_ref.shape[1]
+    per = w_ref.shape[0] // (slow * fast)
     lines = out_ref.shape[1]
     done = 0
     for ref in pieces:
         for i in range(ref.shape[0]):
             block = done % slow * fast + done // slow
             shard = place_ref[0] ^ block
-            w_ref[pl.ds(pl.multiple_of(shard * per, per), per), :] = ref[i, :, :cols]
+            here = pl.ds(pl.multiple_of(shard * per, per), per)
+            w_ref[here, : 3 * span] = ref[i, :per, : 3 * span]
+            extra = ref[i, per:, :LANES].astype(F32)
+            square = jnp.concatenate([extra, jnp.zeros((LANES - extra.shape[0], LANES), F32)], axis=0)
+            w_ref[here, 3 * span :] = square.T[:per].astype(BF16)
             for j in range(seqs):
-                out_ref[block, :, j * span : (j + 1) * span] = ref[i, j * lines : (j + 1) * lines, cols:]
+                out_ref[block, :, j * span : (j + 1) * span] = ref[i, j * lines : (j + 1) * lines, 3 * span :]
             done += 1
     tails = w_ref[:, 3 * span :]
     vec = tails.astype(F32).T
@@ -764,7 +772,7 @@
     slow, fast = fsdp_sizes()
     _, rows, width = x_blocks[0].shape
     total = rows * len(x_blocks)
-    cols = pieces[0].shape[2] - span
+    cols = 3 * span + LANES
     out_shape = [
         jax.ShapeDtypeStruct((slow * fast, width // (slow * fast * len(x_blocks)), width), BF16),
         jax.ShapeDtypeStruct((width, cols), BF16),
@@ -892,9 +900,9 @@
     grad_in = cotangent[0]
 
     place = jnp.stack([lax.axis_index("fsdp"), me])
-    vectors = jnp.stack([router, attn_gain, mlp_gain], axis=1)
-    tails = jnp.pad(vectors, ((0, 0), (0, LANES - vectors.shape[1])))
-    first_own = first_shard(place, qkv_weight, tails, out_weight, heads_width)
+    vectors = jnp.stack([router, attn_gain, mlp_gain])
+    vectors = jnp.pad(vectors, ((0, 8 - vectors.shape[0]), (0, LANES - vectors.shape[1])))
+    first_own = first_shard(place, qkv_weight, vectors, out_weight, heads_width)
     first_slow = gather_slow(first_own)
     first_got = own_fast(first_slow[0])
     picked = pick_rows([stream_in, grad_in], after(row_ids, first_own))

time: 279 us -> 275 us (0.986)
  Pallas kernels: 71.8 us -> 64.1 us
  local copies, waits for them, and re-layouts: 25.1 us -> 30.1 us
  waiting for transfers between devices: 92.2 us -> 87.8 us
    pallas_call x1, Pallas kernels: 11.3 us -> 6.88 us  [hidden_grads(): pl.pallas_call(partial(hidden_grads_kernel, per=total // (seqs * fsdps),...]
    ppermute x38, starting transfers between devices: 35.1 us -> 38.4 us  [flip(): return lax.ppermute(values, axis, [(j, j ^ bit) for j in range(count)])]
    unnamed x101 -> x113, local copies, waits for them, and re-layouts: 15.5 us -> 18.1 us
  transfers between devices with their start and end apart: 41 -> 41, of which waited for: 17 -> 18; matrix products, arithmetic and copies ran while one was open for 11% -> 12% of each run, Pallas kernels for 26% -> 23%
where the time goes in v5:
time: 275 us; the launch traced here: 273 us
  waiting for transfers between devices  87.8 us (32%)
  Pallas kernels  64.1 us (23%)
  starting transfers between devices  41.2 us (15%)
  local copies, waits for them, and re-layouts  30.1 us (11%)
  matrix products  18.7 us (7%)
  other arithmetic  16.7 us (6%)
  between operations  14.8 us (5%)
    ppermute x38, waiting for transfers between devices, flip(): return lax.ppermute(values, axis, [(j, j ^ bit) for j in range(count)])  84.9 us
    ppermute x38, starting transfers between devices, flip(): return lax.ppermute(values, axis, [(j, j ^ bit) for j in range(count)])  38.4 us
    dot_general x14, matrix products, mm(): return lax.dot_general(a, b, (dims, ((), ())), preferred_element_type=F32)  18.7 us
    unnamed x113, local copies, waits for them, and re-layouts  18.1 us
    pallas_call x3, Pallas kernels, one_step(): pl.pallas_call(kernel, grid_spec=pltpu.PrefetchScalarGridSpec(num_scalar_...  15.3 us
    pallas_call x3, Pallas kernels, weight_grad(): pl.pallas_call(partial(weight_grad_kernel, per=per, fsdps=fsdps, seqs=lax...  9.18 us
    pallas_call x1, Pallas kernels, attention_backward(): pl.pallas_call(attention_backward_kernel, grid_spec=pltpu.PrefetchScalarG...  7.62 us
    pallas_call x1, Pallas kernels, hidden_grads(): pl.pallas_call(partial(hidden_grads_kernel, per=total // (seqs * fsdps),...  6.88 us
  transfers between devices with their start and end apart: 41, of which 18 were waited for; matrix products, arithmetic and copies ran while one was open for 12% of the time, Pallas kernels for 23%

profile of v5, /device:TPU:1, one launch (start us, length us, event | category | flops | bytes accessed | tf_op | source)
XLA Modules:
  0.0 273.4 jit_solution(7521310436220075400)
XLA Ops:
  11.3 4.2 %collective-permute-start.4 = (bf16[136,1024]{1,0:T(8,128)(2,1)S(1)}, bf16[136,1024]{1,0:T(8,128)(2,1)S(1)}, u32[]{:S(2)}, u32[]{:S(2)}) collective-permute-start(bf16[136,1024]{1,0:T(8,128)(2,1)S(1)} %first_shard.1), channel_id=1, source_target_pairs={{0,6},{1,7},{2,4},{3,5},{4,2},{5,3},{6,0},{7,1},{8,14},{9,15},{10,... | collective-permute-start | bytes 835592 | tf_op jit(solution)/shard_map/ppermute | solution.py:34
  17.3 2.2 copy-done.1
  19.5 6.0 %pick_rows.1.refs_0_ = bf16[2,256,1024]{2,1,0:T(8,128)(2,1)S(1)} custom-call(s32[256,1]{1,0:T(8,128)S(1)} %copy.33.ids_ref, bf16[2048,1024]{1,0:T(8,128)(2,1)S(1)} %bitcast.97, bf16[2048,1024]{1,0:T(8,128)(2,1)} %bitcast.99), custom_call_target="tpu_custom_call" | custom-call | flops 2147483648 | bytes 8388608 | tf_op jit(solution)/shard_map/pick_rows/pallas_call | solution.py:397
  25.6 3.3 %hidden_shard.1 = bf16[256,1024]{1,0:T(8,128)(2,1)} custom-call(s32[2]{0:T(128)S(1)} %get-tuple-element.111.place_ref, bf16[128,4096]{1,0:T(8,128)(2,1)S(1)} %copy-done.24, bf16[512,1024]{1,0:T(8,128)(2,1)S(1)} %copy-done.25), custom_call_target="tpu_custom_call" | custom-call | bytes 1048576 | tf_op jit(solution)/shard_map/hidden_shard/pallas_call | solution.py:716
  28.9 10.0 %collective-permute-done.3 = bf16[136,1024]{1,0:T(8,128)(2,1)S(1)} collective-permute-done((bf16[136,1024]{1,0:T(8,128)(2,1)S(1)}, bf16[136,1024]{1,0:T(8,128)(2,1)S(1)}, u32[]{:S(2)}, u32[]{:S(2)}) %collective-permute-start.3) | collective-permute-done | bytes 278560 | tf_op jit(solution)/shard_map/ppermute | solution.py:34
  43.5 18.9 %collective-permute-done.1.refs_2_ = bf16[2,256,1024]{2,1,0:T(8,128)(2,1)S(1)} collective-permute-done((bf16[2,256,1024]{2,1,0:T(8,128)(2,1)S(1)}, bf16[2,256,1024]{2,1,0:T(8,128)(2,1)S(1)}, u32[]{:S(2)}, u32[]{:S(2)}) %collective-permute-start.1) | collective-permute-done | bytes 1048608 | tf_op jit(solution)/shard_map/ppermute | solution.py:34
  64.4 2.6 collective-permute-start.7
  67.1 2.2 collective-permute-done.7.refs_3_
  70.3 6.2 %project.1 = (bf16[8,32,1024]{2,1,0:T(8,128)(2,1)}, bf16[1024,896]{1,0:T(8,128)(2,1)}, f32[8,1024]{1,0:T(8,128)S(1)}, bf16[1024,1024]{1,0:T(8,128)(2,1)}, bf16[1...) custom-call(s32[2]{0:T(128)S(1)} %get-tuple-element.111.place_ref, ...), custom_call_target="tpu_custom_call" | custom-call | flops 1879048192 | bytes 12488704 | tf_op jit(solution)/shard_map/project/pallas_call | solution.py:646
  81.9 5.6 %attention_forward.1 = (bf16[1024,256]{1,0:T(8,128)(2,1)S(1)}, f32[8,1024]{1,0:T(8,128)S(1)}) custom-call(s32[4]{0:T(128)S(1)} %get-tuple-element.141.window_ref, s32[4]{0:T(128)S(1)} %scatter_custom_fusion.place_ref, s32[4]{0:T(128)S(1)} %get-tuple-element.140.first_ref, bf16[1024,256]{1,0:T(8,128)(2,1)S(1)} %get-tuple-element.62.q_ref, ...), custom_call_target="tpu_custom_call" | custom-call | flops 536870912 | bytes 2097152 | tf_op jit(solution)/shard_map/attention_forward/pallas_call | solution.py:577
  87.6 3.1 %collective-permute-done.11.refs_2_ = bf16[8,32,1024]{2,1,0:T(8,128)(2,1)} collective-permute-done((bf16[8,32,1024]{2,1,0:T(8,128)(2,1)}, bf16[8,32,1024]{2,1,0:T(8,128)(2,1)}, u32[]{:S(2)}, u32[]{:S(2)}) %collective-permute-start.11) | collective-permute-done | bytes 524320 | tf_op jit(solution)/shard_map/ppermute | solution.py:34
  97.0 8.6 %collective-permute-done.9.refs_6_ = bf16[1024,256]{1,0:T(8,128)(2,1)S(1)} collective-permute-done((bf16[1024,256]{1,0:T(8,128)(2,1)S(1)}, bf16[1024,256]{1,0:T(8,128)(2,1)S(1)}, u32[]{:S(2)}, u32[]{:S(2)}) %collective-permute-start.9) | collective-permute-done | bytes 524320 | tf_op jit(solution)/shard_map/ppermute | solution.py:34
  107.8 7.8 %attention_branch.1 = (f32[256,1024]{1,0:T(8,128)S(1)}, bf16[1024,1024]{1,0:T(8,128)(2,1)}, bf16[1024,1024]{1,0:T(8,128)(2,1)}) custom-call(s32[2]{0:T(128)S(1)} %get-tuple-element.111.place_ref, bf16[2,256,1024]{2,1,0:T(8,128)(2,1)S(1)} %pick_rows.1.refs_0_, bf16[2,256,1024]{2,1,0:T(8,128)(2,1)S(1)} %copy-done.23, bf16[2,256,1024]{2,1,0:T(8,128)(2,1)} %copy-done.45, ...), custom_call_target="tpu_custom_call" | custom-call | flops 2147483648 | bytes 13668352 | tf_op jit(solution)/shard_map/attention_branch/pallas_call | solution.py:646
  116.6 2.8 %fusion.63 = (bf16[8,128,1024]{2,1,0:T(8,128)(2,1)S(1)}, bf16[8,128,1024]{2,1,0:T(8,128)(2,1)S(1)}) fusion(bf16[8,256,1024]{2,1,0:T(8,128)(2,1)} %bitcast.130), kind=kLoop, calls=%fused_computation.138 | loop fusion | bytes 8388608 | tf_op jit(solution)/shard_map/slice | solution.py:917
  119.5 2.9 %multiply_convert_fusion = (bf16[1024,1024]{1,0:T(8,128)(2,1)S(1)}, f32[1024,1024]{1,0:T(8,128)S(1)}) fusion(bf16[1024,1024]{1,0:T(8,128)(2,1)S(1)} %copy-done.37, bf16[1024,1024]{1,0:T(8,128)(2,1)S(1)} %bitcast.108), kind=kOutput, calls=%fused_computation.9 | convolution fusion | flops 2152726528 | bytes 10485760 | tf_op jit(solution)/shard_map/dot_general | solution.py:24
  122.5 3.7 %fusion.5.pre_ref = bf16[1024,1024]{1,0:T(8,128)(2,1)S(1)} fusion(f32[1024,1024]{1,0:T(8,128)S(1)} %get-tuple-element.136, bf16[1024,1024]{1,0:T(8,128)(2,1)S(1)} %copy-done.38, bf16[1024,1024]{1,0:T(8,128)(2,1)S(1)} %bitcast.124), kind=kOutput, calls=%fused_computation.8 | convolution fusion | flops 2157969408 | bytes 10485760 | tf_op jit(solution)/shard_map/dot_general | solution.py:24
  134.1 6.9 %hidden_grads.1 = (bf16[8,2,128,1024]{3,2,1,0:T(8,128)(2,1)S(1)}, f32[1024,128]{1,0:T(8,128)S(1)}) custom-call(s32[2]{0:T(128)S(1)} %get-tuple-element.111.place_ref, bf16[1024,1024]{1,0:T(8,128)(2,1)S(1)} %get-tuple-element.77.act_ref, bf16[1024,1024]{1,0:T(8,128)(2,1)S(1)} %copy-done.38, bf16[1024,1024]{1,0:T(8,128)(2,1)S(1)} %copy-done.37, ...), custom_call_target="tpu_custom_call" | custom-call | flops 4294967296 | bytes 12582912 | tf_op jit(solution)/shard_map/hidden_grads/pallas_call | solution.py:310
  153.9 10.5 %collective-permute-done.20.refs_2_ = bf16[256,1024]{1,0:T(8,128)(2,1)S(1)} collective-permute-done((bf16[256,1024]{1,0:T(8,128)(2,1)S(1)}, bf16[256,1024]{1,0:T(8,128)(2,1)S(1)}, u32[]{:S(2)}, u32[]{:S(2)}) %collective-permute-start.20) | collective-permute-done | bytes 524320 | tf_op jit(solution)/shard_map/ppermute | solution.py:34
  171.0 7.6 %attention_backward.1 = bf16[4,256,768]{2,1,0:T(8,128)(2,1)S(1)} custom-call(s32[4]{0:T(128)S(1)} %get-tuple-element.141.window_ref, s32[4]{0:T(128)S(1)} %scatter_custom_fusion.place_ref, s32[4]{0:T(128)S(1)} %get-tuple-element.140.first_ref, bf16[1024,256]{1,0:T(8,128)(2,1)S(1)} %copy-done.29, bf16[4,256,512]{2,1,0:T(8,128)(2,1)S(1)} %bitcast.116, ...), custom_call_target="tpu_custom_call" | custom-call | flops 1342177280 | bytes 3670016 | tf_op jit(solution)/shard_map/attention_backward/pallas_call | solution.py:608
  178.7 4.7 %weight_grad.4 = (bf16[4,4,32,512]{3,2,1,0:T(8,128)(2,1)}, bf16[4,4,32,512]{3,2,1,0:T(8,128)(2,1)S(1)}, f32[1024,128]{1,0:T(8,128)S(1)}) custom-call(s32[2]{0:T(128)S(1)} %get-tuple-element.111.place_ref, bf16[1024,1024]{1,0:T(8,128)(2,1)S(1)} %copy-done.11, bf16[1024,768]{1,0:T(8,128)(2,1)S(1)} %bitcast.101, bf16[1024,896]{1,0:T(8,128)(2,1)S(1)} %copy-done, ...), custom_call_target="tpu_custom_call" | custom-call | flops 1073741824 | bytes 4194304 | tf_op jit(solution)/shard_map/weight_grad/pallas_call | solution.py:250
  193.7 3.0 %weight_grad.5 = (bf16[4,4,32,384]{3,2,1,0:T(8,128)(2,1)S(1)}, bf16[4,4,32,384]{3,2,1,0:T(8,128)(2,1)S(1)}) custom-call(s32[2]{0:T(128)S(1)} %get-tuple-element.111.place_ref, bf16[1024,1024]{1,0:T(8,128)(2,1)S(1)} %copy-done.12, bf16[1024,768]{1,0:T(8,128)(2,1)S(1)} %bitcast.102, bf16[1024,896]{1,0:T(8,128)(2,1)S(1)} %copy-done, ...), custom_call_target="tpu_custom_call" | custom-call | flops 536870912 | bytes 3407872 | tf_op jit(solution)/shard_map/weight_grad/pallas_call | solution.py:250
  201.3 3.2 %collective-permute-done.29 = bf16[4,4,32,512]{3,2,1,0:T(8,128)(2,1)} collective-permute-done((bf16[4,4,32,512]{3,2,1,0:T(8,128)(2,1)}, bf16[4,4,32,512]{3,2,1,0:T(8,128)(2,1)}, u32[]{:S(2)}, u32[]{:S(2)}) %collective-permute-start.29) | collective-permute-done | bytes 524320 | tf_op jit(solution)/shard_map/ppermute | solution.py:34
  211.4 3.3 %place_rows.2 = bf16[2048,1024]{1,0:T(8,128)(2,1)} custom-call(s32[1,256]{1,0:T(1,128)S(1)} %fusion.77.ids_ref, bf16[256,1024]{1,0:T(8,128)(2,1)S(1)} %get-tuple-element.91.new_ref, bf16[2048,1024]{1,0:T(8,128)(2,1)S(1)} %bitcast.98), custom_call_target="tpu_custom_call" | custom-call | flops 1073741824 | bytes 8388608 | tf_op jit(solution)/shard_map/place_rows/pallas_call | solution.py:428
  216.2 2.9 %collective-permute-start.31 = (bf16[1,4,32,512]{3,2,1,0:T(8,128)(2,1)S(1)}, bf16[1,4,32,512]{3,2,1,0:T(8,128)(2,1)S(1)}, u32[]{:S(2)}, u32[]{:S(2)}) collective-permute-start(bf16[1,4,32,512]{3,2,1,0:T(8,128)(2,1)S(1)} %slice.330), channel_id=1, source_target_pairs={{0,4},{1,5},{2,6},{3,7},{4,0},{5,1},{6,2},{7,3},{8,12},{9,13},{10,... | collective-permute-start | bytes 393224 | tf_op jit(solution)/shard_map/ppermute | solution.py:34
  220.6 7.5 %collective-permute-done.27 = bf16[2,4,32,384]{3,2,1,0:T(8,128)(2,1)S(1)} collective-permute-done((bf16[2,4,32,384]{3,2,1,0:T(8,128)(2,1)S(1)}, bf16[2,4,32,384]{3,2,1,0:T(8,128)(2,1)S(1)}, u32[]{:S(2)}, u32[]{:S(2)}) %collective-permute-start.27) | collective-permute-done | bytes 196640 | tf_op jit(solution)/shard_map/ppermute | solution.py:34
  229.0 3.3 %collective-permute-done.31 = bf16[1,4,32,512]{3,2,1,0:T(8,128)(2,1)S(1)} collective-permute-done((bf16[1,4,32,512]{3,2,1,0:T(8,128)(2,1)S(1)}, bf16[1,4,32,512]{3,2,1,0:T(8,128)(2,1)S(1)}, u32[]{:S(2)}, u32[]{:S(2)}) %collective-permute-start.31) | collective-permute-done | bytes 131104 | tf_op jit(solution)/shard_map/ppermute | solution.py:34
  232.3 8.4 %collective-permute-done.28 = bf16[1,4,32,384]{3,2,1,0:T(8,128)(2,1)S(1)} collective-permute-done((bf16[1,4,32,384]{3,2,1,0:T(8,128)(2,1)S(1)}, bf16[1,4,32,384]{3,2,1,0:T(8,128)(2,1)S(1)}, u32[]{:S(2)}, u32[]{:S(2)}) %collective-permute-start.28) | collective-permute-done | bytes 98336 | tf_op jit(solution)/shard_map/ppermute | solution.py:34
  245.0 2.9 %reduce-scatter.2.cloned.1.call-done = bf16[1,2,128,1024]{3,2,1,0:T(8,128)(2,1)} async-done(((bf16[8,2,128,1024]{3,2,1,0:T(8,128)(2,1)}), bf16[1,2,128,1024]{3,2,1,0:T(8,128)(2,1)}) %reduce-scatter.2.cloned.1.call-update) | async-done | bytes 524304 | tf_op jit(solution)/shard_map/reduce_scatter | solution.py:952
  248.9 2.7 collective-permute-start.38
  254.9 2.1 fusion.14.new_ref
  257.4 3.3 %place_rows.3 = bf16[2048,1024]{1,0:T(8,128)(2,1)} custom-call(s32[1,256]{1,0:T(1,128)S(1)} %fusion.77.ids_ref, bf16[256,1024]{1,0:T(8,128)(2,1)S(1)} %fusion.14.new_ref, bf16[2048,1024]{1,0:T(8,128)(2,1)S(1)} %bitcast.100), custom_call_target="tpu_custom_call" | custom-call | flops 1073741824 | bytes 8388608 | tf_op jit(solution)/shard_map/place_rows/pallas_call | solution.py:428
  261.3 2.6 collective-permute-done.33.refs_2_
  (256 shorter events, 93.5 us)
Async XLA Ops:
  7.2 109.5 %all-gather.3.cloned.1.call-start = ((), (), s32[]{:S(2)}) async-start(), calls=%async_computation.2 | async-start | bytes 4718592 | tf_op jit(solution)/shard_map/all_gather | solution.py:916
  11.3 17.5 %collective-permute-start.4 = (bf16[136,1024]{1,0:T(8,128)(2,1)S(1)}, bf16[136,1024]{1,0:T(8,128)(2,1)S(1)}, u32[]{:S(2)}, u32[]{:S(2)}) collective-permute-start(bf16[136,1024]{1,0:T(8,128)(2,1)S(1)} %first_shard.1), channel_id=1, source_target_pairs={{0,6},{1,7},{2,4},{3,5},{4,2},{5,3},{6,0},{7,1},{8,14},{9,15},{10,... | collective-permute-start | bytes 835592 | tf_op jit(solution)/shard_map/ppermute | solution.py:34
  15.5 23.3 %collective-permute-start.3 = (bf16[136,1024]{1,0:T(8,128)(2,1)S(1)}, bf16[136,1024]{1,0:T(8,128)(2,1)S(1)}, u32[]{:S(2)}, u32[]{:S(2)}) collective-permute-start(bf16[136,1024]{1,0:T(8,128)(2,1)S(1)} %first_shard.1), channel_id=1, source_target_pairs={{0,4},{1,5},{2,6},{3,7},{4,0},{5,1},{6,2},{7,3},{8,12},{9,13},{10,... | collective-permute-start | bytes 835592 | tf_op jit(solution)/shard_map/ppermute | solution.py:34
  15.6 23.3 %collective-permute-start.2 = (bf16[136,1024]{1,0:T(8,128)(2,1)S(1)}, bf16[136,1024]{1,0:T(8,128)(2,1)S(1)}, u32[]{:S(2)}, u32[]{:S(2)}) collective-permute-start(bf16[136,1024]{1,0:T(8,128)(2,1)S(1)} %first_shard.1), channel_id=1, source_target_pairs={{0,2},{1,3},{2,0},{3,1},{4,6},{5,7},{6,4},{7,5},{8,10},{9,11},{10,... | collective-permute-start | bytes 835592 | tf_op jit(solution)/shard_map/ppermute | solution.py:34
  15.9 9.6 %collective-permute-start.5 = (bf16[1,136,1024]{2,1,0:T(8,128)(2,1)S(1)}, bf16[1,136,1024]{2,1,0:T(8,128)(2,1)S(1)}, u32[]{:S(2)}, u32[]{:S(2)}) collective-permute-start(bf16[1,136,1024]{2,1,0:T(8,128)(2,1)S(1)} %bitcast.119), channel_id=1, source_target_pairs={{0,1},{1,0},{2,3},{3,2},{4,5},{5,4},{6,7},{7,6},{8,9},{9,8},{10,11... | collective-permute-start | bytes 835592 | tf_op jit(solution)/shard_map/ppermute | solution.py:34
  38.9 209.0 %reduce-scatter.2.cloned.1.call-start = ((), (), s32[]{:S(2)}) async-start(), calls=%async_computation.1 | async-start | bytes 4718592 | tf_op jit(solution)/shard_map/reduce_scatter | solution.py:952
  38.9 23.5 %collective-permute-start.1 = (bf16[2,256,1024]{2,1,0:T(8,128)(2,1)S(1)}, bf16[2,256,1024]{2,1,0:T(8,128)(2,1)S(1)}, u32[]{:S(2)}, u32[]{:S(2)}) collective-permute-start(bf16[2,256,1024]{2,1,0:T(8,128)(2,1)S(1)} %pick_rows.1.refs_0_), channel_id=1, source_target_pairs={{0,16},{8,24},{16,0},{24,8},{1,17},{9,25},{17,1},{25,9},{2,18},{10... | collective-permute-start | bytes 3145736 | tf_op jit(solution)/shard_map/ppermute | solution.py:34
  40.3 24.1 %collective-permute-start.6 = (bf16[3,136,1024]{2,1,0:T(8,128)(2,1)S(1)}, bf16[3,136,1024]{2,1,0:T(8,128)(2,1)S(1)}, u32[]{:S(2)}, u32[]{:S(2)}) collective-permute-start(bf16[3,136,1024]{2,1,0:T(8,128)(2,1)S(1)} %pad_maximum_fusion.refs_5_), channel_id=1, source_target_pairs={{0,1},{1,0},{2,3},{3,2},{4,5},{5,4},{6,7},{7,6},{8,9},{9,8},{10,11... | collective-permute-start | bytes 2506760 | tf_op jit(solution)/shard_map/ppermute | solution.py:34
  41.6 25.5 %collective-permute-start = (bf16[2,256,1024]{2,1,0:T(8,128)(2,1)S(1)}, bf16[2,256,1024]{2,1,0:T(8,128)(2,1)S(1)}, u32[]{:S(2)}, u32[]{:S(2)}) collective-permute-start(bf16[2,256,1024]{2,1,0:T(8,128)(2,1)S(1)} %pick_rows.1.refs_0_), channel_id=1, source_target_pairs={{0,8},{8,0},{16,24},{24,16},{1,9},{9,1},{17,25},{25,17},{2,10},{10... | collective-permute-start | bytes 3145736 | tf_op jit(solution)/shard_map/ppermute | solution.py:34
  77.3 13.4 %collective-permute-start.11 = (bf16[8,32,1024]{2,1,0:T(8,128)(2,1)}, bf16[8,32,1024]{2,1,0:T(8,128)(2,1)}, u32[]{:S(2)}, u32[]{:S(2)}) collective-permute-start(bf16[8,32,1024]{2,1,0:T(8,128)(2,1)} %get-tuple-element.65.refs_0_), channel_id=1, source_target_pairs={{0,16},{8,24},{16,0},{24,8},{1,17},{9,25},{17,1},{25,9},{2,18},{10... | collective-permute-start | bytes 1572872 | tf_op jit(solution)/shard_map/ppermute | solution.py:34
  80.2 12.4 %collective-permute-start.10 = (bf16[8,32,1024]{2,1,0:T(8,128)(2,1)}, bf16[8,32,1024]{2,1,0:T(8,128)(2,1)S(1)}, u32[]{:S(2)}, u32[]{:S(2)}) collective-permute-start(bf16[8,32,1024]{2,1,0:T(8,128)(2,1)} %get-tuple-element.65.refs_0_), channel_id=1, source_target_pairs={{0,8},{8,0},{16,24},{24,16},{1,9},{9,1},{17,25},{25,17},{2,10},{10... | collective-permute-start | bytes 1572872 | tf_op jit(solution)/shard_map/ppermute | solution.py:34
  92.0 13.6 %collective-permute-start.9 = (bf16[1024,256]{1,0:T(8,128)(2,1)S(1)}, bf16[1024,256]{1,0:T(8,128)(2,1)S(1)}, u32[]{:S(2)}, u32[]{:S(2)}) collective-permute-start(bf16[1024,256]{1,0:T(8,128)(2,1)S(1)} %get-tuple-element.64.refs_4_.a_ref.o_ref), channel_id=1, source_target_pairs={{0,16},{8,24},{16,0},{24,8},{1,17},{9,25},{17,1},{25,9},{2,18},{10... | collective-permute-start | bytes 1572872 | tf_op jit(solution)/shard_map/ppermute | solution.py:34
  92.2 14.2 %collective-permute-start.8 = (bf16[1024,256]{1,0:T(8,128)(2,1)S(1)}, bf16[1024,256]{1,0:T(8,128)(2,1)S(1)}, u32[]{:S(2)}, u32[]{:S(2)}) collective-permute-start(bf16[1024,256]{1,0:T(8,128)(2,1)S(1)} %get-tuple-element.64.refs_4_.a_ref.o_ref), channel_id=1, source_target_pairs={{0,8},{8,0},{16,24},{24,16},{1,9},{9,1},{17,25},{25,17},{2,10},{10... | collective-permute-start | bytes 1572872 | tf_op jit(solution)/shard_map/ppermute | solution.py:34
  129.6 14.3 %collective-permute-start.14 = (bf16[256,1024]{1,0:T(8,128)(2,1)}, bf16[256,1024]{1,0:T(8,128)(2,1)}, u32[]{:S(2)}, u32[]{:S(2)}) collective-permute-start(bf16[256,1024]{1,0:T(8,128)(2,1)} %fusion.28), channel_id=1, source_target_pairs={{0,8},{8,0},{16,24},{24,16},{1,9},{9,1},{17,25},{25,17},{2,10},{10... | collective-permute-start | bytes 1572872 | tf_op jit(solution)/shard_map/ppermute | solution.py:34
  131.2 13.4 %collective-permute-start.16 = (bf16[256,1024]{1,0:T(8,128)(2,1)}, bf16[256,1024]{1,0:T(8,128)(2,1)}, u32[]{:S(2)}, u32[]{:S(2)}) collective-permute-start(bf16[256,1024]{1,0:T(8,128)(2,1)} %add_convert_fusion.1), channel_id=1, source_target_pairs={{0,16},{8,24},{16,0},{24,8},{1,17},{9,25},{17,1},{25,9},{2,18},{10... | collective-permute-start | bytes 1572872 | tf_op jit(solution)/shard_map/ppermute | solution.py:34
  150.6 13.7 %collective-permute-start.20 = (bf16[256,1024]{1,0:T(8,128)(2,1)S(1)}, bf16[256,1024]{1,0:T(8,128)(2,1)S(1)}, u32[]{:S(2)}, u32[]{:S(2)}) collective-permute-start(bf16[256,1024]{1,0:T(8,128)(2,1)S(1)} %fusion.10.refs_0_), channel_id=1, source_target_pairs={{0,16},{8,24},{16,0},{24,8},{1,17},{9,25},{17,1},{25,9},{2,18},{10... | collective-permute-start | bytes 1572872 | tf_op jit(solution)/shard_map/ppermute | solution.py:34
  152.5 33.5 %collective-permute-start.18 = (bf16[256,1024]{1,0:T(8,128)(2,1)S(1)}, bf16[256,1024]{1,0:T(8,128)(2,1)S(1)}, u32[]{:S(2)}, u32[]{:S(2)}) collective-permute-start(bf16[256,1024]{1,0:T(8,128)(2,1)S(1)} %fusion.36), channel_id=1, source_target_pairs={{0,8},{8,0},{16,24},{24,16},{1,9},{9,1},{17,25},{25,17},{2,10},{10... | collective-permute-start | bytes 1572872 | tf_op jit(solution)/shard_map/ppermute | solution.py:34
  153.6 12.9 %collective-permute-start.19 = (bf16[256,1024]{1,0:T(8,128)(2,1)S(1)}, bf16[256,1024]{1,0:T(8,128)(2,1)S(1)}, u32[]{:S(2)}, u32[]{:S(2)}) collective-permute-start(bf16[256,1024]{1,0:T(8,128)(2,1)S(1)} %fusion.32), channel_id=1, source_target_pairs={{0,8},{8,0},{16,24},{24,16},{1,9},{9,1},{17,25},{25,17},{2,10},{10... | collective-permute-start | bytes 1572872 | tf_op jit(solution)/shard_map/ppermute | solution.py:34
  166.6 19.4 %collective-permute-start.22 = (bf16[256,1024]{1,0:T(8,128)(2,1)S(1)}, bf16[256,1024]{1,0:T(8,128)(2,1)S(1)}, u32[]{:S(2)}, u32[]{:S(2)}) collective-permute-start(bf16[256,1024]{1,0:T(8,128)(2,1)S(1)} %add_convert_fusion), channel_id=1, source_target_pairs={{0,16},{8,24},{16,0},{24,8},{1,17},{9,25},{17,1},{25,9},{2,18},{10... | collective-permute-start | bytes 1572872 | tf_op jit(solution)/shard_map/ppermute | solution.py:34
  170.5 13.9 %collective-permute-start.35 = (bf16[4,1,32,1024]{3,2,1,0:T(8,128)(2,1)S(1)}, bf16[4,1,32,1024]{3,2,1,0:T(8,128)(2,1)S(1)}, u32[]{:S(2)}, u32[]{:S(2)}) collective-permute-start(bf16[4,1,32,1024]{3,2,1,0:T(8,128)(2,1)S(1)} %get-tuple-element.83), channel_id=1, source_target_pairs={{0,1},{1,0},{2,3},{3,2},{4,5},{5,4},{6,7},{7,6},{8,9},{9,8},{10,11... | collective-permute-start | bytes 786440 | tf_op jit(solution)/shard_map/ppermute | solution.py:34
  183.4 21.1 %collective-permute-start.29 = (bf16[4,4,32,512]{3,2,1,0:T(8,128)(2,1)}, bf16[4,4,32,512]{3,2,1,0:T(8,128)(2,1)}, u32[]{:S(2)}, u32[]{:S(2)}) collective-permute-start(bf16[4,4,32,512]{3,2,1,0:T(8,128)(2,1)} %get-tuple-element.87), channel_id=1, source_target_pairs={{0,1},{1,0},{2,3},{3,2},{4,5},{5,4},{6,7},{7,6},{8,9},{9,8},{10,11... | collective-permute-start | bytes 1572872 | tf_op jit(solution)/shard_map/ppermute | solution.py:34
  196.7 22.3 %collective-permute-start.26 = (bf16[4,4,32,384]{3,2,1,0:T(8,128)(2,1)S(1)}, bf16[4,4,32,384]{3,2,1,0:T(8,128)(2,1)S(1)}, u32[]{:S(2)}, u32[]{:S(2)}) collective-permute-start(bf16[4,4,32,384]{3,2,1,0:T(8,128)(2,1)S(1)} %get-tuple-element.90), channel_id=1, source_target_pairs={{0,2},{1,3},{2,0},{3,1},{4,6},{5,7},{6,4},{7,5},{8,10},{9,11},{10,... | collective-permute-start | bytes 1179656 | tf_op jit(solution)/shard_map/ppermute | solution.py:34
  198.2 11.1 %collective-permute-start.36 = (bf16[2,1,32,1024]{3,2,1,0:T(8,128)(2,1)S(1)}, bf16[2,1,32,1024]{3,2,1,0:T(8,128)(2,1)S(1)}, u32[]{:S(2)}, u32[]{:S(2)}) collective-permute-start(bf16[2,1,32,1024]{3,2,1,0:T(8,128)(2,1)S(1)} %copy-done.47), channel_id=1, source_target_pairs={{0,2},{1,3},{2,0},{3,1},{4,6},{5,7},{6,4},{7,5},{8,10},{9,11},{10,... | collective-permute-start | bytes 393224 | tf_op jit(solution)/shard_map/ppermute | solution.py:34
  198.9 43.0 %collective-permute-start.23 = (bf16[256,1024]{1,0:T(8,128)(2,1)S(1)}, bf16[256,1024]{1,0:T(8,128)(2,1)S(1)}, u32[]{:S(2)}, u32[]{:S(2)}) collective-permute-start(bf16[256,1024]{1,0:T(8,128)(2,1)S(1)} %convolution_convert_fusion.1), channel_id=1, source_target_pairs={{0,8},{8,0},{16,24},{24,16},{1,9},{9,1},{17,25},{25,17},{2,10},{10... | collective-permute-start | bytes 1572872 | tf_op jit(solution)/shard_map/ppermute | solution.py:34
  201.2 18.4 %collective-permute-start.24 = (bf16[256,1024]{1,0:T(8,128)(2,1)S(1)}, bf16[256,1024]{1,0:T(8,128)(2,1)S(1)}, u32[]{:S(2)}, u32[]{:S(2)}) collective-permute-start(bf16[256,1024]{1,0:T(8,128)(2,1)S(1)} %convolution_convert_fusion), channel_id=1, source_target_pairs={{0,8},{8,0},{16,24},{24,16},{1,9},{9,1},{17,25},{25,17},{2,10},{10... | collective-permute-start | bytes 1572872 | tf_op jit(solution)/shard_map/ppermute | solution.py:34
  205.9 10.1 %collective-permute-start.30 = (bf16[2,4,32,512]{3,2,1,0:T(8,128)(2,1)S(1)}, bf16[2,4,32,512]{3,2,1,0:T(8,128)(2,1)S(1)}, u32[]{:S(2)}, u32[]{:S(2)}) collective-permute-start(bf16[2,4,32,512]{3,2,1,0:T(8,128)(2,1)S(1)} %slice.192), channel_id=1, source_target_pairs={{0,2},{1,3},{2,0},{3,1},{4,6},{5,7},{6,4},{7,5},{8,10},{9,11},{10,... | collective-permute-start | bytes 786440 | tf_op jit(solution)/shard_map/ppermute | solution.py:34
  216.2 16.1 %collective-permute-start.31 = (bf16[1,4,32,512]{3,2,1,0:T(8,128)(2,1)S(1)}, bf16[1,4,32,512]{3,2,1,0:T(8,128)(2,1)S(1)}, u32[]{:S(2)}, u32[]{:S(2)}) collective-permute-start(bf16[1,4,32,512]{3,2,1,0:T(8,128)(2,1)S(1)} %slice.330), channel_id=1, source_target_pairs={{0,4},{1,5},{2,6},{3,7},{4,0},{5,1},{6,2},{7,3},{8,12},{9,13},{10,... | collective-permute-start | bytes 393224 | tf_op jit(solution)/shard_map/ppermute | solution.py:34
  220.2 21.8 %collective-permute-start.25 = (bf16[256,1024]{1,0:T(8,128)(2,1)S(1)}, bf16[256,1024]{1,0:T(8,128)(2,1)S(1)}, u32[]{:S(2)}, u32[]{:S(2)}) collective-permute-start(bf16[256,1024]{1,0:T(8,128)(2,1)S(1)} %fusion.8), channel_id=1, source_target_pairs={{0,16},{8,24},{16,0},{24,8},{1,17},{9,25},{17,1},{25,9},{2,18},{10... | collective-permute-start | bytes 1572872 | tf_op jit(solution)/shard_map/ppermute | solution.py:34
  228.2 12.5 %collective-permute-start.28 = (bf16[1,4,32,384]{3,2,1,0:T(8,128)(2,1)S(1)}, bf16[1,4,32,384]{3,2,1,0:T(8,128)(2,1)S(1)}, u32[]{:S(2)}, u32[]{:S(2)}) collective-permute-start(bf16[1,4,32,384]{3,2,1,0:T(8,128)(2,1)S(1)} %slice.331), channel_id=1, source_target_pairs={{0,4},{1,5},{2,6},{3,7},{4,0},{5,1},{6,2},{7,3},{8,12},{9,13},{10,... | collective-permute-start | bytes 294920 | tf_op jit(solution)/shard_map/ppermute | solution.py:34
  248.9 16.8 %collective-permute-start.38 = (bf16[128,1024]{1,0:T(8,128)(2,1)S(1)}, bf16[128,1024]{1,0:T(8,128)(2,1)S(1)}, u32[]{:S(2)}, u32[]{:S(2)}) collective-permute-start(bf16[128,1024]{1,0:T(8,128)(2,1)S(1)} %get-tuple-element.120), channel_id=1, source_target_pairs={{0,0},{4,4},{1,8},{5,12},{2,16},{6,20},{3,24},{7,28},{8,1},{12,5},... | collective-permute-start | bytes 786440 | tf_op jit(solution)/shard_map/ppermute | solution.py:1026
  253.9 10.1 %collective-permute-start.33 = (bf16[32,1920]{1,0:T(8,128)(2,1)S(1)}, bf16[32,1920]{1,0:T(8,128)(2,1)S(1)}, u32[]{:S(2)}, u32[]{:S(2)}) collective-permute-start(bf16[32,1920]{1,0:T(8,128)(2,1)S(1)} %get-tuple-element.125), channel_id=1, source_target_pairs={{0,16},{8,24},{16,0},{24,8},{1,17},{9,25},{17,1},{25,9},{2,18},{10... | collective-permute-start | bytes 368648 | tf_op jit(solution)/shard_map/ppermute | solution.py:34
  253.9 10.1 %collective-permute-start.32 = (bf16[32,1920]{1,0:T(8,128)(2,1)S(1)}, bf16[32,1920]{1,0:T(8,128)(2,1)S(1)}, u32[]{:S(2)}, u32[]{:S(2)}) collective-permute-start(bf16[32,1920]{1,0:T(8,128)(2,1)S(1)} %get-tuple-element.126), channel_id=1, source_target_pairs={{0,8},{8,0},{16,24},{24,16},{1,9},{9,1},{17,25},{25,17},{2,10},{10... | collective-permute-start | bytes 368648 | tf_op jit(solution)/shard_map/ppermute | solution.py:34
  (65 other events, 338.2 us)
Sparse Core Ops, SparseCore 0:
  39.0 76.1 all-gather.2
  143.9 103.8 reduce-scatter.1

commit v6 on v5

--- a/solution.py
+++ b/solution.py
@@ -583,7 +583,7 @@
             out_specs=[by_rows, lse],
         ),
         out_shape=[jax.ShapeDtypeStruct((rows, width), BF16), jax.ShapeDtypeStruct((8, rows), F32)],
-        compiler_params=pltpu.CompilerParams(vmem_limit_bytes=VMEM_LIMIT),
+        compiler_params=pltpu.CompilerParams(vmem_limit_bytes=GRAD_LIMIT),
         cost_estimate=pl.CostEstimate(
             flops=2 * rows * rows * width,
             transcendentals=rows * rows * width // HD // 2,
@@ -615,7 +615,7 @@
             scratch_shapes=[pltpu.VMEM((blocks, tile, width), F32)] * 2,
         ),
         out_shape=jax.ShapeDtypeStruct((blocks, tile, 3 * width), BF16),
-        compiler_params=pltpu.CompilerParams(vmem_limit_bytes=VMEM_LIMIT),
+        compiler_params=pltpu.CompilerParams(vmem_limit_bytes=GRAD_LIMIT),
         cost_estimate=pl.CostEstimate(
             flops=5 * rows * rows * width,
             transcendentals=rows * rows * width // HD // 2,

time: 275 us -> 275 us (level)
  transfers between devices with their start and end apart: 41 -> 41, of which waited for: 18 -> 20; matrix products, arithmetic and copies ran while one was open for 12% -> 12% of each run, Pallas kernels for 23% -> 24%
where the time goes in v6:
time: 275 us; the launch traced here: 274 us
  waiting for transfers between devices  88.2 us (32%)
  Pallas kernels  65.6 us (24%)
  starting transfers between devices  39.8 us (14%)
  local copies, waits for them, and re-layouts  30.1 us (11%)
  matrix products  18.7 us (7%)
  other arithmetic  16.7 us (6%)
  between operations  14.8 us (5%)
    ppermute x38, waiting for transfers between devices, flip(): return lax.ppermute(values, axis, [(j, j ^ bit) for j in range(count)])  85.2 us
    ppermute x38, starting transfers between devices, flip(): return lax.ppermute(values, axis, [(j, j ^ bit) for j in range(count)])  37 us
    dot_general x14, matrix products, mm(): return lax.dot_general(a, b, (dims, ((), ())), preferred_element_type=F32)  18.7 us
    unnamed x113, local copies, waits for them, and re-layouts  18.1 us
    pallas_call x3, Pallas kernels, one_step(): pl.pallas_call(kernel, grid_spec=pltpu.PrefetchScalarGridSpec(num_scalar_...  15.3 us
    pallas_call x3, Pallas kernels, weight_grad(): pl.pallas_call(partial(weight_grad_kernel, per=per, fsdps=fsdps, seqs=lax...  9.18 us
    pallas_call x1, Pallas kernels, attention_backward(): pl.pallas_call(attention_backward_kernel, grid_spec=pltpu.PrefetchScalarG...  8.49 us
    pallas_call x1, Pallas kernels, hidden_grads(): pl.pallas_call(partial(hidden_grads_kernel, per=total // (seqs * fsdps),...  6.88 us
  transfers between devices with their start and end apart: 41, of which 20 were waited for; matrix products, arithmetic and copies ran while one was open for 12% of the time, Pallas kernels for 24%

profile of v6, /device:TPU:1, one launch (start us, length us, event | category | flops | bytes accessed | tf_op | source)
XLA Modules:
  0.0 273.9 jit_solution(12144028318420743970)
XLA Ops:
  11.3 4.2 %collective-permute-start.4 = (bf16[136,1024]{1,0:T(8,128)(2,1)S(1)}, bf16[136,1024]{1,0:T(8,128)(2,1)S(1)}, u32[]{:S(2)}, u32[]{:S(2)}) collective-permute-start(bf16[136,1024]{1,0:T(8,128)(2,1)S(1)} %first_shard.1), channel_id=1, source_target_pairs={{0,6},{1,7},{2,4},{3,5},{4,2},{5,3},{6,0},{7,1},{8,14},{9,15},{10,... | collective-permute-start | bytes 835592 | tf_op jit(solution)/shard_map/ppermute | solution.py:34
  17.3 2.2 copy-done.1
  19.5 6.0 %pick_rows.1.refs_0_ = bf16[2,256,1024]{2,1,0:T(8,128)(2,1)S(1)} custom-call(s32[256,1]{1,0:T(8,128)S(1)} %copy.33.ids_ref, bf16[2048,1024]{1,0:T(8,128)(2,1)S(1)} %bitcast.97, bf16[2048,1024]{1,0:T(8,128)(2,1)} %bitcast.99), custom_call_target="tpu_custom_call" | custom-call | flops 2147483648 | bytes 8388608 | tf_op jit(solution)/shard_map/pick_rows/pallas_call | solution.py:397
  25.6 3.3 %hidden_shard.1 = bf16[256,1024]{1,0:T(8,128)(2,1)} custom-call(s32[2]{0:T(128)S(1)} %get-tuple-element.111.place_ref, bf16[128,4096]{1,0:T(8,128)(2,1)S(1)} %copy-done.24, bf16[512,1024]{1,0:T(8,128)(2,1)S(1)} %copy-done.25), custom_call_target="tpu_custom_call" | custom-call | bytes 1048576 | tf_op jit(solution)/shard_map/hidden_shard/pallas_call | solution.py:716
  28.9 10.0 %collective-permute-done.3 = bf16[136,1024]{1,0:T(8,128)(2,1)S(1)} collective-permute-done((bf16[136,1024]{1,0:T(8,128)(2,1)S(1)}, bf16[136,1024]{1,0:T(8,128)(2,1)S(1)}, u32[]{:S(2)}, u32[]{:S(2)}) %collective-permute-start.3) | collective-permute-done | bytes 278560 | tf_op jit(solution)/shard_map/ppermute | solution.py:34
  43.5 18.9 %collective-permute-done.1.refs_2_ = bf16[2,256,1024]{2,1,0:T(8,128)(2,1)S(1)} collective-permute-done((bf16[2,256,1024]{2,1,0:T(8,128)(2,1)S(1)}, bf16[2,256,1024]{2,1,0:T(8,128)(2,1)S(1)}, u32[]{:S(2)}, u32[]{:S(2)}) %collective-permute-start.1) | collective-permute-done | bytes 1048608 | tf_op jit(solution)/shard_map/ppermute | solution.py:34
  64.4 2.6 collective-permute-start.7
  67.1 2.2 collective-permute-done.7.refs_3_
  70.3 6.2 %project.1 = (bf16[8,32,1024]{2,1,0:T(8,128)(2,1)}, bf16[1024,896]{1,0:T(8,128)(2,1)}, f32[8,1024]{1,0:T(8,128)S(1)}, bf16[1024,1024]{1,0:T(8,128)(2,1)}, bf16[1...) custom-call(s32[2]{0:T(128)S(1)} %get-tuple-element.111.place_ref, ...), custom_call_target="tpu_custom_call" | custom-call | flops 1879048192 | bytes 12488704 | tf_op jit(solution)/shard_map/project/pallas_call | solution.py:646
  81.9 6.3 %attention_forward.1 = (bf16[1024,256]{1,0:T(8,128)(2,1)S(1)}, f32[8,1024]{1,0:T(8,128)S(1)}) custom-call(s32[4]{0:T(128)S(1)} %get-tuple-element.141.window_ref, s32[4]{0:T(128)S(1)} %scatter_custom_fusion.place_ref, s32[4]{0:T(128)S(1)} %get-tuple-element.140.first_ref, bf16[1024,256]{1,0:T(8,128)(2,1)S(1)} %get-tuple-element.62.q_ref, ...), custom_call_target="tpu_custom_call" | custom-call | flops 536870912 | bytes 2097152 | tf_op jit(solution)/shard_map/attention_forward/pallas_call | solution.py:577
  88.3 2.4 collective-permute-done.11.refs_2_
  97.0 8.6 %collective-permute-done.9.refs_6_ = bf16[1024,256]{1,0:T(8,128)(2,1)S(1)} collective-permute-done((bf16[1024,256]{1,0:T(8,128)(2,1)S(1)}, bf16[1024,256]{1,0:T(8,128)(2,1)S(1)}, u32[]{:S(2)}, u32[]{:S(2)}) %collective-permute-start.9) | collective-permute-done | bytes 524320 | tf_op jit(solution)/shard_map/ppermute | solution.py:34
  107.8 7.8 %attention_branch.1 = (f32[256,1024]{1,0:T(8,128)S(1)}, bf16[1024,1024]{1,0:T(8,128)(2,1)}, bf16[1024,1024]{1,0:T(8,128)(2,1)}) custom-call(s32[2]{0:T(128)S(1)} %get-tuple-element.111.place_ref, bf16[2,256,1024]{2,1,0:T(8,128)(2,1)S(1)} %pick_rows.1.refs_0_, bf16[2,256,1024]{2,1,0:T(8,128)(2,1)S(1)} %copy-done.23, bf16[2,256,1024]{2,1,0:T(8,128)(2,1)} %copy-done.45, ...), custom_call_target="tpu_custom_call" | custom-call | flops 2147483648 | bytes 13668352 | tf_op jit(solution)/shard_map/attention_branch/pallas_call | solution.py:646
  116.6 2.8 %fusion.63 = (bf16[8,128,1024]{2,1,0:T(8,128)(2,1)S(1)}, bf16[8,128,1024]{2,1,0:T(8,128)(2,1)S(1)}) fusion(bf16[8,256,1024]{2,1,0:T(8,128)(2,1)} %bitcast.130), kind=kLoop, calls=%fused_computation.138 | loop fusion | bytes 8388608 | tf_op jit(solution)/shard_map/slice | solution.py:917
  119.5 2.9 %multiply_convert_fusion = (bf16[1024,1024]{1,0:T(8,128)(2,1)S(1)}, f32[1024,1024]{1,0:T(8,128)S(1)}) fusion(bf16[1024,1024]{1,0:T(8,128)(2,1)S(1)} %copy-done.37, bf16[1024,1024]{1,0:T(8,128)(2,1)S(1)} %bitcast.108), kind=kOutput, calls=%fused_computation.9 | convolution fusion | flops 2152726528 | bytes 10485760 | tf_op jit(solution)/shard_map/dot_general | solution.py:24
  122.5 3.7 %fusion.5.pre_ref = bf16[1024,1024]{1,0:T(8,128)(2,1)S(1)} fusion(f32[1024,1024]{1,0:T(8,128)S(1)} %get-tuple-element.136, bf16[1024,1024]{1,0:T(8,128)(2,1)S(1)} %copy-done.38, bf16[1024,1024]{1,0:T(8,128)(2,1)S(1)} %bitcast.124), kind=kOutput, calls=%fused_computation.8 | convolution fusion | flops 2157969408 | bytes 10485760 | tf_op jit(solution)/shard_map/dot_general | solution.py:24
  134.1 6.9 %hidden_grads.1 = (bf16[8,2,128,1024]{3,2,1,0:T(8,128)(2,1)S(1)}, f32[1024,128]{1,0:T(8,128)S(1)}) custom-call(s32[2]{0:T(128)S(1)} %get-tuple-element.111.place_ref, bf16[1024,1024]{1,0:T(8,128)(2,1)S(1)} %get-tuple-element.77.act_ref, bf16[1024,1024]{1,0:T(8,128)(2,1)S(1)} %copy-done.38, bf16[1024,1024]{1,0:T(8,128)(2,1)S(1)} %copy-done.37, ...), custom_call_target="tpu_custom_call" | custom-call | flops 4294967296 | bytes 12582912 | tf_op jit(solution)/shard_map/hidden_grads/pallas_call | solution.py:310
  153.9 10.5 %collective-permute-done.20.refs_2_ = bf16[256,1024]{1,0:T(8,128)(2,1)S(1)} collective-permute-done((bf16[256,1024]{1,0:T(8,128)(2,1)S(1)}, bf16[256,1024]{1,0:T(8,128)(2,1)S(1)}, u32[]{:S(2)}, u32[]{:S(2)}) %collective-permute-start.20) | collective-permute-done | bytes 524320 | tf_op jit(solution)/shard_map/ppermute | solution.py:34
  171.0 8.5 %attention_backward.1 = bf16[4,256,768]{2,1,0:T(8,128)(2,1)S(1)} custom-call(s32[4]{0:T(128)S(1)} %get-tuple-element.141.window_ref, s32[4]{0:T(128)S(1)} %scatter_custom_fusion.place_ref, s32[4]{0:T(128)S(1)} %get-tuple-element.140.first_ref, bf16[1024,256]{1,0:T(8,128)(2,1)S(1)} %copy-done.29, bf16[4,256,512]{2,1,0:T(8,128)(2,1)S(1)} %bitcast.116, ...), custom_call_target="tpu_custom_call" | custom-call | flops 1342177280 | bytes 3670016 | tf_op jit(solution)/shard_map/attention_backward/pallas_call | solution.py:608
  179.5 4.7 %weight_grad.4 = (bf16[4,4,32,512]{3,2,1,0:T(8,128)(2,1)}, bf16[4,4,32,512]{3,2,1,0:T(8,128)(2,1)S(1)}, f32[1024,128]{1,0:T(8,128)S(1)}) custom-call(s32[2]{0:T(128)S(1)} %get-tuple-element.111.place_ref, bf16[1024,1024]{1,0:T(8,128)(2,1)S(1)} %copy-done.11, bf16[1024,768]{1,0:T(8,128)(2,1)S(1)} %bitcast.101, bf16[1024,896]{1,0:T(8,128)(2,1)S(1)} %copy-done, ...), custom_call_target="tpu_custom_call" | custom-call | flops 1073741824 | bytes 4194304 | tf_op jit(solution)/shard_map/weight_grad/pallas_call | solution.py:250
  194.5 3.0 %weight_grad.5 = (bf16[4,4,32,384]{3,2,1,0:T(8,128)(2,1)S(1)}, bf16[4,4,32,384]{3,2,1,0:T(8,128)(2,1)S(1)}) custom-call(s32[2]{0:T(128)S(1)} %get-tuple-element.111.place_ref, bf16[1024,1024]{1,0:T(8,128)(2,1)S(1)} %copy-done.12, bf16[1024,768]{1,0:T(8,128)(2,1)S(1)} %bitcast.102, bf16[1024,896]{1,0:T(8,128)(2,1)S(1)} %copy-done, ...), custom_call_target="tpu_custom_call" | custom-call | flops 536870912 | bytes 3407872 | tf_op jit(solution)/shard_map/weight_grad/pallas_call | solution.py:250
  202.2 3.4 %collective-permute-done.29 = bf16[4,4,32,512]{3,2,1,0:T(8,128)(2,1)} collective-permute-done((bf16[4,4,32,512]{3,2,1,0:T(8,128)(2,1)}, bf16[4,4,32,512]{3,2,1,0:T(8,128)(2,1)}, u32[]{:S(2)}, u32[]{:S(2)}) %collective-permute-start.29) | collective-permute-done | bytes 524320 | tf_op jit(solution)/shard_map/ppermute | solution.py:34
  211.4 3.3 %place_rows.2 = bf16[2048,1024]{1,0:T(8,128)(2,1)} custom-call(s32[1,256]{1,0:T(1,128)S(1)} %fusion.77.ids_ref, bf16[256,1024]{1,0:T(8,128)(2,1)S(1)} %get-tuple-element.91.new_ref, bf16[2048,1024]{1,0:T(8,128)(2,1)S(1)} %bitcast.98), custom_call_target="tpu_custom_call" | custom-call | flops 1073741824 | bytes 8388608 | tf_op jit(solution)/shard_map/place_rows/pallas_call | solution.py:428
  216.4 2.6 collective-permute-start.31
  221.4 6.7 %collective-permute-done.27 = bf16[2,4,32,384]{3,2,1,0:T(8,128)(2,1)S(1)} collective-permute-done((bf16[2,4,32,384]{3,2,1,0:T(8,128)(2,1)S(1)}, bf16[2,4,32,384]{3,2,1,0:T(8,128)(2,1)S(1)}, u32[]{:S(2)}, u32[]{:S(2)}) %collective-permute-start.27) | collective-permute-done | bytes 196640 | tf_op jit(solution)/shard_map/ppermute | solution.py:34
  228.8 3.4 %collective-permute-done.31 = bf16[1,4,32,512]{3,2,1,0:T(8,128)(2,1)S(1)} collective-permute-done((bf16[1,4,32,512]{3,2,1,0:T(8,128)(2,1)S(1)}, bf16[1,4,32,512]{3,2,1,0:T(8,128)(2,1)S(1)}, u32[]{:S(2)}, u32[]{:S(2)}) %collective-permute-start.31) | collective-permute-done | bytes 131104 | tf_op jit(solution)/shard_map/ppermute | solution.py:34
  232.2 8.4 %collective-permute-done.28 = bf16[1,4,32,384]{3,2,1,0:T(8,128)(2,1)S(1)} collective-permute-done((bf16[1,4,32,384]{3,2,1,0:T(8,128)(2,1)S(1)}, bf16[1,4,32,384]{3,2,1,0:T(8,128)(2,1)S(1)}, u32[]{:S(2)}, u32[]{:S(2)}) %collective-permute-start.28) | collective-permute-done | bytes 98336 | tf_op jit(solution)/shard_map/ppermute | solution.py:34
  244.9 3.0 %reduce-scatter.2.cloned.1.call-done = bf16[1,2,128,1024]{3,2,1,0:T(8,128)(2,1)} async-done(((bf16[8,2,128,1024]{3,2,1,0:T(8,128)(2,1)}), bf16[1,2,128,1024]{3,2,1,0:T(8,128)(2,1)}) %reduce-scatter.2.cloned.1.call-update) | async-done | bytes 524304 | tf_op jit(solution)/shard_map/reduce_scatter | solution.py:952
  248.9 2.7 collective-permute-start.38
  254.9 2.1 fusion.14.new_ref
  257.4 3.3 %place_rows.3 = bf16[2048,1024]{1,0:T(8,128)(2,1)} custom-call(s32[1,256]{1,0:T(1,128)S(1)} %fusion.77.ids_ref, bf16[256,1024]{1,0:T(8,128)(2,1)S(1)} %fusion.14.new_ref, bf16[2048,1024]{1,0:T(8,128)(2,1)S(1)} %bitcast.100), custom_call_target="tpu_custom_call" | custom-call | flops 1073741824 | bytes 8388608 | tf_op jit(solution)/shard_map/place_rows/pallas_call | solution.py:428
  261.9 2.6 collective-permute-done.33.refs_2_
  (256 shorter events, 93.7 us)
Async XLA Ops:
  7.2 109.5 %all-gather.3.cloned.1.call-start = ((), (), s32[]{:S(2)}) async-start(), calls=%async_computation.2 | async-start | bytes 4718592 | tf_op jit(solution)/shard_map/all_gather | solution.py:916
  11.3 17.5 %collective-permute-start.4 = (bf16[136,1024]{1,0:T(8,128)(2,1)S(1)}, bf16[136,1024]{1,0:T(8,128)(2,1)S(1)}, u32[]{:S(2)}, u32[]{:S(2)}) collective-permute-start(bf16[136,1024]{1,0:T(8,128)(2,1)S(1)} %first_shard.1), channel_id=1, source_target_pairs={{0,6},{1,7},{2,4},{3,5},{4,2},{5,3},{6,0},{7,1},{8,14},{9,15},{10,... | collective-permute-start | bytes 835592 | tf_op jit(solution)/shard_map/ppermute | solution.py:34
  15.5 23.3 %collective-permute-start.3 = (bf16[136,1024]{1,0:T(8,128)(2,1)S(1)}, bf16[136,1024]{1,0:T(8,128)(2,1)S(1)}, u32[]{:S(2)}, u32[]{:S(2)}) collective-permute-start(bf16[136,1024]{1,0:T(8,128)(2,1)S(1)} %first_shard.1), channel_id=1, source_target_pairs={{0,4},{1,5},{2,6},{3,7},{4,0},{5,1},{6,2},{7,3},{8,12},{9,13},{10,... | collective-permute-start | bytes 835592 | tf_op jit(solution)/shard_map/ppermute | solution.py:34
  15.6 23.3 %collective-permute-start.2 = (bf16[136,1024]{1,0:T(8,128)(2,1)S(1)}, bf16[136,1024]{1,0:T(8,128)(2,1)S(1)}, u32[]{:S(2)}, u32[]{:S(2)}) collective-permute-start(bf16[136,1024]{1,0:T(8,128)(2,1)S(1)} %first_shard.1), channel_id=1, source_target_pairs={{0,2},{1,3},{2,0},{3,1},{4,6},{5,7},{6,4},{7,5},{8,10},{9,11},{10,... | collective-permute-start | bytes 835592 | tf_op jit(solution)/shard_map/ppermute | solution.py:34
  15.9 9.6 %collective-permute-start.5 = (bf16[1,136,1024]{2,1,0:T(8,128)(2,1)S(1)}, bf16[1,136,1024]{2,1,0:T(8,128)(2,1)S(1)}, u32[]{:S(2)}, u32[]{:S(2)}) collective-permute-start(bf16[1,136,1024]{2,1,0:T(8,128)(2,1)S(1)} %bitcast.119), channel_id=1, source_target_pairs={{0,1},{1,0},{2,3},{3,2},{4,5},{5,4},{6,7},{7,6},{8,9},{9,8},{10,11... | collective-permute-start | bytes 835592 | tf_op jit(solution)/shard_map/ppermute | solution.py:34
  38.9 209.0 %reduce-scatter.2.cloned.1.call-start = ((), (), s32[]{:S(2)}) async-start(), calls=%async_computation.1 | async-start | bytes 4718592 | tf_op jit(solution)/shard_map/reduce_scatter | solution.py:952
  38.9 23.5 %collective-permute-start.1 = (bf16[2,256,1024]{2,1,0:T(8,128)(2,1)S(1)}, bf16[2,256,1024]{2,1,0:T(8,128)(2,1)S(1)}, u32[]{:S(2)}, u32[]{:S(2)}) collective-permute-start(bf16[2,256,1024]{2,1,0:T(8,128)(2,1)S(1)} %pick_rows.1.refs_0_), channel_id=1, source_target_pairs={{0,16},{8,24},{16,0},{24,8},{1,17},{9,25},{17,1},{25,9},{2,18},{10... | collective-permute-start | bytes 3145736 | tf_op jit(solution)/shard_map/ppermute | solution.py:34
  40.3 24.1 %collective-permute-start.6 = (bf16[3,136,1024]{2,1,0:T(8,128)(2,1)S(1)}, bf16[3,136,1024]{2,1,0:T(8,128)(2,1)S(1)}, u32[]{:S(2)}, u32[]{:S(2)}) collective-permute-start(bf16[3,136,1024]{2,1,0:T(8,128)(2,1)S(1)} %pad_maximum_fusion.refs_5_), channel_id=1, source_target_pairs={{0,1},{1,0},{2,3},{3,2},{4,5},{5,4},{6,7},{7,6},{8,9},{9,8},{10,11... | collective-permute-start | bytes 2506760 | tf_op jit(solution)/shard_map/ppermute | solution.py:34
  41.6 25.5 %collective-permute-start = (bf16[2,256,1024]{2,1,0:T(8,128)(2,1)S(1)}, bf16[2,256,1024]{2,1,0:T(8,128)(2,1)S(1)}, u32[]{:S(2)}, u32[]{:S(2)}) collective-permute-start(bf16[2,256,1024]{2,1,0:T(8,128)(2,1)S(1)} %pick_rows.1.refs_0_), channel_id=1, source_target_pairs={{0,8},{8,0},{16,24},{24,16},{1,9},{9,1},{17,25},{25,17},{2,10},{10... | collective-permute-start | bytes 3145736 | tf_op jit(solution)/shard_map/ppermute | solution.py:34
  77.3 13.4 %collective-permute-start.11 = (bf16[8,32,1024]{2,1,0:T(8,128)(2,1)}, bf16[8,32,1024]{2,1,0:T(8,128)(2,1)}, u32[]{:S(2)}, u32[]{:S(2)}) collective-permute-start(bf16[8,32,1024]{2,1,0:T(8,128)(2,1)} %get-tuple-element.65.refs_0_), channel_id=1, source_target_pairs={{0,16},{8,24},{16,0},{24,8},{1,17},{9,25},{17,1},{25,9},{2,18},{10... | collective-permute-start | bytes 1572872 | tf_op jit(solution)/shard_map/ppermute | solution.py:34
  80.2 12.4 %collective-permute-start.10 = (bf16[8,32,1024]{2,1,0:T(8,128)(2,1)}, bf16[8,32,1024]{2,1,0:T(8,128)(2,1)S(1)}, u32[]{:S(2)}, u32[]{:S(2)}) collective-permute-start(bf16[8,32,1024]{2,1,0:T(8,128)(2,1)} %get-tuple-element.65.refs_0_), channel_id=1, source_target_pairs={{0,8},{8,0},{16,24},{24,16},{1,9},{9,1},{17,25},{25,17},{2,10},{10... | collective-permute-start | bytes 1572872 | tf_op jit(solution)/shard_map/ppermute | solution.py:34
  92.0 13.6 %collective-permute-start.9 = (bf16[1024,256]{1,0:T(8,128)(2,1)S(1)}, bf16[1024,256]{1,0:T(8,128)(2,1)S(1)}, u32[]{:S(2)}, u32[]{:S(2)}) collective-permute-start(bf16[1024,256]{1,0:T(8,128)(2,1)S(1)} %get-tuple-element.64.refs_4_.a_ref.o_ref), channel_id=1, source_target_pairs={{0,16},{8,24},{16,0},{24,8},{1,17},{9,25},{17,1},{25,9},{2,18},{10... | collective-permute-start | bytes 1572872 | tf_op jit(solution)/shard_map/ppermute | solution.py:34
  92.2 14.2 %collective-permute-start.8 = (bf16[1024,256]{1,0:T(8,128)(2,1)S(1)}, bf16[1024,256]{1,0:T(8,128)(2,1)S(1)}, u32[]{:S(2)}, u32[]{:S(2)}) collective-permute-start(bf16[1024,256]{1,0:T(8,128)(2,1)S(1)} %get-tuple-element.64.refs_4_.a_ref.o_ref), channel_id=1, source_target_pairs={{0,8},{8,0},{16,24},{24,16},{1,9},{9,1},{17,25},{25,17},{2,10},{10... | collective-permute-start | bytes 1572872 | tf_op jit(solution)/shard_map/ppermute | solution.py:34
  129.6 14.3 %collective-permute-start.14 = (bf16[256,1024]{1,0:T(8,128)(2,1)}, bf16[256,1024]{1,0:T(8,128)(2,1)}, u32[]{:S(2)}, u32[]{:S(2)}) collective-permute-start(bf16[256,1024]{1,0:T(8,128)(2,1)} %fusion.28), channel_id=1, source_target_pairs={{0,8},{8,0},{16,24},{24,16},{1,9},{9,1},{17,25},{25,17},{2,10},{10... | collective-permute-start | bytes 1572872 | tf_op jit(solution)/shard_map/ppermute | solution.py:34
  131.2 13.4 %collective-permute-start.16 = (bf16[256,1024]{1,0:T(8,128)(2,1)}, bf16[256,1024]{1,0:T(8,128)(2,1)}, u32[]{:S(2)}, u32[]{:S(2)}) collective-permute-start(bf16[256,1024]{1,0:T(8,128)(2,1)} %add_convert_fusion.1), channel_id=1, source_target_pairs={{0,16},{8,24},{16,0},{24,8},{1,17},{9,25},{17,1},{25,9},{2,18},{10... | collective-permute-start | bytes 1572872 | tf_op jit(solution)/shard_map/ppermute | solution.py:34
  150.6 13.7 %collective-permute-start.20 = (bf16[256,1024]{1,0:T(8,128)(2,1)S(1)}, bf16[256,1024]{1,0:T(8,128)(2,1)S(1)}, u32[]{:S(2)}, u32[]{:S(2)}) collective-permute-start(bf16[256,1024]{1,0:T(8,128)(2,1)S(1)} %fusion.10.refs_0_), channel_id=1, source_target_pairs={{0,16},{8,24},{16,0},{24,8},{1,17},{9,25},{17,1},{25,9},{2,18},{10... | collective-permute-start | bytes 1572872 | tf_op jit(solution)/shard_map/ppermute | solution.py:34
  152.5 34.3 %collective-permute-start.18 = (bf16[256,1024]{1,0:T(8,128)(2,1)S(1)}, bf16[256,1024]{1,0:T(8,128)(2,1)S(1)}, u32[]{:S(2)}, u32[]{:S(2)}) collective-permute-start(bf16[256,1024]{1,0:T(8,128)(2,1)S(1)} %fusion.36), channel_id=1, source_target_pairs={{0,8},{8,0},{16,24},{24,16},{1,9},{9,1},{17,25},{25,17},{2,10},{10... | collective-permute-start | bytes 1572872 | tf_op jit(solution)/shard_map/ppermute | solution.py:34
  153.6 12.9 %collective-permute-start.19 = (bf16[256,1024]{1,0:T(8,128)(2,1)S(1)}, bf16[256,1024]{1,0:T(8,128)(2,1)S(1)}, u32[]{:S(2)}, u32[]{:S(2)}) collective-permute-start(bf16[256,1024]{1,0:T(8,128)(2,1)S(1)} %fusion.32), channel_id=1, source_target_pairs={{0,8},{8,0},{16,24},{24,16},{1,9},{9,1},{17,25},{25,17},{2,10},{10... | collective-permute-start | bytes 1572872 | tf_op jit(solution)/shard_map/ppermute | solution.py:34
  166.6 20.2 %collective-permute-start.22 = (bf16[256,1024]{1,0:T(8,128)(2,1)S(1)}, bf16[256,1024]{1,0:T(8,128)(2,1)S(1)}, u32[]{:S(2)}, u32[]{:S(2)}) collective-permute-start(bf16[256,1024]{1,0:T(8,128)(2,1)S(1)} %add_convert_fusion), channel_id=1, source_target_pairs={{0,16},{8,24},{16,0},{24,8},{1,17},{9,25},{17,1},{25,9},{2,18},{10... | collective-permute-start | bytes 1572872 | tf_op jit(solution)/shard_map/ppermute | solution.py:34
  170.5 14.8 %collective-permute-start.35 = (bf16[4,1,32,1024]{3,2,1,0:T(8,128)(2,1)S(1)}, bf16[4,1,32,1024]{3,2,1,0:T(8,128)(2,1)S(1)}, u32[]{:S(2)}, u32[]{:S(2)}) collective-permute-start(bf16[4,1,32,1024]{3,2,1,0:T(8,128)(2,1)S(1)} %get-tuple-element.83), channel_id=1, source_target_pairs={{0,1},{1,0},{2,3},{3,2},{4,5},{5,4},{6,7},{7,6},{8,9},{9,8},{10,11... | collective-permute-start | bytes 786440 | tf_op jit(solution)/shard_map/ppermute | solution.py:34
  184.3 21.4 %collective-permute-start.29 = (bf16[4,4,32,512]{3,2,1,0:T(8,128)(2,1)}, bf16[4,4,32,512]{3,2,1,0:T(8,128)(2,1)}, u32[]{:S(2)}, u32[]{:S(2)}) collective-permute-start(bf16[4,4,32,512]{3,2,1,0:T(8,128)(2,1)} %get-tuple-element.87), channel_id=1, source_target_pairs={{0,1},{1,0},{2,3},{3,2},{4,5},{5,4},{6,7},{7,6},{8,9},{9,8},{10,11... | collective-permute-start | bytes 1572872 | tf_op jit(solution)/shard_map/ppermute | solution.py:34
  197.6 21.4 %collective-permute-start.26 = (bf16[4,4,32,384]{3,2,1,0:T(8,128)(2,1)S(1)}, bf16[4,4,32,384]{3,2,1,0:T(8,128)(2,1)S(1)}, u32[]{:S(2)}, u32[]{:S(2)}) collective-permute-start(bf16[4,4,32,384]{3,2,1,0:T(8,128)(2,1)S(1)} %get-tuple-element.90), channel_id=1, source_target_pairs={{0,2},{1,3},{2,0},{3,1},{4,6},{5,7},{6,4},{7,5},{8,10},{9,11},{10,... | collective-permute-start | bytes 1179656 | tf_op jit(solution)/shard_map/ppermute | solution.py:34
  198.2 11.7 %collective-permute-start.36 = (bf16[2,1,32,1024]{3,2,1,0:T(8,128)(2,1)S(1)}, bf16[2,1,32,1024]{3,2,1,0:T(8,128)(2,1)S(1)}, u32[]{:S(2)}, u32[]{:S(2)}) collective-permute-start(bf16[2,1,32,1024]{3,2,1,0:T(8,128)(2,1)S(1)} %copy-done.47), channel_id=1, source_target_pairs={{0,2},{1,3},{2,0},{3,1},{4,6},{5,7},{6,4},{7,5},{8,10},{9,11},{10,... | collective-permute-start | bytes 393224 | tf_op jit(solution)/shard_map/ppermute | solution.py:34
  199.8 42.1 %collective-permute-start.23 = (bf16[256,1024]{1,0:T(8,128)(2,1)S(1)}, bf16[256,1024]{1,0:T(8,128)(2,1)S(1)}, u32[]{:S(2)}, u32[]{:S(2)}) collective-permute-start(bf16[256,1024]{1,0:T(8,128)(2,1)S(1)} %convolution_convert_fusion.1), channel_id=1, source_target_pairs={{0,8},{8,0},{16,24},{24,16},{1,9},{9,1},{17,25},{25,17},{2,10},{10... | collective-permute-start | bytes 1572872 | tf_op jit(solution)/shard_map/ppermute | solution.py:34
  202.1 17.5 %collective-permute-start.24 = (bf16[256,1024]{1,0:T(8,128)(2,1)S(1)}, bf16[256,1024]{1,0:T(8,128)(2,1)S(1)}, u32[]{:S(2)}, u32[]{:S(2)}) collective-permute-start(bf16[256,1024]{1,0:T(8,128)(2,1)S(1)} %convolution_convert_fusion), channel_id=1, source_target_pairs={{0,8},{8,0},{16,24},{24,16},{1,9},{9,1},{17,25},{25,17},{2,10},{10... | collective-permute-start | bytes 1572872 | tf_op jit(solution)/shard_map/ppermute | solution.py:34
  216.4 15.8 %collective-permute-start.31 = (bf16[1,4,32,512]{3,2,1,0:T(8,128)(2,1)S(1)}, bf16[1,4,32,512]{3,2,1,0:T(8,128)(2,1)S(1)}, u32[]{:S(2)}, u32[]{:S(2)}) collective-permute-start(bf16[1,4,32,512]{3,2,1,0:T(8,128)(2,1)S(1)} %slice.330), channel_id=1, source_target_pairs={{0,4},{1,5},{2,6},{3,7},{4,0},{5,1},{6,2},{7,3},{8,12},{9,13},{10,... | collective-permute-start | bytes 393224 | tf_op jit(solution)/shard_map/ppermute | solution.py:34
  220.2 21.7 %collective-permute-start.25 = (bf16[256,1024]{1,0:T(8,128)(2,1)S(1)}, bf16[256,1024]{1,0:T(8,128)(2,1)S(1)}, u32[]{:S(2)}, u32[]{:S(2)}) collective-permute-start(bf16[256,1024]{1,0:T(8,128)(2,1)S(1)} %fusion.8), channel_id=1, source_target_pairs={{0,16},{8,24},{16,0},{24,8},{1,17},{9,25},{17,1},{25,9},{2,18},{10... | collective-permute-start | bytes 1572872 | tf_op jit(solution)/shard_map/ppermute | solution.py:34
  228.2 12.4 %collective-permute-start.28 = (bf16[1,4,32,384]{3,2,1,0:T(8,128)(2,1)S(1)}, bf16[1,4,32,384]{3,2,1,0:T(8,128)(2,1)S(1)}, u32[]{:S(2)}, u32[]{:S(2)}) collective-permute-start(bf16[1,4,32,384]{3,2,1,0:T(8,128)(2,1)S(1)} %slice.331), channel_id=1, source_target_pairs={{0,4},{1,5},{2,6},{3,7},{4,0},{5,1},{6,2},{7,3},{8,12},{9,13},{10,... | collective-permute-start | bytes 294920 | tf_op jit(solution)/shard_map/ppermute | solution.py:34
  248.9 17.3 %collective-permute-start.38 = (bf16[128,1024]{1,0:T(8,128)(2,1)S(1)}, bf16[128,1024]{1,0:T(8,128)(2,1)S(1)}, u32[]{:S(2)}, u32[]{:S(2)}) collective-permute-start(bf16[128,1024]{1,0:T(8,128)(2,1)S(1)} %get-tuple-element.120), channel_id=1, source_target_pairs={{0,0},{4,4},{1,8},{5,12},{2,16},{6,20},{3,24},{7,28},{8,1},{12,5},... | collective-permute-start | bytes 786440 | tf_op jit(solution)/shard_map/ppermute | solution.py:1026
  252.6 9.3 %collective-permute-start.34 = (bf16[32,1920]{1,0:T(8,128)(2,1)S(1)}, bf16[32,1920]{1,0:T(8,128)(2,1)S(1)}, u32[]{:S(2)}, u32[]{:S(2)}) collective-permute-start(bf16[32,1920]{1,0:T(8,128)(2,1)S(1)} %get-tuple-element.124), channel_id=1, source_target_pairs={{0,24},{8,16},{16,8},{24,0},{1,25},{9,17},{17,9},{25,1},{2,26},{10... | collective-permute-start | bytes 368648 | tf_op jit(solution)/shard_map/ppermute | solution.py:34
  253.8 10.7 %collective-permute-start.33 = (bf16[32,1920]{1,0:T(8,128)(2,1)S(1)}, bf16[32,1920]{1,0:T(8,128)(2,1)S(1)}, u32[]{:S(2)}, u32[]{:S(2)}) collective-permute-start(bf16[32,1920]{1,0:T(8,128)(2,1)S(1)} %get-tuple-element.125), channel_id=1, source_target_pairs={{0,16},{8,24},{16,0},{24,8},{1,17},{9,25},{17,1},{25,9},{2,18},{10... | collective-permute-start | bytes 368648 | tf_op jit(solution)/shard_map/ppermute | solution.py:34
  253.8 10.7 %collective-permute-start.32 = (bf16[32,1920]{1,0:T(8,128)(2,1)S(1)}, bf16[32,1920]{1,0:T(8,128)(2,1)S(1)}, u32[]{:S(2)}, u32[]{:S(2)}) collective-permute-start(bf16[32,1920]{1,0:T(8,128)(2,1)S(1)} %get-tuple-element.126), channel_id=1, source_target_pairs={{0,8},{8,0},{16,24},{24,16},{1,9},{9,1},{17,25},{25,17},{2,10},{10... | collective-permute-start | bytes 368648 | tf_op jit(solution)/shard_map/ppermute | solution.py:34
  (65 other events, 338.5 us)
Sparse Core Ops, SparseCore 0:
  39.0 76.1 all-gather.2
  143.9 103.8 reduce-scatter.1
